TPU v7x, 128 devices: a whole 4x4x4 slice. The times are simulated.
128 devices in a mesh: seq: 8 (over z, y_hi), chan: 8 (over x, core), dp: 2 (over y_lo).
Axes of the slice: x: 4, y: 4 (y_hi: 2, y_lo: 2; y = y_hi * 2 + y_lo), z: 4, core: 2. Of those that a mesh axis runs over, the one named last changes fastest.
Arguments:
- tokens: bfloat16 [2, 1024, 8192], P('dp', 'seq'), may hold values from -6 to 6
- in_weight: bfloat16 [8192, 3, 4096], P('seq', None, 'chan'), may hold values from -0.0625 to 0.0625
- short_taps: float32 [3, 3, 4096], P(None, None, 'chan'), may hold values from -1 to 1
- long_filter: float32 [1024, 4096], P('seq', 'chan'), may hold values from -1.25 to 1.25
- skip_gain: float32 [4096], P('chan'), may hold values from 0.5 to 1.5
- cotangent: bfloat16 [2, 1024, 4096], P('dp', 'seq', 'chan'), may hold values from -6 to 6
Outputs:
- hyena_out: bfloat16 [2, 1024, 4096], P('dp', 'seq', 'chan')
- grad_tokens: bfloat16 [2, 1024, 8192], P('dp', None, ('seq', 'chan'))
- grad_weight: bfloat16 [8192, 3, 4096], P('seq', None, 'chan')
- grad_filter: float32 [1024, 4096], P('seq', 'chan')
All inputs are finite; a program needn't handle non-finite values.
Results may differ from a plain program's by a relative error of at most 0.02.
Values may be sent and summed in bfloat16 or wider, within the bound.
No kernel may reach another device: no remote copies, remote signals or barrier semaphores. Data moves between devices by JAX's collectives and lax.ppermute only.
A program may use at most 128 MiB of HBM per device.

v0:
```python
import math

import jax
import jax.numpy as jnp
from jax import lax
from jax.sharding import PartitionSpec as P


def partner_2(shard, axis, stride):
    return lax.ppermute(shard, axis, [(i, i ^ 1 << stride) for i in range(lax.axis_size(axis))])


def shifted(value, axis, steps):
    count = lax.axis_size(axis)
    leading, last = (max(0, -steps), min(count, count - steps))
    return lax.ppermute(value, axis, [(source, source + steps) for source in range(leading, last)])


def complex_mul(left, right):
    return jnp.stack(
        [left[0] * right[0] - left[1] * right[1], left[0] * right[1] + left[1] * right[0]]
    )


def conjugate(signal):
    return jnp.stack([signal[0], -signal[1]])


def dft_tables(length):
    index = jnp.arange(length, dtype=jnp.int32)
    product = index[:, None] * index[None, :] % length
    phases = 2.0 * math.pi / length * product.astype(jnp.float32)
    return (jnp.cos(phases), jnp.sin(phases))


def table_apply(cos_table, sin_table, sign, signal, form):
    high = lax.Precision.HIGHEST
    real_cos = jnp.einsum(form, cos_table, signal[0], precision=high)
    imag_cos = jnp.einsum(form, cos_table, signal[1], precision=high)
    real_sin = jnp.einsum(form, sin_table, signal[0], precision=high)
    imag_sin = jnp.einsum(form, sin_table, signal[1], precision=high)
    return jnp.stack([real_cos - sign * imag_sin, imag_cos + sign * real_sin])


def reverse_bits(seq_pos, seq_count):
    bit_total = seq_count.bit_length() - 1
    result = jnp.zeros((), jnp.int32)
    for bit_pos in range(bit_total):
        result = result + seq_pos // (1 << bit_pos) % 2 * (1 << bit_total - 1 - bit_pos)
    return result


def pairs_forward(signal, seq_count, seq_pos):
    bit_total = seq_count.bit_length() - 1
    for bit_pos in reversed(range(bit_total)):
        half_span = 1 << bit_pos
        partner = partner_2(signal, "seq", bit_pos)
        offset = (seq_pos % half_span).astype(jnp.float32)
        phases = -math.pi * offset / half_span
        twiddle = jnp.stack([jnp.cos(phases), jnp.sin(phases)])
        is_upper = seq_pos // half_span % 2 == 1
        signal = jnp.where(is_upper, complex_mul(partner - signal, twiddle), signal + partner)
    return signal


def pairs_inverse(signal, seq_count, seq_pos):
    bit_total = seq_count.bit_length() - 1
    for bit_pos in range(bit_total):
        half_span = 1 << bit_pos
        partner = partner_2(signal.astype(jnp.bfloat16), "seq", bit_pos).astype(signal.dtype)
        offset = (seq_pos % half_span).astype(jnp.float32)
        phases = math.pi * offset / half_span
        twiddle = jnp.stack([jnp.cos(phases), jnp.sin(phases)])
        is_upper = seq_pos // half_span % 2 == 1
        signal = jnp.where(
            is_upper, partner - complex_mul(signal, twiddle), signal + complex_mul(partner, twiddle)
        )
    return signal


def position_twiddle(spec_order, tok_rows, full_len, sign):
    k_index = 2 * spec_order + jnp.arange(2, dtype=jnp.int32)
    pos_rows = jnp.arange(tok_rows, dtype=jnp.int32)
    product = k_index[:, None] * pos_rows[None, :] % full_len
    phases = sign * 2.0 * math.pi / full_len * product.astype(jnp.float32)
    return jnp.stack([jnp.cos(phases), jnp.sin(phases)])[:, None, :, :, None]


def forward_spectrum(rows_in, seq_count, seq_pos):
    tok_rows = rows_in.shape[1]
    full_len = 2 * seq_count * tok_rows
    phase_shift = math.pi * seq_pos.astype(jnp.float32) / seq_count
    real_part = jnp.stack([rows_in, rows_in * jnp.cos(phase_shift)], axis=1)
    imag_part = jnp.stack([jnp.zeros_like(rows_in), -rows_in * jnp.sin(phase_shift)], axis=1)
    signal = jnp.stack([real_part, imag_part])
    signal = pairs_forward(signal, seq_count, seq_pos)
    spec_order = reverse_bits(seq_pos, seq_count)
    signal = complex_mul(signal, position_twiddle(spec_order, tok_rows, full_len, -1.0))
    cos_table, sin_table = dft_tables(tok_rows)
    return table_apply(cos_table, sin_table, -1.0, signal, "ka,gbac->gbkc")


def inverse_spectrum(signal, seq_count, seq_pos):
    tok_rows = signal.shape[3]
    full_len = 2 * seq_count * tok_rows
    cos_table, sin_table = dft_tables(tok_rows)
    signal = table_apply(cos_table, sin_table, 1.0, signal, "ka,gbac->gbkc")
    spec_order = reverse_bits(seq_pos, seq_count)
    signal = complex_mul(signal, position_twiddle(spec_order, tok_rows, full_len, 1.0))
    signal = pairs_inverse(signal, seq_count, seq_pos)
    phase_shift = math.pi * seq_pos.astype(jnp.float32) / seq_count
    combined = (
        signal[0][:, 0]
        + jnp.cos(phase_shift) * signal[0][:, 1]
        - jnp.sin(phase_shift) * signal[1][:, 1]
    )
    return combined / full_len


def local(tokens, in_weight, short_taps, long_filter, skip_gain, cotangent):
    seq_count = lax.axis_size("seq")
    seq_pos = lax.axis_index("seq")
    tok_rows = tokens.shape[1]
    slab_rows = in_weight.shape[0]
    chan_cols = in_weight.shape[2]
    taps_len = short_taps.shape[1]
    grad_scale = 1.0 / math.sqrt(lax.axis_size("dp") * seq_count * tok_rows)
    spread = lax.all_to_all(tokens[0], "seq", split_axis=1, concat_axis=0, tiled=True)
    flat_weight = in_weight.reshape(slab_rows, 3 * chan_cols)
    projected = lax.psum_scatter(
        jnp.dot(spread, flat_weight, preferred_element_type=jnp.float32),
        "seq",
        scatter_dimension=0,
        tiled=True,
    ).reshape(tok_rows, 3, chan_cols)
    rim_rows = shifted(projected[tok_rows - (taps_len - 1) :], "seq", 1)
    extended = jnp.concatenate([rim_rows, projected], axis=0)
    streams = jnp.zeros_like(projected)
    for tap_pos in range(taps_len):
        begin = taps_len - 1 - tap_pos
        streams = streams + short_taps[:, tap_pos, :] * extended[begin : begin + tok_rows]
    queries = streams[:, 0]
    keys_in = streams[:, 1]
    values_in = streams[:, 2]
    gated_in = keys_in * values_in
    spectra = forward_spectrum(jnp.stack([gated_in, long_filter]), seq_count, seq_pos)
    gated_freq = spectra[:, 0:1]
    filter_freq = spectra[:, 1:2]
    conv_out = (
        inverse_spectrum(complex_mul(gated_freq, filter_freq), seq_count, seq_pos)[0]
        + skip_gain * gated_in
    )
    hyena_out = (queries * conv_out).astype(jnp.bfloat16)[None]
    grad_in = cotangent[0].astype(jnp.float32)
    d_conv = grad_in * queries
    d_query = grad_in * conv_out
    conv_freq = forward_spectrum(d_conv[None], seq_count, seq_pos)
    pair_freq = jnp.concatenate(
        [
            complex_mul(conjugate(filter_freq), conv_freq),
            complex_mul(conjugate(gated_freq), conv_freq),
        ],
        axis=1,
    )
    back_rows = inverse_spectrum(pair_freq, seq_count, seq_pos)
    d_gated = back_rows[0] + skip_gain * d_conv
    filter_part = back_rows[1] * grad_scale
    d_streams = jnp.stack([d_query, d_gated * values_in, d_gated * keys_in], axis=1)
    rim_next = shifted(d_streams[: taps_len - 1], "seq", -1)
    ext_next = jnp.concatenate([d_streams, rim_next], axis=0)
    d_projected = jnp.zeros_like(d_streams)
    for tap_pos in range(taps_len):
        d_projected = (
            d_projected + short_taps[:, tap_pos, :] * ext_next[tap_pos : tap_pos + tok_rows]
        )
    d_projected = d_projected.astype(jnp.bfloat16).reshape(tok_rows, 3 * chan_cols)
    shard_rows = lax.all_gather(d_projected, "seq", axis=0, tiled=True)
    weight_total = lax.dot_general(
        spread, shard_rows, (((0,), (0,)), ((), ())), preferred_element_type=jnp.float32
    )
    token_block = lax.dot_general(
        shard_rows, flat_weight, (((1,), (1,)), ((), ())), preferred_element_type=jnp.float32
    )
    grad_tokens = lax.psum_scatter(
        token_block.astype(jnp.bfloat16), "chan", scatter_dimension=1, tiled=True
    )[None]
    weight_sum, filter_sum = (
        lax.psum((weight_total * grad_scale).astype(jnp.bfloat16), "dp").astype(jnp.float32),
        lax.psum(filter_part.astype(jnp.bfloat16), "dp").astype(jnp.float32),
    )
    grad_weight = weight_sum.astype(jnp.bfloat16).reshape(slab_rows, 3, chan_cols)
    return (hyena_out, grad_tokens, grad_weight, filter_sum)


def solution(mesh):
    placed = (
        P("dp", "seq", None),
        P("seq", None, "chan"),
        P(None, None, "chan"),
        P("seq", "chan"),
        P("chan"),
        P("dp", "seq", "chan"),
    )
    return jax.shard_map(
        local,
        mesh=mesh,
        in_specs=placed,
        out_specs=(
            P("dp", "seq", "chan"),
            P("dp", None, ("seq", "chan")),
            P("seq", None, "chan"),
            P("seq", "chan"),
        ),
        check_vma=False,
    )
```

profile of v0, /device:TPU:0, one launch (start us, length us, event | category | flops | bytes accessed | tf_op | source)
XLA Modules:
  0.0 743.1 jit_solution(11029934226150978450)
XLA Ops:
  7.2 4.1 copy.90
  11.3 8.0 %all-to-all-start = ((bf16[128,8,1024]{0,2,1:T(8,128)(2,1)}), bf16[128,8,1024]{0,2,1:T(8,128)(2,1)S(1)}, u32[]{:S(2)}, u32[]{:S(2)}) async-start(bf16[128,8,1024]{0,2,1:T(8,128)(2,1)} %bitcast.318), calls=%async_computation | async-start | bytes 4194304 | tf_op jit(solution)/shard_map/all_to_all | solution.py:128
  19.3 4.6 copy.92
  24.0 23.8 %all-to-all-done = bf16[128,8,1024]{0,2,1:T(8,128)(2,1)S(1)} async-done(((bf16[128,8,1024]{0,2,1:T(8,128)(2,1)}), bf16[128,8,1024]{0,2,1:T(8,128)(2,1)S(1)}, u32[]{:S(2)}, u32[]{:S(2)}) %all-to-all-start) | async-done | bytes 2097184 | tf_op jit(solution)/shard_map/all_to_all | solution.py:128
  47.8 2.6 copy.91
  50.4 8.6 %fusion.204 = f32[1024,1536]{1,0:T(8,128)} fusion(bf16[1024,1024]{1,0:T(8,128)(2,1)} %bitcast.327, bf16[1024,1536]{0,1:T(8,128)(2,1)} %bitcast.323), kind=kOutput, calls=%fused_computation.316 | convolution fusion | flops 3221225472 | bytes 11534336 | tf_op jit(solution)/shard_map/dot_general | solution.py:131
  59.7 95.1 %reduce-scatter.5.cloned.1.call-done = f32[128,1536]{1,0:T(8,128)} async-done(((f32[1024,1536]{1,0:T(8,128)}), f32[128,1536]{1,0:T(8,128)}) %reduce-scatter.5.cloned.1.call-update) | async-done | bytes 786448 | tf_op jit(solution)/shard_map/reduce_scatter | solution.py:130
  155.7 2.4 collective-permute-start
  162.6 4.8 collective-permute-start.1
  167.6 44.0 %collective-permute-done.1 = f32[2,2,2,128,512]{4,3,1,2,0:T(8,128)} collective-permute-done((f32[2,2,2,128,512]{4,3,1,2,0:T(8,128)}, f32[2,2,2,128,512]{4,3,1,2,0:T(8,128)}, u32[]{:S(2)}, u32[]{:S(2)}) %collective-permute-start.1) | collective-permute-done | bytes 2097184 | tf_op jit(solution)/shard_map/ppermute | solution.py:10
  211.6 2.1 fusion.183
  214.0 4.5 maximum_select_fusion
  218.5 2.0 collective-permute-start.2
  220.7 43.1 %collective-permute-done.2 = f32[2,2,2,128,512]{4,3,1,2,0:T(8,128)} collective-permute-done((f32[2,2,2,128,512]{4,3,1,2,0:T(8,128)}, f32[2,2,2,128,512]{4,3,1,2,0:T(8,128)}, u32[]{:S(2)}, u32[]{:S(2)}) %collective-permute-start.2) | collective-permute-done | bytes 2097184 | tf_op jit(solution)/shard_map/ppermute | solution.py:10
  263.7 3.8 fusion.212
  269.1 4.9 maximum_select_fusion.1
  274.0 2.5 collective-permute-start.3
  276.7 43.5 %collective-permute-done.3 = f32[2,2,2,128,512]{4,3,1,2,0:T(8,128)S(1)} collective-permute-done((f32[2,2,2,128,512]{4,3,1,2,0:T(8,128)}, f32[2,2,2,128,512]{4,3,1,2,0:T(8,128)S(1)}, u32[]{:S(2)}, u32[]{:S(2)}) %collective-permute-start.3) | collective-permute-done | bytes 2097184 | tf_op jit(solution)/shard_map/ppermute | solution.py:10
  320.2 2.1 sub.247
  322.6 2.4 maximum_select_fusion.2
  325.3 1.9 fusion.30
  327.2 1.9 fusion.26
  329.2 2.0 fusion.7
  331.1 2.0 fusion.5
  337.3 2.2 collective-permute-start.4
  339.5 8.7 %collective-permute-done.4 = bf16[2,1,2,128,512]{4,3,2,1,0:T(8,128)(2,1)S(1)} collective-permute-done((bf16[2,1,2,128,512]{4,3,2,1,0:T(8,128)(2,1)S(1)}, bf16[2,1,2,128,512]{4,3,2,1,0:T(8,128)(2,1)S(1)}, u32[]{:S(2)}, u32[]{:S(2)}) %collective-permute-start.4) | collective-permute-done | bytes 524320 | tf_op jit(solution)/shard_map/ppermute | solution.py:10
  351.0 8.8 %collective-permute-done.5 = bf16[2,1,2,128,512]{4,3,2,1,0:T(8,128)(2,1)S(1)} collective-permute-done((bf16[2,1,2,128,512]{4,3,2,1,0:T(8,128)(2,1)S(1)}, bf16[2,1,2,128,512]{4,3,2,1,0:T(8,128)(2,1)S(1)}, u32[]{:S(2)}, u32[]{:S(2)}) %collective-permute-start.5) | collective-permute-done | bytes 524320 | tf_op jit(solution)/shard_map/ppermute | solution.py:10
  362.7 10.8 %collective-permute-done.6 = bf16[2,1,2,128,512]{4,3,2,1,0:T(8,128)(2,1)S(1)} collective-permute-done((bf16[2,1,2,128,512]{4,3,2,1,0:T(8,128)(2,1)}, bf16[2,1,2,128,512]{4,3,2,1,0:T(8,128)(2,1)S(1)}, u32[]{:S(2)}, u32[]{:S(2)}) %collective-permute-start.6) | collective-permute-done | bytes 524320 | tf_op jit(solution)/shard_map/ppermute | solution.py:10
  376.1 23.1 %collective-permute-done.7 = f32[2,1,2,128,512]{4,3,2,1,0:T(8,128)S(1)} collective-permute-done((f32[2,1,2,128,512]{4,3,2,1,0:T(8,128)S(1)}, f32[2,1,2,128,512]{4,3,2,1,0:T(8,128)S(1)}, u32[]{:S(2)}, u32[]{:S(2)}) %collective-permute-start.7) | collective-permute-done | bytes 1048608 | tf_op jit(solution)/shard_map/ppermute | solution.py:10
  399.9 2.8 collective-permute-start.8
  402.7 12.8 %collective-permute-done.8 = f32[2,1,2,128,512]{4,3,2,1,0:T(8,128)S(1)} collective-permute-done((f32[2,1,2,128,512]{4,3,2,1,0:T(8,128)S(1)}, f32[2,1,2,128,512]{4,3,2,1,0:T(8,128)S(1)}, u32[]{:S(2)}, u32[]{:S(2)}) %collective-permute-start.8) | collective-permute-done | bytes 1048608 | tf_op jit(solution)/shard_map/ppermute | solution.py:10
  416.9 4.7 collective-permute-start.9
  421.6 12.8 %collective-permute-done.9 = f32[2,1,2,128,512]{4,3,2,1,0:T(8,128)S(1)} collective-permute-done((f32[2,1,2,128,512]{4,3,2,1,0:T(8,128)S(1)}, f32[2,1,2,128,512]{4,3,2,1,0:T(8,128)S(1)}, u32[]{:S(2)}, u32[]{:S(2)}) %collective-permute-start.9) | collective-permute-done | bytes 1048608 | tf_op jit(solution)/shard_map/ppermute | solution.py:10
  446.4 3.9 collective-permute-start.10
  450.5 12.6 %collective-permute-done.10 = bf16[2,2,2,128,512]{4,3,1,2,0:T(8,128)(2,1)S(1)} collective-permute-done((bf16[2,2,2,128,512]{4,3,1,2,0:T(8,128)(2,1)S(1)}, bf16[2,2,2,128,512]{4,3,1,2,0:T(8,128)(2,1)S(1)}, u32[]{:S(2)}, u32[]{:S(2)}) %collective-permute-start.10) | collective-permute-done | bytes 1048608 | tf_op jit(solution)/shard_map/ppermute | solution.py:10
  464.6 2.1 collective-permute-start.11
  467.1 12.4 %collective-permute-done.11 = bf16[2,2,2,128,512]{4,3,1,2,0:T(8,128)(2,1)S(1)} collective-permute-done((bf16[2,2,2,128,512]{4,3,1,2,0:T(8,128)(2,1)S(1)}, bf16[2,2,2,128,512]{4,3,1,2,0:T(8,128)(2,1)S(1)}, u32[]{:S(2)}, u32[]{:S(2)}) %collective-permute-start.11) | collective-permute-done | bytes 1048608 | tf_op jit(solution)/shard_map/ppermute | solution.py:10
  481.1 16.8 %collective-permute-start.12 = (bf16[2,2,2,128,512]{4,3,1,2,0:T(8,128)(2,1)S(1)}, bf16[2,2,2,128,512]{4,3,1,2,0:T(8,128)(2,1)S(1)}, u32[]{:S(2)}, u32[]{:S(2)}) collective-permute-start(bf16[2,2,2,128,512]{4,3,1,2,0:T(8,128)(2,1)S(1)} %get-tuple-element.8), channel_id=1, source_target_pairs={{0,64},{16,80},{32,96},{48,112},{64,0},{80,16},{96,32},{112,48},{1... | collective-permute-start | bytes 3145736 | tf_op jit(solution)/shard_map/ppermute | solution.py:10
  498.2 12.5 %collective-permute-done.12 = bf16[2,2,2,128,512]{4,3,1,2,0:T(8,128)(2,1)S(1)} collective-permute-done((bf16[2,2,2,128,512]{4,3,1,2,0:T(8,128)(2,1)S(1)}, bf16[2,2,2,128,512]{4,3,1,2,0:T(8,128)(2,1)S(1)}, u32[]{:S(2)}, u32[]{:S(2)}) %collective-permute-start.12) | collective-permute-done | bytes 1048608 | tf_op jit(solution)/shard_map/ppermute | solution.py:10
  514.1 5.8 collective-permute-done.13
  521.9 66.3 %all-gather.2.cloned.1.call-done = bf16[1024,1536]{0,1:T(8,128)(2,1)} async-done(((bf16[128,1536]{0,1:T(8,128)(2,1)}), bf16[1024,1536]{0,1:T(8,128)(2,1)}) %all-gather.2.cloned.1.call-update) | async-done | bytes 3145744 | tf_op jit(solution)/shard_map/all_gather | solution.py:177
  588.2 6.8 multiply_convert_fusion
  595.0 4.7 copy.118
  600.0 6.3 convolution_convert_fusion
  606.4 2.6 copy.149
  609.0 84.0 %all-reduce.5.cloned.1.call-done = (bf16[1024,3,512]{2,0,1:T(8,128)(2,1)}, bf16[128,512]{1,0:T(8,128)(2,1)}) async-done(((bf16[1024,3,512]{2,0,1:T(8,128)(2,1)}, bf16[128,512]{1,0:T(8,128)(2,1)}), (bf16[1024,3,512]{2,0,1:T(8,128)(2,1)}, bf16[128,512]{1,0:T(8,128)(2,1)})) %all-reduce.5.cloned.1.call-update) | async-done | bytes 3276816 | tf_op jit(solution)/shard_map/psum | solution.py:188
  694.6 35.9 %reduce-scatter.7.cloned.1.call-done = bf16[128,1024]{1,0:T(8,128)(2,1)} async-done(((bf16[1024,1024]{1,0:T(8,128)(2,1)}), bf16[128,1024]{1,0:T(8,128)(2,1)}) %reduce-scatter.7.cloned.1.call-update) | async-done | bytes 262160
  732.3 3.8 copy.178
  (147 shorter events, 47.5 us)
Async XLA Ops:
  11.3 36.5 %all-to-all-start = ((bf16[128,8,1024]{0,2,1:T(8,128)(2,1)}), bf16[128,8,1024]{0,2,1:T(8,128)(2,1)S(1)}, u32[]{:S(2)}, u32[]{:S(2)}) async-start(bf16[128,8,1024]{0,2,1:T(8,128)(2,1)} %bitcast.318), calls=%async_computation | async-start | bytes 4194304 | tf_op jit(solution)/shard_map/all_to_all | solution.py:128
  19.3 135.6 %reduce-scatter.5.cloned.1.call-start = ((), (), s32[]{:S(2)}) async-start(), calls=%async_computation.3 | async-start | bytes 7077888 | tf_op jit(solution)/shard_map/reduce_scatter | solution.py:130
  59.0 0.7 copy-start.18
  59.0 529.2 %all-gather.2.cloned.1.call-start = ((), (), s32[]{:S(2)}) async-start(), calls=%async_computation.4 | async-start | bytes 3538944 | tf_op jit(solution)/shard_map/all_gather | solution.py:177
  155.7 4.3 collective-permute-start
  158.3 2.0 copy-start.11
  159.7 1.0 copy-start.10
  162.6 49.0 %collective-permute-start.1 = (f32[2,2,2,128,512]{4,3,1,2,0:T(8,128)}, f32[2,2,2,128,512]{4,3,1,2,0:T(8,128)}, u32[]{:S(2)}, u32[]{:S(2)}) collective-permute-start(f32[2,2,2,128,512]{4,3,1,2,0:T(8,128)} %pad_maximum_fusion), channel_id=1, source_target_pairs={{0,64},{16,80},{32,96},{48,112},{64,0},{80,16},{96,32},{112,48},{1... | collective-permute-start | bytes 6291464 | tf_op jit(solution)/shard_map/ppermute | solution.py:10
  214.0 4.5 copy-start
  214.0 4.5 copy-start.2
  218.5 45.3 %collective-permute-start.2 = (f32[2,2,2,128,512]{4,3,1,2,0:T(8,128)}, f32[2,2,2,128,512]{4,3,1,2,0:T(8,128)}, u32[]{:S(2)}, u32[]{:S(2)}) collective-permute-start(f32[2,2,2,128,512]{4,3,1,2,0:T(8,128)} %maximum_select_fusion), channel_id=1, source_target_pairs={{0,32},{16,48},{32,0},{48,16},{64,96},{80,112},{96,64},{112,80},{1... | collective-permute-start | bytes 6291464 | tf_op jit(solution)/shard_map/ppermute | solution.py:10
  267.6 1.2 copy-start.1
  267.6 1.5 copy-start.3
  274.0 46.3 %collective-permute-start.3 = (f32[2,2,2,128,512]{4,3,1,2,0:T(8,128)}, f32[2,2,2,128,512]{4,3,1,2,0:T(8,128)S(1)}, u32[]{:S(2)}, u32[]{:S(2)}) collective-permute-start(f32[2,2,2,128,512]{4,3,1,2,0:T(8,128)} %maximum_select_fusion.1), channel_id=1, source_target_pairs={{0,16},{16,0},{32,48},{48,32},{64,80},{80,64},{96,112},{112,96},{1... | collective-permute-start | bytes 6291464 | tf_op jit(solution)/shard_map/ppermute | solution.py:10
  276.7 48.3 %copy-start.13 = (f32[2,128]{1,0:T(2,128)}, f32[2,128]{1,0:T(2,128)S(1)}, u32[]{:S(2)}) copy-start(f32[2,128]{1,0:T(2,128)S(1)} %get-tuple-element.80) | copy-start | bytes 3076
  276.7 48.3 %copy-start.15 = (f32[2,128]{1,0:T(2,128)}, f32[2,128]{1,0:T(2,128)S(1)}, u32[]{:S(2)}) copy-start(f32[2,128]{1,0:T(2,128)S(1)} %get-tuple-element.81) | copy-start | bytes 3076
  276.7 59.4 %copy-start.19 = (f32[2,128]{1,0:T(2,128)}, f32[2,128]{1,0:T(2,128)S(1)}, u32[]{:S(2)}) copy-start(f32[2,128]{1,0:T(2,128)S(1)} %get-tuple-element.78) | copy-start | bytes 3076
  276.7 59.4 %copy-start.21 = (f32[2,128]{1,0:T(2,128)}, f32[2,128]{1,0:T(2,128)S(1)}, u32[]{:S(2)}) copy-start(f32[2,128]{1,0:T(2,128)S(1)} %get-tuple-element.79) | copy-start | bytes 3076
  331.1 2.1 copy-start.4
  333.1 1.0 copy-start.6
  337.3 11.0 %collective-permute-start.4 = (bf16[2,1,2,128,512]{4,3,2,1,0:T(8,128)(2,1)S(1)}, bf16[2,1,2,128,512]{4,3,2,1,0:T(8,128)(2,1)S(1)}, u32[]{:S(2)}, u32[]{:S(2)}) collective-permute-start(bf16[2,1,2,128,512]{4,3,2,1,0:T(8,128)(2,1)S(1)} %fusion.32), channel_id=1, source_target_pairs={{0,16},{16,0},{32,48},{48,32},{64,80},{80,64},{96,112},{112,96},{1... | collective-permute-start | bytes 1572872 | tf_op jit(solution)/shard_map/ppermute | solution.py:10
  348.9 10.8 %collective-permute-start.5 = (bf16[2,1,2,128,512]{4,3,2,1,0:T(8,128)(2,1)S(1)}, bf16[2,1,2,128,512]{4,3,2,1,0:T(8,128)(2,1)S(1)}, u32[]{:S(2)}, u32[]{:S(2)}) collective-permute-start(bf16[2,1,2,128,512]{4,3,2,1,0:T(8,128)(2,1)S(1)} %get-tuple-element.17), channel_id=1, source_target_pairs={{0,32},{16,48},{32,0},{48,16},{64,96},{80,112},{96,64},{112,80},{1... | collective-permute-start | bytes 1572872 | tf_op jit(solution)/shard_map/ppermute | solution.py:10
  360.0 2.5 copy-start.9
  361.3 12.2 %collective-permute-start.6 = (bf16[2,1,2,128,512]{4,3,2,1,0:T(8,128)(2,1)}, bf16[2,1,2,128,512]{4,3,2,1,0:T(8,128)(2,1)S(1)}, u32[]{:S(2)}, u32[]{:S(2)}) collective-permute-start(bf16[2,1,2,128,512]{4,3,2,1,0:T(8,128)(2,1)} %get-tuple-element.15), channel_id=1, source_target_pairs={{0,64},{16,80},{32,96},{48,112},{64,0},{80,16},{96,32},{112,48},{1... | collective-permute-start | bytes 1572872 | tf_op jit(solution)/shard_map/ppermute | solution.py:10
  374.2 0.7 copy-start.17
  376.0 23.2 %collective-permute-start.7 = (f32[2,1,2,128,512]{4,3,2,1,0:T(8,128)S(1)}, f32[2,1,2,128,512]{4,3,2,1,0:T(8,128)S(1)}, u32[]{:S(2)}, u32[]{:S(2)}) collective-permute-start(f32[2,1,2,128,512]{4,3,2,1,0:T(8,128)S(1)} %pad_maximum_fusion.3), channel_id=1, source_target_pairs={{0,64},{16,80},{32,96},{48,112},{64,0},{80,16},{96,32},{112,48},{1... | collective-permute-start | bytes 3145736 | tf_op jit(solution)/shard_map/ppermute | solution.py:10
  399.9 15.6 %collective-permute-start.8 = (f32[2,1,2,128,512]{4,3,2,1,0:T(8,128)S(1)}, f32[2,1,2,128,512]{4,3,2,1,0:T(8,128)S(1)}, u32[]{:S(2)}, u32[]{:S(2)}) collective-permute-start(f32[2,1,2,128,512]{4,3,2,1,0:T(8,128)S(1)} %maximum_select_fusion.3), channel_id=1, source_target_pairs={{0,32},{16,48},{32,0},{48,16},{64,96},{80,112},{96,64},{112,80},{1... | collective-permute-start | bytes 3145736 | tf_op jit(solution)/shard_map/ppermute | solution.py:10
  416.9 17.5 %collective-permute-start.9 = (f32[2,1,2,128,512]{4,3,2,1,0:T(8,128)S(1)}, f32[2,1,2,128,512]{4,3,2,1,0:T(8,128)S(1)}, u32[]{:S(2)}, u32[]{:S(2)}) collective-permute-start(f32[2,1,2,128,512]{4,3,2,1,0:T(8,128)S(1)} %maximum_select_fusion.4), channel_id=1, source_target_pairs={{0,16},{16,0},{32,48},{48,32},{64,80},{80,64},{96,112},{112,96},{1... | collective-permute-start | bytes 3145736 | tf_op jit(solution)/shard_map/ppermute | solution.py:10
  434.7 0.7 copy-start.14
  434.8 0.7 copy-start.16
  435.4 3.6 copy-start.5
  435.4 3.6 copy-start.7
  443.3 1.3 copy-start.20
  443.3 1.3 copy-start.22
  446.4 16.6 %collective-permute-start.10 = (bf16[2,2,2,128,512]{4,3,1,2,0:T(8,128)(2,1)S(1)}, bf16[2,2,2,128,512]{4,3,1,2,0:T(8,128)(2,1)S(1)}, u32[]{:S(2)}, u32[]{:S(2)}) collective-permute-start(bf16[2,2,2,128,512]{4,3,1,2,0:T(8,128)(2,1)S(1)} %fusion.3), channel_id=1, source_target_pairs={{0,16},{16,0},{32,48},{48,32},{64,80},{80,64},{96,112},{112,96},{1... | collective-permute-start | bytes 3145736 | tf_op jit(solution)/shard_map/ppermute | solution.py:10
  464.6 14.9 %collective-permute-start.11 = (bf16[2,2,2,128,512]{4,3,1,2,0:T(8,128)(2,1)S(1)}, bf16[2,2,2,128,512]{4,3,1,2,0:T(8,128)(2,1)S(1)}, u32[]{:S(2)}, u32[]{:S(2)}) collective-permute-start(bf16[2,2,2,128,512]{4,3,1,2,0:T(8,128)(2,1)S(1)} %get-tuple-element.10), channel_id=1, source_target_pairs={{0,32},{16,48},{32,0},{48,16},{64,96},{80,112},{96,64},{112,80},{1... | collective-permute-start | bytes 3145736 | tf_op jit(solution)/shard_map/ppermute | solution.py:10
  481.1 29.5 %collective-permute-start.12 = (bf16[2,2,2,128,512]{4,3,1,2,0:T(8,128)(2,1)S(1)}, bf16[2,2,2,128,512]{4,3,1,2,0:T(8,128)(2,1)S(1)}, u32[]{:S(2)}, u32[]{:S(2)}) collective-permute-start(bf16[2,2,2,128,512]{4,3,1,2,0:T(8,128)(2,1)S(1)} %get-tuple-element.8), channel_id=1, source_target_pairs={{0,64},{16,80},{32,96},{48,112},{64,0},{80,16},{96,32},{112,48},{1... | collective-permute-start | bytes 3145736 | tf_op jit(solution)/shard_map/ppermute | solution.py:10
  512.6 7.4 copy-start.12
  512.8 7.1 collective-permute-start.13
  520.0 68.2 %copy-start.8 = (bf16[8,128,1024]{2,1,0:T(8,128)(2,1)S(1)}, bf16[8,128,1024]{2,1,0:T(8,128)(2,1)}, u32[]{:S(2)}) copy-start(bf16[8,128,1024]{2,1,0:T(8,128)(2,1)} %copy.91) | copy-start | bytes 6291460
  521.2 171.8 %all-reduce.5.cloned.1.call-start = ((), (), s32[]{:S(2)}) async-start(), calls=%async_computation.6 | async-start | bytes 6553600 | tf_op jit(solution)/shard_map/psum | solution.py:188
  599.7 130.8 %reduce-scatter.7.cloned.1.call-start = ((), (), s32[]{:S(2)}) async-start(), calls=%async_computation.5 | async-start | bytes 2359296
Sparse Core Ops, SparseCore 0:
  59.1 95.6 reduce-scatter.4
  521.3 66.8 all-gather.1
  599.8 93.1 all-reduce.4
  696.0 34.5 reduce-scatter.6
where the time goes:
time: 751 us; the launch traced here: 743 us
  waiting for transfers between devices  556 us (74%)
  starting transfers between devices  56.9 us (8%)
  matrix products  43.9 us (6%)
  other arithmetic  39.1 us (5%)
  local copies, waits for them, and re-layouts  31.3 us (4%)
  between operations  16 us (2%)
    ppermute x12, waiting for transfers between devices, partner_2(): lax.ppermute(shard, axis, [(i, i ^ 1 << stride) for i in range(lax.axis_s...  245 us
    reduce_scatter x1, waiting for transfers between devices, local(): lax.psum_scatter(jnp.dot(spread, flat_weight, preferred_element_type=jnp....  95.1 us
    psum x1, waiting for transfers between devices, local(): lax.psum((weight_total * grad_scale).astype(jnp.bfloat16), 'dp')  84 us
    all_gather x1, waiting for transfers between devices, local(): shard_rows = lax.all_gather(d_projected, 'seq', axis=0, tiled=True)  66.3 us
    ppermute x12, starting transfers between devices, partner_2(): lax.ppermute(shard, axis, [(i, i ^ 1 << stride) for i in range(lax.axis_s...  44.7 us
    unnamed x5, waiting for transfers between devices  36 us
    all_to_all x1, waiting for transfers between devices, local(): lax.all_to_all(tokens[0], 'seq', split_axis=1, concat_axis=0, tiled=True)  23.8 us
    unnamed x53, local copies, waits for them, and re-layouts  20 us
  transfers between devices with their start and end apart: 19, of which 18 were waited for; matrix products, arithmetic and copies ran while one was open for 3% of the time, Pallas kernels for 0%

commit v1 on v0

v1 whole, which is shorter than its diff:
```python
import functools
import math

import jax
import jax.numpy as jnp
from jax import lax
from jax.experimental import pallas as pl
from jax.experimental.pallas import tpu as pltpu
from jax.sharding import PartitionSpec as P

BF = jnp.bfloat16
F32 = jnp.float32
VMEM_BYTES = 48 << 20
NT = (((1,), (1,)), ((), ()))
NN = (((1,), (0,)), ((), ()))


def params():
    return pltpu.CompilerParams(vmem_limit_bytes=VMEM_BYTES)


def cost(flops, bytes_accessed):
    return pl.CostEstimate(flops=flops, bytes_accessed=bytes_accessed, transcendentals=0)


def matmul(left, right, dims):
    return lax.dot_general(left, right, dims, preferred_element_type=F32)


def split(value):
    high = value.astype(BF)
    return high, (value - high.astype(F32)).astype(BF)


def edge_kernel(cot_ref, filter_ref, out_ref):
    slabs, rows, _ = out_ref.shape
    chans = rows // 3
    high, low = split(jnp.transpose(filter_ref[...]))
    cot = jnp.transpose(cot_ref[0].astype(F32)).astype(BF)
    for slab in range(slabs):
        part = slice(slab * chans, (slab + 1) * chans)
        out_ref[slab, :chans] = cot[part]
        out_ref[slab, chans : 2 * chans] = high[part]
        out_ref[slab, 2 * chans :] = low[part]


def edge_rows(cotangent, long_filter, slabs):
    _, tok_rows, chan_cols = cotangent.shape
    return pl.pallas_call(
        edge_kernel,
        out_shape=jax.ShapeDtypeStruct((slabs, 3 * chan_cols // slabs, tok_rows), BF),
        compiler_params=params(),
        cost_estimate=cost(0, 8 * tok_rows * chan_cols),
        name="edge_rows",
    )(cotangent, long_filter)


def flip_kernel(weight_ref, out_ref):
    out_ref[0] = jnp.transpose(weight_ref[0])


def flip_weight(weight):
    streams, slab_rows, chan_cols = weight.shape
    half = chan_cols // 2
    return pl.pallas_call(
        flip_kernel,
        grid=(streams, 2),
        in_specs=[pl.BlockSpec((1, slab_rows, half), lambda i, j: (i, 0, j))],
        out_specs=pl.BlockSpec((1, half, slab_rows), lambda i, j: (i, j, 0)),
        out_shape=jax.ShapeDtypeStruct((streams, chan_cols, slab_rows), BF),
        compiler_params=params(),
        cost_estimate=cost(0, 4 * weight.size),
        name="flip_weight",
    )(weight)


def table_kernel(cos_a_ref, sin_a_ref, cos_b_ref, sin_b_ref, out_ref):
    steps = cos_b_ref.shape[0]
    cos_a = cos_a_ref[0]
    sin_a = sin_a_ref[0]
    cos_b = cos_b_ref[...]
    sin_b = sin_b_ref[...]
    for pos, table in enumerate((cos_a * cos_b - sin_a * sin_b, sin_a * cos_b + cos_a * sin_b)):
        high, low = split(table)
        out_ref[pos] = high
        out_ref[2 + pos] = low


def angle(product, period):
    phases = 2.0 * math.pi / period * (product % period).astype(F32)
    return jnp.cos(phases), jnp.sin(phases)


def tables(count):
    steps = 64
    odd = 2 * jnp.arange(count, dtype=jnp.int32)[None, :] + 1
    period = 8 * count
    base = jnp.arange(count // steps, dtype=jnp.int32)[:, None] * (2 * steps)
    fine = 2 * jnp.arange(steps, dtype=jnp.int32)[:, None] + 1
    cos_a, sin_a = angle(base * odd, period)
    cos_b, sin_b = angle(fine * odd, period)
    return pl.pallas_call(
        table_kernel,
        grid=(count // steps,),
        in_specs=[
            pl.BlockSpec((1, 1, count), lambda i: (i, 0, 0)),
            pl.BlockSpec((1, 1, count), lambda i: (i, 0, 0)),
            pl.BlockSpec((steps, count), lambda i: (0, 0)),
            pl.BlockSpec((steps, count), lambda i: (0, 0)),
        ],
        out_specs=pl.BlockSpec((4, steps, count), lambda i: (0, i, 0)),
        out_shape=jax.ShapeDtypeStruct((4, count, count), BF),
        compiler_params=params(),
        cost_estimate=cost(0, 8 * count * count),
        name="tables",
    )(cos_a[:, None], sin_a[:, None], cos_b, sin_b)


def position_rows(tokens_ref, out_ref):
    _, blocks, rows, width = tokens_ref.shape
    group = tokens_ref.shape[0] * rows
    for block in range(blocks):
        out_ref[block * group : (block + 1) * group] = tokens_ref[:, block].reshape(group, width)


def project_kernel(tokens_ref, weight_ref, out_ref, spread_ref):
    @pl.when(pl.program_id(0) == 0)
    def _():
        position_rows(tokens_ref, spread_ref)

    slabs, _, chans, positions = out_ref.shape
    result = matmul(weight_ref[0], spread_ref[...], NT).astype(BF)
    out_ref[:, 0] = result.reshape(slabs, chans, positions)


def project(tokens, weight, slabs):
    groups, blocks, rows, width = tokens.shape
    streams, chan_cols, _ = weight.shape
    positions = groups * blocks * rows
    chans = chan_cols // slabs
    return pl.pallas_call(
        project_kernel,
        grid=(streams,),
        in_specs=[
            pl.BlockSpec(tokens.shape, lambda i: (0, 0, 0, 0)),
            pl.BlockSpec((1, chan_cols, width), lambda i: (i, 0, 0)),
        ],
        out_specs=pl.BlockSpec((slabs, 1, chans, positions), lambda i: (0, i, 0, 0)),
        out_shape=jax.ShapeDtypeStruct((slabs, streams, chans, positions), BF),
        scratch_shapes=[pltpu.VMEM((positions, width), BF)],
        compiler_params=params(),
        cost_estimate=cost(
            2 * positions * width * streams * chan_cols,
            2 * (tokens.size + weight.size + positions * streams * chan_cols),
        ),
        name="project",
    )(tokens, weight)


def turn_kernel(tokens_ref, out_ref, spread_ref):
    position_rows(tokens_ref, spread_ref)
    out_ref[...] = jnp.transpose(spread_ref[...])


def turn_tokens(tokens):
    groups, blocks, rows, width = tokens.shape
    positions = groups * blocks * rows
    part = width // 4
    return pl.pallas_call(
        turn_kernel,
        grid=(4,),
        in_specs=[pl.BlockSpec((groups, blocks, rows, part), lambda i: (0, 0, 0, i))],
        out_specs=pl.BlockSpec((part, positions), lambda i: (i, 0)),
        out_shape=jax.ShapeDtypeStruct((width, positions), BF),
        scratch_shapes=[pltpu.VMEM((positions, part), BF)],
        compiler_params=params(),
        cost_estimate=cost(0, 4 * tokens.size),
        name="turn_tokens",
    )(tokens)


def delayed(value, steps):
    if steps == 0:
        return value
    lane = lax.broadcasted_iota(jnp.int32, value.shape, 1)
    return jnp.where(lane < steps, 0.0, pltpu.roll(value, steps, 1))


def advanced(value, steps):
    if steps == 0:
        return value
    lanes = value.shape[1]
    lane = lax.broadcasted_iota(jnp.int32, value.shape, 1)
    return jnp.where(lane >= lanes - steps, 0.0, pltpu.roll(value, lanes - steps, 1))


def transform(value, high_table, low_table):
    high, low = split(value)
    return (
        matmul(high, high_table, NN) + matmul(low, high_table, NN) + matmul(high, low_table, NN)
    )


def operator_kernel(grad_scale, parts_ref, edge_ref, taps_ref, phase_ref, table_ref, grads_ref, out_ref):
    sources, streams, chans, positions = parts_ref.shape
    taps_len = (taps_ref.shape[1] - 1) // streams
    blocks, _, block_len = edge_ref.shape

    def tap(stream, pos):
        column = stream * taps_len + pos
        return taps_ref[:, column : column + 1]

    filtered = []
    for stream in range(streams):
        total = parts_ref[0, stream].astype(F32)
        for source in range(1, sources):
            total = total + parts_ref[source, stream].astype(F32)
        acc = tap(stream, 0) * total
        for pos in range(1, taps_len):
            acc = acc + tap(stream, pos) * delayed(total, pos)
        filtered.append(acc)
    query, key, value = filtered
    skip = taps_ref[:, streams * taps_len : streams * taps_len + 1]

    def edge(row):
        return jnp.concatenate(
            [edge_ref[block, row * chans : (row + 1) * chans].astype(F32) for block in range(blocks)],
            axis=1,
        )

    cot = edge(0)
    long_filter = edge(1) + edge(2)
    gated = key * value
    d_conv = cot * query
    stacked = jnp.concatenate([gated, long_filter, d_conv], axis=0)
    cos_all = transform(stacked, table_ref[0], table_ref[2])
    sin_all = transform(stacked, table_ref[1], table_ref[3])
    g_cos, h_cos, d_cos = (cos_all[i * chans : (i + 1) * chans] for i in range(3))
    g_sin, h_sin, d_sin = (sin_all[i * chans : (i + 1) * chans] for i in range(3))
    cos_phase = phase_ref[0:1]
    sin_phase = phase_ref[1:2]
    h_real = h_cos * cos_phase + h_sin * sin_phase
    h_imag = h_cos * sin_phase - h_sin * cos_phase
    conv_real = g_cos * h_real + g_sin * h_imag
    conv_imag = g_cos * h_imag - g_sin * h_real
    back_real = h_real * d_cos - h_imag * d_sin
    back_imag = -(h_real * d_sin + h_imag * d_cos)
    corr_real = g_cos * d_cos + g_sin * d_sin
    corr_imag = g_sin * d_cos - g_cos * d_sin
    lag_real = corr_real * cos_phase + corr_imag * sin_phase
    lag_imag = corr_imag * cos_phase - corr_real * sin_phase
    scale = 1.0 / positions
    real_all = jnp.concatenate([conv_real, back_real, lag_real], axis=0) * scale
    imag_all = jnp.concatenate([conv_imag, back_imag, lag_imag], axis=0) * scale
    result = transform(real_all, table_ref[0], table_ref[2]) - transform(
        imag_all, table_ref[1], table_ref[3]
    )
    conv_out = result[:chans] + skip * gated
    d_gated = result[chans : 2 * chans] + skip * d_conv
    filter_part = (result[2 * chans :] * grad_scale).astype(BF)
    hyena_out = (query * conv_out).astype(BF)
    for block in range(blocks):
        lanes = slice(block * block_len, (block + 1) * block_len)
        out_ref[block, :chans] = hyena_out[:, lanes]
        out_ref[block, chans:] = filter_part[:, lanes]
    for stream, grad in enumerate((cot * conv_out, d_gated * value, d_gated * key)):
        acc = tap(stream, 0) * grad
        for pos in range(1, taps_len):
            acc = acc + tap(stream, pos) * advanced(grad, pos)
        grads_ref[stream * chans : (stream + 1) * chans] = acc.astype(BF)


def operator(parts, edge, taps, phase, table, grad_scale):
    sources, streams, chans, positions = parts.shape
    blocks, _, block_len = edge.shape
    return pl.pallas_call(
        functools.partial(operator_kernel, grad_scale),
        out_shape=(
            jax.ShapeDtypeStruct((streams * chans, positions), BF),
            jax.ShapeDtypeStruct((blocks, 2 * chans, block_len), BF),
        ),
        compiler_params=params(),
        cost_estimate=cost(24 * streams * chans * positions * positions, 2 * (parts.size + table.size)),
        name="operator",
    )(parts, edge, taps, phase, table)


def token_kernel(dp_ref, weight_ref, grads_ref, out_ref):
    streams, _, chan_cols = weight_ref.shape
    positions = grads_ref.shape[-1]
    total = None
    for stream in range(streams):
        grads = grads_ref[:, 0, stream].reshape(chan_cols, positions)
        part = matmul(weight_ref[stream], grads, NN)
        total = part if total is None else total + part
    out_ref[...] = total.astype(BF)


def token_part(dp_pos, weight, grads):
    streams, slab_rows, chan_cols = weight.shape
    slabs, batches, _, chans, positions = grads.shape
    part = slab_rows // 4
    return pl.pallas_call(
        token_kernel,
        grid_spec=pltpu.PrefetchScalarGridSpec(
            num_scalar_prefetch=1,
            grid=(4,),
            in_specs=[
                pl.BlockSpec((streams, part, chan_cols), lambda j, dp: (0, j, 0)),
                pl.BlockSpec((slabs, 1, streams, chans, positions), lambda j, dp: (0, dp[0], 0, 0, 0)),
            ],
            out_specs=pl.BlockSpec((part, positions), lambda j, dp: (j, 0)),
        ),
        out_shape=jax.ShapeDtypeStruct((slab_rows, positions), BF),
        compiler_params=params(),
        cost_estimate=cost(
            2 * streams * slab_rows * chan_cols * positions,
            2 * (weight.size + grads.size // batches + slab_rows * positions),
        ),
        name="token_part",
    )(dp_pos, weight, grads)


def weight_kernel(grad_scale, dp_ref, own_ref, other_ref, own_grads_ref, other_grads_ref, out_ref):
    chan_cols = out_ref.shape[2]
    positions = own_ref.shape[1]
    own = own_grads_ref[...].reshape(chan_cols, positions)
    other = other_grads_ref[...].reshape(chan_cols, positions)
    total = matmul(own_ref[...], own, NT) + matmul(other_ref[...], other, NT)
    out_ref[0] = (total * grad_scale).astype(BF)


def weight_grad(dp_pos, own, other, grads, grad_scale):
    slabs, _, streams, chans, positions = grads.shape
    slab_rows = own.shape[0]
    chan_cols = slabs * chans
    block = (slabs, 1, 1, chans, positions)
    return pl.pallas_call(
        functools.partial(weight_kernel, grad_scale),
        grid_spec=pltpu.PrefetchScalarGridSpec(
            num_scalar_prefetch=1,
            grid=(streams,),
            in_specs=[
                pl.BlockSpec(own.shape, lambda i, dp: (0, 0)),
                pl.BlockSpec(own.shape, lambda i, dp: (0, 0)),
                pl.BlockSpec(block, lambda i, dp: (0, dp[0], i, 0, 0)),
                pl.BlockSpec(block, lambda i, dp: (0, 1 - dp[0], i, 0, 0)),
            ],
            out_specs=pl.BlockSpec((1, slab_rows, chan_cols), lambda i, dp: (i, 0, 0)),
        ),
        out_shape=jax.ShapeDtypeStruct((streams, slab_rows, chan_cols), BF),
        compiler_params=params(),
        cost_estimate=cost(
            4 * streams * slab_rows * chan_cols * positions,
            2 * (2 * own.size + grads.size + streams * slab_rows * chan_cols),
        ),
        name="weight_grad",
    )(dp_pos, own, other, grads, grads)


def total_kernel(parts_ref, out_ref):
    total = parts_ref[0].astype(F32)
    for pos in range(1, parts_ref.shape[0]):
        total = total + parts_ref[pos].astype(F32)
    out_ref[0] = jnp.transpose(total).astype(BF)


def token_total(parts):
    _, rows, positions = parts.shape
    return pl.pallas_call(
        total_kernel,
        out_shape=jax.ShapeDtypeStruct((1, positions, rows), BF),
        compiler_params=params(),
        cost_estimate=cost(0, 2 * parts.size),
        name="token_total",
    )(parts)


def finish_kernel(own_ref, other_ref, out_ref, filter_ref):
    slabs, rows, block_len = own_ref.shape
    chans = rows // 2
    out = own_ref[:, :chans].reshape(slabs * chans, block_len)
    own = own_ref[:, chans:].reshape(slabs * chans, block_len).astype(F32)
    other = other_ref[...].reshape(slabs * chans, block_len).astype(F32)
    out_ref[0] = jnp.transpose(out.astype(F32)).astype(BF)
    filter_ref[...] = jnp.transpose(own + other)


def finish(own, other):
    slabs, rows, block_len = own.shape
    chan_cols = slabs * rows // 2
    return pl.pallas_call(
        finish_kernel,
        out_shape=(
            jax.ShapeDtypeStruct((1, block_len, chan_cols), BF),
            jax.ShapeDtypeStruct((block_len, chan_cols), F32),
        ),
        compiler_params=params(),
        cost_estimate=cost(0, 4 * own.size),
        name="finish",
    )(own, other)


def local(tokens, in_weight, short_taps, long_filter, skip_gain, cotangent):
    seq_count = lax.axis_size("seq")
    seq_pos = lax.axis_index("seq")
    chan_count = lax.axis_size("chan")
    chan_pos = lax.axis_index("chan")
    dp_pos = lax.axis_index("dp").astype(jnp.int32)[None]
    tok_rows = tokens.shape[1]
    slab_rows = in_weight.shape[0]
    chan_cols = in_weight.shape[2]
    streams, taps_len = short_taps.shape[:2]
    positions = seq_count * tok_rows
    chans = chan_cols // seq_count
    share = tok_rows // chan_count
    grad_scale = 1.0 / math.sqrt(lax.axis_size("dp") * positions)
    weight = jnp.transpose(in_weight, (1, 0, 2))

    mine = lax.dynamic_slice_in_dim(tokens[0], chan_pos * share, share, 0)
    mine = jnp.transpose(mine.reshape(share, seq_count, slab_rows), (1, 0, 2))
    mine = lax.all_to_all(mine, "seq", split_axis=0, concat_axis=0, tiled=True)
    swapped = lax.ppermute(mine, "dp", [(0, 1), (1, 0)])
    own_tokens = lax.all_gather(mine, "chan", axis=0)
    other_tokens = lax.all_gather(swapped, "chan", axis=0)

    edge = lax.all_to_all(
        edge_rows(cotangent, long_filter, seq_count), "seq", split_axis=0, concat_axis=0, tiled=True
    )
    taps = jnp.concatenate([short_taps.reshape(streams * taps_len, chan_cols), skip_gain[None]])
    taps = jnp.transpose(lax.dynamic_slice_in_dim(taps, seq_pos * chans, chans, 1))
    table = tables(positions)
    odd = 2 * jnp.arange(positions, dtype=jnp.int32) + 1
    phase = jnp.stack(angle(odd, 8 * positions))

    parts = project(own_tokens, flip_weight(weight), seq_count)
    parts = lax.all_to_all(parts, "seq", split_axis=0, concat_axis=0, tiled=True)
    grads, outs = operator(parts, edge, taps, phase, table, grad_scale)

    all_grads = lax.all_gather(grads, ("seq", "dp"), axis=0)
    all_grads = all_grads.reshape(seq_count, -1, streams, chans, positions)
    outs = lax.all_to_all(outs, "seq", split_axis=0, concat_axis=0, tiled=True)
    other_filter = lax.ppermute(outs[:, chans:], "dp", [(0, 1), (1, 0)])
    hyena_out, grad_filter = finish(outs, other_filter)

    token_block = token_part(dp_pos, weight, all_grads)
    token_block = token_block.reshape(chan_count, -1, positions)
    token_block = lax.all_to_all(token_block, "chan", split_axis=0, concat_axis=0, tiled=True)
    grad_tokens = token_total(token_block)
    grad_weight = weight_grad(
        dp_pos, turn_tokens(own_tokens), turn_tokens(other_tokens), all_grads, grad_scale
    )
    return (hyena_out, grad_tokens, jnp.transpose(grad_weight, (1, 0, 2)), grad_filter)


def solution(mesh):
    placed = (
        P("dp", "seq", None),
        P("seq", None, "chan"),
        P(None, None, "chan"),
        P("seq", "chan"),
        P("chan"),
        P("dp", "seq", "chan"),
    )
    return jax.shard_map(
        local,
        mesh=mesh,
        in_specs=placed,
        out_specs=(
            P("dp", "seq", "chan"),
            P("dp", None, ("seq", "chan")),
            P("seq", None, "chan"),
            P("seq", "chan"),
        ),
        check_vma=False,
    )
```

time: 751 us -> 234 us (0.31)
  waiting for transfers between devices: 556 us -> 110 us
  Pallas kernels: 0 us -> 51.2 us
  matrix products: 43.9 us -> 0 us
  starting transfers between devices: 56.9 us -> 21 us
  other arithmetic: 39.1 us -> 3.34 us
  blocking collectives: 0 us -> 16.7 us
  local copies, waits for them, and re-layouts: 31.3 us -> 15.4 us
    ppermute x14 -> x2, waiting for transfers between devices: 251 us -> 6.71 us  [the longest x1 6.71 us: local(): swapped = lax.ppermute(mine, 'dp', [(0, 1), (1, 0)])]
    reduce_scatter x1 -> x0, waiting for transfers between devices: 95.1 us -> none  [local(): lax.psum_scatter(jnp.dot(spread, flat_weight, preferred_element_type=jnp....]
    psum x1 -> x0, waiting for transfers between devices: 84 us -> none  [local(): lax.psum((weight_total * grad_scale).astype(jnp.bfloat16), 'dp')]
    pallas_call x0 -> x11, Pallas kernels: none -> 51.2 us  [the longest x1 11.4 us: operator(): pl.pallas_call(functools.partial(operator_kernel, grad_scale), out_shape=...]
    ppermute x14 -> x2, starting transfers between devices: 48.4 us -> 2.42 us  [the longest x1 1.76 us: local(): other_filter = lax.ppermute(outs[:, chans:], 'dp', [(0, 1), (1, 0)])]
    dot_general x19 -> x0, matrix products: 43.9 us -> none  [the longest x1 8.6 us: local(): jnp.dot(spread, flat_weight, preferred_element_type=jnp.float32)]
    unnamed x5 -> x3, waiting for transfers between devices: 36 us -> 0.05 us
    all_to_all x0 -> x1, blocking collectives: none -> 16.7 us  [local(): mine = lax.all_to_all(mine, 'seq', split_axis=0, concat_axis=0, tiled=True)]
  transfers between devices with their start and end apart: 19 -> 9, of which waited for: 18 -> 5; matrix products, arithmetic and copies ran while one was open for 3% -> 1% of each run, Pallas kernels for 0% -> 16%
where the time goes in v1:
time: 234 us; the launch traced here: 231 us
  waiting for transfers between devices  110 us (47%)
  Pallas kernels  51.2 us (22%)
  starting transfers between devices  21 us (9%)
  blocking collectives  16.7 us (7%)
  local copies, waits for them, and re-layouts  15.4 us (7%)
  between operations  14 us (6%)
  other arithmetic  3.34 us (1%)
    all_gather x1, waiting for transfers between devices, local(): all_grads = lax.all_gather(grads, ('seq', 'dp'), axis=0)  47.6 us
    all_to_all x1, waiting for transfers between devices, local(): lax.all_to_all(parts, 'seq', split_axis=0, concat_axis=0, tiled=True)  28.9 us
    all_to_all x1, blocking collectives, local(): mine = lax.all_to_all(mine, 'seq', split_axis=0, concat_axis=0, tiled=True)  16.7 us
    unnamed x34, local copies, waits for them, and re-layouts  15.2 us
    all_gather x1, waiting for transfers between devices, local(): other_tokens = lax.all_gather(swapped, 'chan', axis=0)  14.4 us
    all_gather x1, waiting for transfers between devices, local(): own_tokens = lax.all_gather(mine, 'chan', axis=0)  12.2 us
    pallas_call x1, Pallas kernels, operator(): pl.pallas_call(functools.partial(operator_kernel, grad_scale), out_shape=...  11.4 us
    pallas_call x1, Pallas kernels, weight_grad(): pl.pallas_call(functools.partial(weight_kernel, grad_scale), grid_spec=pl...  9.77 us
  transfers between devices with their start and end apart: 9, of which 5 were waited for; matrix products, arithmetic and copies ran while one was open for 1% of the time, Pallas kernels for 16%

profile of v1, /device:TPU:0, one launch (start us, length us, event | category | flops | bytes accessed | tf_op | source)
XLA Modules:
  0.0 231.5 jit_solution(6057725822364385257)
XLA Ops:
  7.2 0.0 copy-start
  7.2 0.0 all-gather.7.cloned.1.call-start
  7.3 1.5 copy-done
  8.8 0.2 copy.23
  8.9 0.2 copy.19
  9.1 16.7 %all_to_all.25 = bf16[8,16,1024]{2,1,0:T(8,128)(2,1)} all-to-all(bf16[8,16,1024]{2,1,0:T(8,128)(2,1)S(1)} %copy.19), channel_id=1, replica_groups=mesh['seq'=8,'chan'=8,'dp'=2] {'seq'}, dimensions={0} | all-to-all | bytes 524288 | tf_op jit(solution)/shard_map/all_to_all | solution.py:422
  25.8 0.0 all-gather.7.cloned.1.call-update
  25.9 0.9 edge_rows.1
  26.8 3.5 %all-to-all-start.2 = ((bf16[8,192,128]{2,1,0:T(8,128)(2,1)}), bf16[8,192,128]{2,1,0:T(8,128)(2,1)S(1)}, u32[]{:S(2)}, u32[]{:S(2)}) async-start(bf16[8,192,128]{2,1,0:T(8,128)(2,1)} %edge_rows.1), calls=%async_computation.2 | async-start | bytes 786432 | tf_op jit(solution)/shard_map/all_to_all | solution.py:427
  30.3 4.1 %flip_weight.1.weight_ref = bf16[3,512,1024]{2,1,0:T(8,128)(2,1)S(1)} custom-call(bf16[3,1024,512]{2,1,0:T(8,128)(2,1)} %bitcast.14), custom_call_target="tpu_custom_call" | custom-call | bytes 6291456 | tf_op jit(solution)/shard_map/flip_weight/pallas_call | solution.py:65
  34.4 1.7 copy-done.3
  36.1 12.2 %all-gather.7.cloned.1.call-done = bf16[64,16,1024]{2,1,0:T(8,128)(2,1)} async-done(((bf16[8,16,1024]{2,1,0:T(8,128)(2,1)}), bf16[64,16,1024]{2,1,0:T(8,128)(2,1)}) %all-gather.7.cloned.1.call-update) | async-done | bytes 2097168 | tf_op jit(solution)/shard_map/all_gather | solution.py:424
  48.3 1.6 copy-done.4
  49.9 5.4 %project.1 = bf16[8,3,64,1024]{3,2,1,0:T(8,128)(2,1)S(1)} custom-call(bf16[8,8,16,1024]{3,2,1,0:T(8,128)(2,1)S(1)} %bitcast.16, bf16[3,512,1024]{2,1,0:T(8,128)(2,1)} %copy-done.3), custom_call_target="tpu_custom_call" | custom-call | flops 3221225472 | bytes 8388608 | tf_op jit(solution)/shard_map/project/pallas_call | solution.py:141
  55.3 1.7 copy-done.2
  57.0 7.0 %all-to-all-start.1 = ((bf16[8,3,64,1024]{3,2,1,0:T(8,128)(2,1)}), bf16[8,3,64,1024]{3,2,1,0:T(8,128)(2,1)}, u32[]{:S(2)}, u32[]{:S(2)}) async-start(bf16[8,3,64,1024]{3,2,1,0:T(8,128)(2,1)} %copy-done.2), calls=%async_computation.1 | async-start | bytes 6291456 | tf_op jit(solution)/shard_map/all_to_all | solution.py:437
  64.0 0.0 all-gather.9.cloned.1.call-start
  64.1 0.1 fusion.7
  64.2 0.1 copy.22
  64.3 0.1 fusion.5
  64.4 1.9 fusion.11
  66.3 1.1 fusion.3
  67.4 7.8 %tables.1.table_ref = bf16[4,1024,1024]{2,1,0:T(8,128)(2,1)} custom-call(f32[16,1,1024]{2,1,0:T(1,128)S(1)} %get-tuple-element.13.cos_a_ref, f32[16,1,1024]{2,1,0:T(1,128)S(1)} %get-tuple-element.12.sin_a_ref, f32[64,1024]{1,0:T(8,128)S(1)} %get-tuple-element.15.cos_b_ref, f32[64,1024]{1,0:T(8,128)S(1)} %get-tuple-element.14.sin_b_ref), custom_call_target="tpu_custom_call" | custom-call | bytes 8388608 | tf_op jit(solution)/shard_map/tables/pallas_call | solution.py:102
  75.2 0.1 fusion.13
  75.3 28.9 %all-to-all-done.1.parts_ref = bf16[8,3,64,1024]{3,2,1,0:T(8,128)(2,1)} async-done(((bf16[8,3,64,1024]{3,2,1,0:T(8,128)(2,1)}), bf16[8,3,64,1024]{3,2,1,0:T(8,128)(2,1)}, u32[]{:S(2)}, u32[]{:S(2)}) %all-to-all-start.1) | async-done | bytes 3145760 | tf_op jit(solution)/shard_map/all_to_all | solution.py:437
  104.3 11.4 %operator.1 = (bf16[192,1024]{1,0:T(8,128)(2,1)}, bf16[8,128,128]{2,1,0:T(8,128)(2,1)}) custom-call(bf16[8,3,64,1024]{3,2,1,0:T(8,128)(2,1)} %all-to-all-done.1.parts_ref, bf16[8,192,128]{2,1,0:T(8,128)(2,1)S(1)} %all-to-all-done.2.edge_ref, f32[64,10]{1,0:T(8,128)S(1)} %bitcast.20, f32[2,1024]{1,0:T(2,128)S(1)} %pad_maximum_fusion.phase_ref, ...), custom_call_target="tpu_custom_call" | custom-call | flops 4831838208 | bytes 11534336 | tf_op jit(solution)/shard_map/operator/pallas_call | solution.py:276
  115.6 0.0 all-gather.9.cloned.1.call-update
  115.6 0.0 all-gather.11.cloned.1.call-start
  115.7 0.7 collective-permute-start.1
  116.4 6.7 %collective-permute-done.1 = bf16[8,16,1024]{2,1,0:T(8,128)(2,1)S(1)} collective-permute-done((bf16[8,16,1024]{2,1,0:T(8,128)(2,1)S(1)}, bf16[8,16,1024]{2,1,0:T(8,128)(2,1)S(1)}, u32[]{:S(2)}, u32[]{:S(2)}) %collective-permute-start.1) | collective-permute-done | bytes 262176 | tf_op jit(solution)/shard_map/ppermute | solution.py:423
  123.1 0.7 copy-done.13
  123.8 0.0 all-gather.11.cloned.1.call-update
  123.8 3.6 %all-to-all-start.3 = ((bf16[8,128,128]{2,1,0:T(8,128)(2,1)}), bf16[8,128,128]{2,1,0:T(8,128)(2,1)S(1)}, u32[]{:S(2)}, u32[]{:S(2)}) async-start(bf16[8,128,128]{2,1,0:T(8,128)(2,1)} %get-tuple-element.8), calls=%async_computation.3 | async-start | bytes 524288 | tf_op jit(solution)/shard_map/all_to_all | solution.py:442
  127.4 47.6 %all-gather.9.cloned.1.call-done = bf16[3072,1024]{1,0:T(8,128)(2,1)} async-done(((bf16[192,1024]{1,0:T(8,128)(2,1)}), bf16[3072,1024]{1,0:T(8,128)(2,1)}) %all-gather.9.cloned.1.call-update) | async-done | bytes 6291472 | tf_op jit(solution)/shard_map/all_gather | solution.py:440
  175.0 1.9 copy-done.1
  176.9 6.1 %token_part.1 = bf16[1024,1024]{1,0:T(8,128)(2,1)S(1)} custom-call(s32[1]{0:T(128)} %bitcast.5.dp_ref, bf16[3,1024,512]{2,1,0:T(8,128)(2,1)S(1)} %bitcast.15, bf16[8,2,3,64,1024]{4,3,2,1,0:T(8,128)(2,1)} %bitcast.24), custom_call_target="tpu_custom_call" | custom-call | flops 3221225472 | bytes 8388608 | tf_op jit(solution)/shard_map/token_part/pallas_call | solution.py:303
  183.0 1.4 copy-done.7
  184.4 4.4 %all-to-all-start.4 = ((bf16[8,128,1024]{2,1,0:T(8,128)(2,1)}), bf16[8,128,1024]{2,1,0:T(8,128)(2,1)}, u32[]{:S(2)}, u32[]{:S(2)}) async-start(bf16[8,128,1024]{2,1,0:T(8,128)(2,1)} %bitcast.19), calls=%async_computation.4 | async-start | bytes 4194304 | tf_op jit(solution)/shard_map/all_to_all | solution.py:448
  188.8 1.8 collective-permute-start
  190.6 1.6 copy-done.5
  192.1 1.1 turn_tokens.2.own_ref
  193.3 1.3 copy-done.8
  194.6 14.4 %all-gather.11.cloned.1.call-done = bf16[64,16,1024]{2,1,0:T(8,128)(2,1)} async-done(((bf16[8,16,1024]{2,1,0:T(8,128)(2,1)}), bf16[64,16,1024]{2,1,0:T(8,128)(2,1)}) %all-gather.11.cloned.1.call-update) | async-done | bytes 2097168 | tf_op jit(solution)/shard_map/all_gather | solution.py:425
  208.9 1.6 copy-done.6
  210.5 1.1 turn_tokens.3.other_ref
  211.7 0.9 finish.1
  212.5 9.8 %weight_grad.1 = bf16[3,1024,512]{2,1,0:T(8,128)(2,1)} custom-call(s32[1]{0:T(128)} %bitcast.5.dp_ref, bf16[1024,1024]{1,0:T(8,128)(2,1)S(1)} %copy-done.9, bf16[1024,1024]{1,0:T(8,128)(2,1)S(1)} %turn_tokens.3.other_ref, bf16[8,2,3,64,1024]{4,3,2,1,0:T(8,128)(2,1)} %bitcast.25, bf16[8,2,3,64,1024]{4,3,2,1,0:T(8,128)(2,1)} %bitcast.26), custom_call_target="tpu_custom_call" | custom-call | flops 6442450944 | bytes 13631488 | tf_op jit(solution)/shard_map/weight_grad/pallas_call | solution.py:338
  222.3 2.6 %token_total.1 = bf16[1,1024,128]{2,1,0:T(8,128)(2,1)} custom-call(bf16[8,128,1024]{2,1,0:T(8,128)(2,1)} %all-to-all-done.4.parts_ref), custom_call_target="tpu_custom_call" | custom-call | bytes 2097152 | tf_op jit(solution)/shard_map/token_total/pallas_call | solution.py:370
  (32 shorter events, 0.1 us)
Async XLA Ops:
  7.2 1.6 copy-start
  7.2 18.7 %copy-start.11 = (bf16[1,128,512]{2,1,0:T(8,128)(2,1)S(1)}, bf16[1,128,512]{2,1,0:T(8,128)(2,1)}, u32[]{:S(2)}) copy-start(bf16[1,128,512]{2,1,0:T(8,128)(2,1)} %cot_ref.1) | copy-start | bytes 393220
  7.2 18.7 %copy-start.10 = (f32[128,512]{1,0:T(8,128)S(1)}, f32[128,512]{1,0:T(8,128)}, u32[]{:S(2)}) copy-start(f32[128,512]{1,0:T(8,128)} %filter_ref.1) | copy-start | bytes 786436
  7.2 41.1 %all-gather.7.cloned.1.call-start = ((), (), s32[]{:S(2)}) async-start(), calls=%async_computation.5 | async-start | bytes 2359296 | tf_op jit(solution)/shard_map/all_gather | solution.py:424
  26.8 30.2 %all-to-all-start.2 = ((bf16[8,192,128]{2,1,0:T(8,128)(2,1)}), bf16[8,192,128]{2,1,0:T(8,128)(2,1)S(1)}, u32[]{:S(2)}, u32[]{:S(2)}) async-start(bf16[8,192,128]{2,1,0:T(8,128)(2,1)} %edge_rows.1), calls=%async_computation.2 | async-start | bytes 786432 | tf_op jit(solution)/shard_map/all_to_all | solution.py:427
  34.4 1.7 copy-start.3
  48.3 1.6 copy-start.4
  55.3 1.7 copy-start.2
  57.0 7.1 %copy-start.14 = (f32[3,3,512]{2,1,0:T(4,128)S(1)}, f32[3,3,512]{2,1,0:T(4,128)}, u32[]{:S(2)}) copy-start(f32[3,3,512]{2,1,0:T(4,128)} %param.8) | copy-start | bytes 55300
  57.0 7.1 %copy-start.15 = (f32[512]{0:T(512)S(1)}, f32[512]{0:T(512)}, u32[]{:S(2)}) copy-start(f32[512]{0:T(512)} %param.10) | copy-start | bytes 6148
  57.0 47.2 %all-to-all-start.1 = ((bf16[8,3,64,1024]{3,2,1,0:T(8,128)(2,1)}), bf16[8,3,64,1024]{3,2,1,0:T(8,128)(2,1)}, u32[]{:S(2)}, u32[]{:S(2)}) async-start(bf16[8,3,64,1024]{3,2,1,0:T(8,128)(2,1)} %copy-done.2), calls=%async_computation.1 | async-start | bytes 6291456 | tf_op jit(solution)/shard_map/all_to_all | solution.py:437
  64.0 111.0 %all-gather.9.cloned.1.call-start = ((), (), s32[]{:S(2)}) async-start(), calls=%async_computation.6 | async-start | bytes 6684672 | tf_op jit(solution)/shard_map/all_gather | solution.py:440
  104.2 11.4 %copy-start.12 = (bf16[8,16,1024]{2,1,0:T(8,128)(2,1)S(1)}, bf16[8,16,1024]{2,1,0:T(8,128)(2,1)}, u32[]{:S(2)}) copy-start(bf16[8,16,1024]{2,1,0:T(8,128)(2,1)} %all_to_all.25) | copy-start | bytes 786436
  115.6 93.3 %all-gather.11.cloned.1.call-start = ((), (), s32[]{:S(2)}) async-start(), calls=%async_computation.7 | async-start | bytes 2359296 | tf_op jit(solution)/shard_map/all_gather | solution.py:425
  115.7 7.4 %collective-permute-start.1 = (bf16[8,16,1024]{2,1,0:T(8,128)(2,1)S(1)}, bf16[8,16,1024]{2,1,0:T(8,128)(2,1)S(1)}, u32[]{:S(2)}, u32[]{:S(2)}) collective-permute-start(bf16[8,16,1024]{2,1,0:T(8,128)(2,1)S(1)} %copy-done.12), channel_id=1, source_target_pairs={{0,1},{1,0},{2,3},{3,2},{4,5},{5,4},{6,7},{7,6},{8,9},{9,8},{10,11... | collective-permute-start | bytes 786440 | tf_op jit(solution)/shard_map/ppermute | solution.py:423
  123.1 0.7 copy-start.13
  123.8 60.6 %all-to-all-start.3 = ((bf16[8,128,128]{2,1,0:T(8,128)(2,1)}), bf16[8,128,128]{2,1,0:T(8,128)(2,1)S(1)}, u32[]{:S(2)}, u32[]{:S(2)}) async-start(bf16[8,128,128]{2,1,0:T(8,128)(2,1)} %get-tuple-element.8), calls=%async_computation.3 | async-start | bytes 524288 | tf_op jit(solution)/shard_map/all_to_all | solution.py:442
  175.0 1.9 copy-start.1
  183.0 1.4 copy-start.7
  184.4 37.9 %all-to-all-start.4 = ((bf16[8,128,1024]{2,1,0:T(8,128)(2,1)}), bf16[8,128,1024]{2,1,0:T(8,128)(2,1)}, u32[]{:S(2)}, u32[]{:S(2)}) async-start(bf16[8,128,1024]{2,1,0:T(8,128)(2,1)} %bitcast.19), calls=%async_computation.4 | async-start | bytes 4194304 | tf_op jit(solution)/shard_map/all_to_all | solution.py:448
  188.8 22.9 %collective-permute-start = (bf16[8,64,128]{2,1,0:T(8,128)(2,1)S(1)}, bf16[8,64,128]{2,1,0:T(8,128)(2,1)S(1)}, u32[]{:S(2)}, u32[]{:S(2)}) collective-permute-start(bf16[8,64,128]{2,1,0:T(8,128)(2,1)S(1)} %slice.4), channel_id=1, source_target_pairs={{0,1},{1,0},{2,3},{3,2},{4,5},{5,4},{6,7},{7,6},{8,9},{9,8},{10,11... | collective-permute-start | bytes 393224 | tf_op jit(solution)/shard_map/ppermute | solution.py:443
  190.5 1.6 copy-start.5
  193.3 1.3 copy-start.8
  208.9 1.6 copy-start.6
  210.5 2.0 copy-start.9
Sparse Core Ops, SparseCore 0:
  26.0 22.2 all-gather.6
  115.8 59.1 all-gather.8
  177.3 31.5 all-gather.10

commit v2 on v1

v2 whole, which is shorter than its diff:
```python
import functools
import math

import jax
import jax.numpy as jnp
from jax import lax
from jax.experimental import pallas as pl
from jax.experimental.pallas import tpu as pltpu
from jax.sharding import PartitionSpec as P

BF = jnp.bfloat16
F32 = jnp.float32
VMEM_BYTES = 60 << 20
NT = (((1,), (1,)), ((), ()))
NN = (((1,), (0,)), ((), ()))


def params(limit=VMEM_BYTES):
    return pltpu.CompilerParams(vmem_limit_bytes=limit)


def cost(flops, bytes_accessed):
    return pl.CostEstimate(flops=flops, bytes_accessed=bytes_accessed, transcendentals=0)


def kept(shape, dtype=BF):
    return pltpu.HBM(shape, dtype)


def matmul(left, right, dims):
    return lax.dot_general(left, right, dims, preferred_element_type=F32)


def split(value):
    high = value.astype(BF)
    return high, (value - high.astype(F32)).astype(BF)


def edge_kernel(cot_ref, filter_ref, out_ref):
    slabs, rows, lanes = out_ref.shape
    block_len = filter_ref.shape[0]
    chans = filter_ref.shape[1] // slabs
    taps = jnp.transpose(filter_ref[...]).astype(BF)
    cot = jnp.transpose(cot_ref[0].astype(F32)).astype(BF)
    for slab in range(slabs):
        part = slice(slab * chans, (slab + 1) * chans)
        fold(out_ref.at[slab], 0, jnp.concatenate([cot[part], taps[part]], axis=0))


def fold(out_ref, first, value):
    rows, block_len = value.shape
    count = rows * block_len // out_ref.shape[1]
    for pos in range(rows // count):
        out_ref[first : first + count, pos * block_len : (pos + 1) * block_len] = value[
            pos * count : (pos + 1) * count
        ]


def unfold(value, block_len):
    return jnp.concatenate(
        [value[:, at : at + block_len] for at in range(0, value.shape[1], block_len)], axis=0
    )


def edge_rows(cotangent, long_filter, slabs):
    _, tok_rows, chan_cols = cotangent.shape
    lanes = slabs * tok_rows
    return pl.pallas_call(
        edge_kernel,
        out_shape=kept((slabs, 2 * tok_rows * chan_cols // slabs // lanes, lanes)),
        compiler_params=params(),
        cost_estimate=cost(0, 8 * tok_rows * chan_cols),
        name="edge_rows",
    )(cotangent, long_filter)


def arrange_kernel(groups, weight_ref, *out_refs):
    flipped = jnp.transpose(weight_ref[0])
    chans = groups[-1][1]
    slabs = flipped.shape[0] // chans
    for pos, (first, last) in enumerate(groups):
        rows = [flipped[slab * chans + first : slab * chans + last] for slab in range(slabs)]
        rows = jnp.concatenate(rows, axis=0)
        out_refs[2 * pos][0] = rows
        out_refs[2 * pos + 1][0] = jnp.transpose(rows)


def arrange_weight(weight, groups):
    streams, slab_rows, chan_cols = weight.shape
    slabs = chan_cols // groups[-1][1]
    shapes, specs = [], []
    for first, last in groups:
        rows = slabs * (last - first)
        for dims in ((rows, slab_rows), (slab_rows, rows)):
            shapes.append(kept((streams, *dims)))
            specs.append(pl.BlockSpec((1, *dims), lambda i: (i, 0, 0)))
    return pl.pallas_call(
        functools.partial(arrange_kernel, groups),
        grid=(streams,),
        in_specs=[pl.BlockSpec((1, slab_rows, chan_cols), lambda i: (i, 0, 0))],
        out_specs=specs,
        out_shape=shapes,
        compiler_params=params(),
        cost_estimate=cost(0, 6 * weight.size),
        name="arrange_weight",
    )(weight)


def table_kernel(cos_a_ref, sin_a_ref, cos_b_ref, sin_b_ref, out_ref):
    cos_a = cos_a_ref[0]
    sin_a = sin_a_ref[0]
    cos_b = cos_b_ref[...]
    sin_b = sin_b_ref[...]
    out_ref[0] = (cos_a * cos_b - sin_a * sin_b).astype(BF)
    out_ref[1] = (sin_a * cos_b + cos_a * sin_b).astype(BF)


def angle(product, period):
    phases = 2.0 * math.pi / period * (product % period).astype(F32)
    return jnp.cos(phases), jnp.sin(phases)


def tables(count):
    steps = 64
    odd = 2 * jnp.arange(count, dtype=jnp.int32)[None, :] + 1
    period = 8 * count
    base = jnp.arange(count // steps, dtype=jnp.int32)[:, None] * (2 * steps)
    fine = 2 * jnp.arange(steps, dtype=jnp.int32)[:, None] + 1
    cos_a, sin_a = angle(base * odd, period)
    cos_b, sin_b = angle(fine * odd, period)
    return pl.pallas_call(
        table_kernel,
        grid=(count // steps,),
        in_specs=[
            pl.BlockSpec((1, 1, count), lambda i: (i, 0, 0)),
            pl.BlockSpec((1, 1, count), lambda i: (i, 0, 0)),
            pl.BlockSpec((steps, count), lambda i: (0, 0)),
            pl.BlockSpec((steps, count), lambda i: (0, 0)),
        ],
        out_specs=pl.BlockSpec((2, steps, count), lambda i: (0, i, 0)),
        out_shape=jax.ShapeDtypeStruct((2, count, count), BF),
        compiler_params=params(),
        cost_estimate=cost(0, 4 * count * count),
        name="tables",
    )(cos_a[:, None], sin_a[:, None], cos_b, sin_b)


def first_kernel(core_ref, mine_ref, theirs_ref, weight_ref, edge_ref, out_ref, spread_ref):
    blocks, half, _ = mine_ref.shape
    core = core_ref[0]
    step = pl.program_id(0)

    @pl.when(step == 0)
    def _():
        for block in range(blocks):
            base = 2 * block * half
            spread_ref[pl.ds(pl.multiple_of(base + core * half, half), half)] = mine_ref[block]
            spread_ref[pl.ds(pl.multiple_of(base + (1 - core) * half, half), half)] = theirs_ref[block]
        out_ref[:, out_ref.shape[1] - edge_ref.shape[1] :] = edge_ref[...]

    slabs, _, positions = out_ref.shape
    chans = weight_ref.shape[1] // slabs
    result = matmul(weight_ref[0], spread_ref[...], NT).astype(BF).reshape(slabs, chans, positions)
    out_ref[:, pl.ds(pl.multiple_of(step * chans, chans), chans)] = result


def rest_kernel(spread_ref, weight_ref, out_ref):
    slabs, _, chans, positions = out_ref.shape
    result = matmul(weight_ref[0], spread_ref[...], NT).astype(BF)
    out_ref[:, 0] = result.reshape(slabs, chans, positions)


def project_first(core, mine, theirs, weight, edge):
    blocks, half, width = mine.shape
    streams, rows, _ = weight.shape
    slabs, edge_len, positions = edge.shape
    out_dims = (slabs, streams * rows // slabs + edge_len, positions)
    return pl.pallas_call(
        first_kernel,
        grid_spec=pltpu.PrefetchScalarGridSpec(
            num_scalar_prefetch=1,
            grid=(streams,),
            in_specs=[
                pl.BlockSpec(mine.shape, lambda i, core: (0, 0, 0)),
                pl.BlockSpec(mine.shape, lambda i, core: (0, 0, 0)),
                pl.BlockSpec((1, rows, width), lambda i, core: (i, 0, 0)),
                pl.BlockSpec(edge.shape, lambda i, core: (0, 0, 0)),
            ],
            out_specs=[
                pl.BlockSpec(out_dims, lambda i, core: (0, 0, 0)),
                pl.BlockSpec((positions, width), lambda i, core: (0, 0)),
            ],
        ),
        out_shape=(kept(out_dims), kept((positions, width))),
        compiler_params=params(),
        cost_estimate=cost(
            2 * positions * width * streams * rows,
            2 * (2 * positions * width + weight.size + positions * streams * rows),
        ),
        name="project_first",
    )(core, mine, theirs, weight, edge)


def project_rest(spread, weight, slabs):
    positions, width = spread.shape
    streams, rows, _ = weight.shape
    chans = rows // slabs
    return pl.pallas_call(
        rest_kernel,
        grid=(streams,),
        in_specs=[
            pl.BlockSpec((positions, width), lambda i: (0, 0)),
            pl.BlockSpec((1, rows, width), lambda i: (i, 0, 0)),
        ],
        out_specs=pl.BlockSpec((slabs, 1, chans, positions), lambda i: (0, i, 0, 0)),
        out_shape=kept((slabs, streams, chans, positions)),
        compiler_params=params(),
        cost_estimate=cost(
            2 * positions * width * streams * rows,
            2 * (spread.size + weight.size + positions * streams * rows),
        ),
        name="project_rest",
    )(spread, weight)


def turn_kernel(tokens_ref, out_ref):
    out_ref[...] = jnp.transpose(tokens_ref[...])


def turn_tokens(tokens):
    positions, width = tokens.shape
    part = width // 4
    return pl.pallas_call(
        turn_kernel,
        grid=(4,),
        in_specs=[pl.BlockSpec((positions, part), lambda i: (0, i))],
        out_specs=pl.BlockSpec((part, positions), lambda i: (i, 0)),
        out_shape=kept((width, positions)),
        compiler_params=params(),
        cost_estimate=cost(0, 4 * tokens.size),
        name="turn_tokens",
    )(tokens)


def turn_shares_kernel(tokens_ref, out_ref, spread_ref):
    chips, cores, blocks, rows, _ = tokens_ref.shape
    for block in range(blocks):
        for core in range(cores):
            for chip in range(chips):
                base = ((block * cores + core) * chips + chip) * rows
                spread_ref[base : base + rows] = tokens_ref[chip, core, block]
    out_ref[...] = jnp.transpose(spread_ref[...])


def turn_shares(tokens):
    chips, cores, blocks, rows, width = tokens.shape
    positions = chips * cores * blocks * rows
    part = width // 4
    return pl.pallas_call(
        turn_shares_kernel,
        grid=(4,),
        in_specs=[pl.BlockSpec((chips, cores, blocks, rows, part), lambda i: (0, 0, 0, 0, i))],
        out_specs=pl.BlockSpec((part, positions), lambda i: (i, 0)),
        out_shape=kept((width, positions)),
        scratch_shapes=[pltpu.VMEM((positions, part), BF)],
        compiler_params=params(),
        cost_estimate=cost(0, 4 * tokens.size),
        name="turn_shares",
    )(tokens)


def delayed(value, steps):
    if steps == 0:
        return value
    lane = lax.broadcasted_iota(jnp.int32, value.shape, 1)
    return jnp.where(lane < steps, 0.0, pltpu.roll(value, steps, 1))


def advanced(value, steps):
    if steps == 0:
        return value
    lanes = value.shape[1]
    lane = lax.broadcasted_iota(jnp.int32, value.shape, 1)
    return jnp.where(lane >= lanes - steps, 0.0, pltpu.roll(value, lanes - steps, 1))


def transform(value, table):
    rows = value.shape[0]
    result = matmul(jnp.concatenate(split(value), axis=0), table, NN)
    return result[:rows] + result[rows:]


def operator_kernel(first, grad_scale, proj, edge, taps_ref, phase_ref, table):
    chans, positions = proj[0].shape
    streams = len(proj)
    taps_len = (taps_ref.shape[1] - 1) // streams
    own = slice(first, first + chans)

    def tap(stream, pos):
        column = stream * taps_len + pos
        return taps_ref[own, column : column + 1]

    filtered = []
    for stream, total in enumerate(proj):
        acc = tap(stream, 0) * total
        for pos in range(1, taps_len):
            acc = acc + tap(stream, pos) * delayed(total, pos)
        filtered.append(acc)
    query, key, value = filtered
    skip = taps_ref[own, streams * taps_len : streams * taps_len + 1]
    half = edge.shape[0] // 2
    cot = edge[first : first + chans].astype(F32)
    long_filter = edge[half + first : half + first + chans].astype(F32)
    gated = key * value
    d_conv = cot * query
    stacked = jnp.concatenate([gated, long_filter, d_conv], axis=0)
    table_ref = table()
    cos_all = transform(stacked, table_ref[0])
    sin_all = transform(stacked, table_ref[1])
    g_cos, h_cos, d_cos = (cos_all[i * chans : (i + 1) * chans] for i in range(3))
    g_sin, h_sin, d_sin = (sin_all[i * chans : (i + 1) * chans] for i in range(3))
    cos_phase = phase_ref[0:1]
    sin_phase = phase_ref[1:2]
    h_real = h_cos * cos_phase + h_sin * sin_phase
    h_imag = h_cos * sin_phase - h_sin * cos_phase
    conv_real = g_cos * h_real + g_sin * h_imag
    conv_imag = g_cos * h_imag - g_sin * h_real
    back_real = h_real * d_cos - h_imag * d_sin
    back_imag = -(h_real * d_sin + h_imag * d_cos)
    corr_real = g_cos * d_cos + g_sin * d_sin
    corr_imag = g_sin * d_cos - g_cos * d_sin
    lag_real = corr_real * cos_phase + corr_imag * sin_phase
    lag_imag = corr_imag * cos_phase - corr_real * sin_phase
    real_all = jnp.concatenate([conv_real, back_real, lag_real], axis=0)
    imag_all = jnp.concatenate([conv_imag, back_imag, lag_imag], axis=0)
    result = transform(real_all, table_ref[0]) - transform(imag_all, table_ref[1])
    scale = 1.0 / positions
    conv_out = result[:chans] * scale + skip * gated
    d_gated = result[chans : 2 * chans] * scale + skip * d_conv
    filter_part = (result[2 * chans :] * (scale * grad_scale)).astype(BF)
    hyena_out = (query * conv_out).astype(BF)
    grads = []
    for stream, grad in enumerate((cot * conv_out, d_gated * value, d_gated * key)):
        acc = tap(stream, 0) * grad
        for pos in range(1, taps_len):
            acc = acc + tap(stream, pos) * advanced(grad, pos)
        grads.append(acc.astype(BF))
    return grads, hyena_out, filter_part


def summed(parts_ref, row, count):
    total = parts_ref[0, row : row + count].astype(F32)
    for source in range(1, parts_ref.shape[0]):
        total = total + parts_ref[source, row : row + count].astype(F32)
    return total


def load_table(table_ref, held_ref, sem):
    copy = pltpu.make_async_copy(table_ref, held_ref, sem)
    copy.start()

    def ready():
        copy.wait()
        return held_ref

    return ready


def operator_first_kernel(
    group, grad_scale, parts_ref, taps_ref, phase_ref, table_ref, grads_ref, out_ref, edge_ref, held_ref, sem
):
    table = load_table(table_ref, held_ref, sem)
    chans = group[1] - group[0]
    streams = grads_ref.shape[0] // chans
    sources, rows, positions = parts_ref.shape
    edge = jnp.concatenate(
        [
            unfold(parts_ref[source, streams * chans :], positions // sources)
            for source in range(sources)
        ],
        axis=1,
    )
    edge_ref[...] = edge
    proj = [summed(parts_ref, stream * chans, chans) for stream in range(streams)]
    grads, hyena_out, filter_part = operator_kernel(
        group[0], grad_scale, proj, edge, taps_ref, phase_ref, table
    )
    for stream, grad in enumerate(grads):
        grads_ref[stream * chans : (stream + 1) * chans] = grad
    out_ref[:chans] = hyena_out
    out_ref[chans:] = filter_part


def operator_first(group, parts, taps, phase, table, grad_scale, streams):
    sources, rows, positions = parts.shape
    chans = group[1] - group[0]
    full = pl.BlockSpec(memory_space=pltpu.VMEM)
    return pl.pallas_call(
        functools.partial(operator_first_kernel, group, grad_scale),
        in_specs=[full, full, full, pl.BlockSpec(memory_space=pl.ANY)],
        out_shape=(
            kept((streams * chans, positions)),
            jax.ShapeDtypeStruct((2 * chans, positions), BF),
            jax.ShapeDtypeStruct((2 * taps.shape[0], positions), BF),
        ),
        scratch_shapes=[pltpu.VMEM(table.shape, BF), pltpu.SemaphoreType.DMA],
        compiler_params=params(),
        cost_estimate=cost(16 * streams * chans * positions * positions, 2 * (parts.size + table.size)),
        name="operator_first",
    )(parts, taps, phase, table)


def operator_last_kernel(
    group, grad_scale, parts_ref, taps_ref, phase_ref, table_ref, outs_ref, edge_ref, out_ref, held_ref, sem
):
    table = load_table(table_ref, held_ref, sem)
    sources, streams, chans, positions = parts_ref.shape
    proj = []
    for stream in range(streams):
        total = parts_ref[0, stream].astype(F32)
        for source in range(1, sources):
            total = total + parts_ref[source, stream].astype(F32)
        proj.append(total)
    grads, hyena_out, filter_part = operator_kernel(
        group[0], grad_scale, proj, edge_ref[...], taps_ref, phase_ref, table
    )
    before = outs_ref.shape[0] // 2
    columns = jnp.concatenate([outs_ref[:before], hyena_out, outs_ref[before:], filter_part], axis=0)
    devices = out_ref.shape[0]
    block_len = positions // sources
    for device in range(devices):
        for stream, grad in enumerate(grads):
            out_ref[device, stream * chans : (stream + 1) * chans] = grad
        lane = device // (devices // sources) * block_len
        fold(out_ref.at[device], streams * chans, columns[:, lane : lane + block_len])


def operator_last(group, parts, taps, phase, table, outs, edge, grad_scale, devices):
    sources, streams, chans, positions = parts.shape
    full = pl.BlockSpec(memory_space=pltpu.VMEM)
    rows = streams * chans + 2 * taps.shape[0] // sources
    return pl.pallas_call(
        functools.partial(operator_last_kernel, group, grad_scale),
        in_specs=[full, full, full, pl.BlockSpec(memory_space=pl.ANY), full, full],
        out_shape=kept((devices, rows, positions)),
        scratch_shapes=[pltpu.VMEM(table.shape, BF), pltpu.SemaphoreType.DMA],
        compiler_params=params(),
        cost_estimate=cost(16 * streams * chans * positions * positions, 2 * (parts.size + table.size)),
        name="operator_last",
    )(parts, taps, phase, table, outs, edge)


def token_kernel(pos_ref, *refs):
    sent_ref, held_ref = refs[-2:]
    positions = sent_ref.shape[1]
    total = None
    for weight_ref, grads_ref in zip(refs[0:-2:2], refs[1:-2:2]):
        streams, chips, _, rows, cols = weight_ref.shape
        for stream in range(streams):
            weight = weight_ref[stream, :, 0].reshape(chips * rows, cols)
            part = matmul(weight, grads_ref[:, 0, stream].reshape(cols, positions), NN)
            total = part if total is None else total + part
    total = total.astype(BF)

    @pl.when(pl.program_id(0) == 0)
    def _():
        sent_ref[...] = total

    @pl.when(pl.program_id(0) == 1)
    def _():
        held_ref[...] = total


def token_part(pos, weights, grads, chan_count):
    operands, specs = [], []
    flops = 0
    for weight, grad in zip(weights, grads):
        streams, slab_rows, cols = weight.shape
        slabs, _, _, chans, positions = grad.shape
        rows = slab_rows // chan_count
        operands += [weight.reshape(streams, chan_count // 2, 2, rows, cols), grad]
        specs += [
            pl.BlockSpec(
                (streams, chan_count // 2, 1, rows, cols),
                lambda j, pos: (0, 0, jnp.where(j == 0, 1 - pos[1], pos[1]), 0, 0),
            ),
            pl.BlockSpec((slabs, 1, streams, chans, positions), lambda j, pos: (0, pos[0], 0, 0, 0)),
        ]
        flops += 2 * weight.size * positions
    return pl.pallas_call(
        token_kernel,
        grid_spec=pltpu.PrefetchScalarGridSpec(
            num_scalar_prefetch=1,
            grid=(2,),
            in_specs=specs,
            out_specs=[pl.BlockSpec((slab_rows // 2, positions), lambda j, pos: (0, 0))] * 2,
        ),
        out_shape=(kept((slab_rows // 2, positions)), kept((slab_rows // 2, positions))),
        compiler_params=params(),
        cost_estimate=cost(flops, 8 * slab_rows * positions),
        name="token_part",
    )(pos, *operands)


def weight_kernel(grad_scale, pos_ref, own_ref, other_ref, *refs):
    out_ref, rows_ref = refs[-2:]
    slabs = refs[0].shape[0]
    chans = out_ref.shape[2] // slabs
    total = None
    for batch, tokens_ref in enumerate((own_ref, other_ref)):
        first = 0
        for grads_ref in refs[batch:-2:2]:
            count = grads_ref.shape[3]
            for slab in range(slabs):
                base = slab * chans + first
                rows_ref[batch, base : base + count] = grads_ref[slab, 0, 0]
            first += count
        part = matmul(tokens_ref[...], rows_ref[batch], NT)
        total = part if total is None else total + part
    out_ref[0] = (total * grad_scale).astype(BF)


def weight_grad(pos, own, other, grads, grad_scale, streams):
    slabs, _, _, _, positions = grads[0].shape
    slab_rows = own.shape[0]
    chan_cols = slabs * sum(grad.shape[3] for grad in grads)
    operands, specs = [], []
    for grad in grads:
        block = (slabs, 1, 1, grad.shape[3], positions)
        operands += [grad, grad]
        specs += [
            pl.BlockSpec(block, lambda i, pos: (0, pos[0], i, 0, 0)),
            pl.BlockSpec(block, lambda i, pos: (0, 1 - pos[0], i, 0, 0)),
        ]
    return pl.pallas_call(
        functools.partial(weight_kernel, grad_scale),
        grid_spec=pltpu.PrefetchScalarGridSpec(
            num_scalar_prefetch=1,
            grid=(streams,),
            in_specs=[
                pl.BlockSpec(own.shape, lambda i, pos: (0, 0)),
                pl.BlockSpec(own.shape, lambda i, pos: (0, 0)),
                *specs,
            ],
            out_specs=pl.BlockSpec((1, slab_rows, chan_cols), lambda i, pos: (i, 0, 0)),
            scratch_shapes=[pltpu.VMEM((2, chan_cols, positions), BF)],
        ),
        out_shape=jax.ShapeDtypeStruct((streams, slab_rows, chan_cols), BF),
        compiler_params=params(),
        cost_estimate=cost(
            4 * streams * slab_rows * chan_cols * positions,
            2 * (2 * own.size + 2 * streams * chan_cols * positions + streams * slab_rows * chan_cols),
        ),
        name="weight_grad",
    )(pos, own, other, *operands)


def total_kernel(parts_ref, out_ref):
    total = parts_ref[0].astype(F32)
    for pos in range(1, parts_ref.shape[0]):
        total = total + parts_ref[pos].astype(F32)
    out_ref[0] = jnp.transpose(total).astype(BF)


def token_total(parts):
    _, rows, positions = parts.shape
    return pl.pallas_call(
        total_kernel,
        out_shape=jax.ShapeDtypeStruct((1, positions, rows), BF),
        compiler_params=params(24 << 20),
        cost_estimate=cost(0, 2 * parts.size),
        name="token_total",
    )(parts)


def finish_kernel(block_len, pos_ref, own_ref, other_ref, out_ref, filter_ref):
    slabs = own_ref.shape[0]
    hyena, filters = [], []
    for slab in range(slabs):
        own = unfold(own_ref[slab, 0, 0], block_len)
        other = unfold(other_ref[slab, 0, 0], block_len)
        chans = own.shape[0] // 2
        hyena.append(own[:chans].astype(F32))
        filters.append(own[chans:].astype(F32) + other[chans:].astype(F32))
    out_ref[0] = jnp.transpose(jnp.concatenate(hyena, axis=0)).astype(BF)
    filter_ref[...] = jnp.transpose(jnp.concatenate(filters, axis=0))


def finish(pos, received, chan_cols):
    slabs, batches, parts, rows, positions = received.shape
    block_len = positions // slabs
    block = (slabs, 1, 1, rows, positions)
    return pl.pallas_call(
        functools.partial(finish_kernel, block_len),
        grid_spec=pltpu.PrefetchScalarGridSpec(
            num_scalar_prefetch=1,
            grid=(1,),
            in_specs=[
                pl.BlockSpec(block, lambda i, pos: (0, pos[0], parts - 1, 0, 0)),
                pl.BlockSpec(block, lambda i, pos: (0, 1 - pos[0], parts - 1, 0, 0)),
            ],
            out_specs=[
                pl.BlockSpec((1, block_len, chan_cols), lambda i, pos: (0, 0, 0)),
                pl.BlockSpec((block_len, chan_cols), lambda i, pos: (0, 0)),
            ],
        ),
        out_shape=(
            jax.ShapeDtypeStruct((1, block_len, chan_cols), BF),
            jax.ShapeDtypeStruct((block_len, chan_cols), F32),
        ),
        compiler_params=params(),
        cost_estimate=cost(0, 8 * slabs * rows * positions),
        name="finish",
    )(pos, received, received)


def exchange(value, axis, groups=None):
    return lax.all_to_all(
        value, axis, split_axis=0, concat_axis=0, tiled=True, axis_index_groups=groups
    )


def local(tokens, in_weight, short_taps, long_filter, skip_gain, cotangent):
    seq_count = lax.axis_size("seq")
    seq_pos = lax.axis_index("seq")
    dp_count = lax.axis_size("dp")
    chan_count = lax.axis_size("chan")
    chan_pos = lax.axis_index("chan").astype(jnp.int32)
    core = chan_pos % 2
    pos = jnp.stack([lax.axis_index("dp").astype(jnp.int32), core])
    tok_rows = tokens.shape[1]
    slab_rows = in_weight.shape[0]
    chan_cols = in_weight.shape[2]
    streams, taps_len = short_taps.shape[:2]
    positions = seq_count * tok_rows
    chans = chan_cols // seq_count
    half = tok_rows // 2
    share = tok_rows // chan_count
    chips = chan_count // 2
    grad_scale = 1.0 / math.sqrt(dp_count * positions)
    groups = ((0, chans * 3 // 4), (chans * 3 // 4, chans))
    cores = [(i, i ^ 1) for i in range(chan_count)]
    batches = [(0, 1), (1, 0)]
    weight = jnp.transpose(in_weight, (1, 0, 2))

    mine = lax.dynamic_slice_in_dim(tokens[0], core * half, half, 0)
    mine = jnp.transpose(mine.reshape(half, seq_count, slab_rows), (1, 0, 2))
    taps = jnp.concatenate([short_taps.reshape(streams * taps_len, chan_cols), skip_gain[None]])
    taps = jnp.transpose(lax.dynamic_slice_in_dim(taps, seq_pos * chans, chans, 1))
    odd = 2 * jnp.arange(positions, dtype=jnp.int32) + 1
    phase = jnp.stack(angle(odd, 8 * positions))
    mine, edge, arranged, table, taps, phase = lax.optimization_barrier(
        (
            exchange(mine, "seq"),
            edge_rows(cotangent, long_filter, seq_count),
            arrange_weight(weight, groups),
            tables(positions),
            taps,
            phase,
        )
    )
    flipped_a, weight_a, flipped_b, weight_b = arranged
    theirs = lax.ppermute(mine, "chan", cores)
    parts_a, spread = project_first(core[None], mine, theirs, flipped_a, edge)
    shares = lax.dynamic_slice_in_dim(mine, chan_pos // 2 * share, share, 1)
    shares = lax.ppermute(shares, "dp", batches)
    parts_a, shares = lax.optimization_barrier((parts_a, shares))
    shares = lax.all_gather(shares, "chan", axis=0)
    shares = shares.reshape(chips, 2, seq_count, share, slab_rows)
    parts_a, parts_b = lax.optimization_barrier(
        (exchange(parts_a, "seq"), project_rest(spread, flipped_b, seq_count))
    )
    parts_b = exchange(parts_b, "seq")

    grads_a, outs, edge = operator_first(groups[0], parts_a, taps, phase, table, grad_scale, streams)
    grads_a, shares = lax.optimization_barrier((grads_a, shares))
    grads_a = lax.all_gather(grads_a, ("seq", "dp"), axis=0)
    grads_b = operator_last(
        groups[1], parts_b, taps, phase, table, outs, edge, grad_scale, seq_count * dp_count
    )
    grads_b = exchange(grads_b, ("seq", "dp"))
    grads_a = grads_a.reshape(seq_count, dp_count, streams, -1, positions)
    grads_b = grads_b.reshape(seq_count, dp_count, streams + 1, -1, positions)
    finished = finish(pos, grads_b, chan_cols)
    own, other = turn_tokens(spread), turn_shares(shares)
    grads_a, finished, own, other = lax.optimization_barrier((grads_a, finished, own, other))
    hyena_out, grad_filter = finished

    grads = (grads_a, grads_b)
    sent, held = token_part(pos, (weight_a, weight_b), grads, chan_count)
    received = lax.ppermute(sent, "chan", cores)
    token_block = (held.astype(F32) + received.astype(F32)).astype(BF)
    token_block = exchange(
        token_block.reshape(chips, -1, positions),
        "chan",
        [[chip * 2 + side for chip in range(chips)] for side in range(2)],
    )
    grad_tokens = token_total(token_block)
    grad_weight = weight_grad(pos, own, other, grads, grad_scale, streams)
    return (hyena_out, grad_tokens, jnp.transpose(grad_weight, (1, 0, 2)), grad_filter)


def solution(mesh):
    placed = (
        P("dp", "seq", None),
        P("seq", None, "chan"),
        P(None, None, "chan"),
        P("seq", "chan"),
        P("chan"),
        P("dp", "seq", "chan"),
    )
    return jax.shard_map(
        local,
        mesh=mesh,
        in_specs=placed,
        out_specs=(
            P("dp", "seq", "chan"),
            P("dp", None, ("seq", "chan")),
            P("seq", None, "chan"),
            P("seq", "chan"),
        ),
        check_vma=False,
    )
```

time: 234 us -> 222 us (0.949)
  waiting for transfers between devices: 110 us -> 71.4 us
  Pallas kernels: 51.2 us -> 76.1 us
  local copies, waits for them, and re-layouts: 15.4 us -> 5.24 us
  other arithmetic: 3.34 us -> 8.55 us
  starting transfers between devices: 21 us -> 25.1 us
  blocking collectives: 16.7 us -> 20.3 us
    all_gather x3 -> x2, waiting for transfers between devices: 74.1 us -> 0.02 us  [the longest x1 0.02 us: local(): shares = lax.all_gather(shares, 'chan', axis=0)]
    all_to_all x4, waiting for transfers between devices: 28.9 us -> 66.5 us  [exchange(): lax.all_to_all(value, axis, split_axis=0, concat_axis=0, tiled=True, axis...]
    pallas_call x7 -> x9, Pallas kernels: 25 us -> 44.4 us  [the longest x1 7.57 us: operator_first(): pl.pallas_call(functools.partial(operator_first_kernel, group, grad_scale...]
    unnamed x34 -> x14, local copies, waits for them, and re-layouts: 15.2 us -> 3.58 us
    all_to_all x4, starting transfers between devices: 18.5 us -> 24.2 us  [exchange(): lax.all_to_all(value, axis, split_axis=0, concat_axis=0, tiled=True, axis...]
    pallas_call x1, Pallas kernels: 6.05 us -> 9.79 us  [token_part(): pl.pallas_call(token_kernel, grid_spec=pltpu.PrefetchScalarGridSpec(num_s...]
    all_to_all x1, blocking collectives: 16.7 us -> 20.3 us  [exchange(): lax.all_to_all(value, axis, split_axis=0, concat_axis=0, tiled=True, axis...]
    convert_element_type x0 -> x1, other arithmetic: none -> 2.61 us  [local(): token_block = (held.astype(F32) + received.astype(F32)).astype(BF)]
  transfers between devices with their start and end apart: 9 -> 9, of which waited for: 5 -> 5; matrix products, arithmetic and copies ran while one was open for 1% -> 3% of each run, Pallas kernels for 16% -> 30%
where the time goes in v2:
time: 222 us; the launch traced here: 221 us
  Pallas kernels  76.1 us (34%)
  waiting for transfers between devices  71.4 us (32%)
  starting transfers between devices  25.1 us (11%)
  blocking collectives  20.3 us (9%)
  between operations  14.2 us (6%)
  other arithmetic  8.55 us (4%)
  local copies, waits for them, and re-layouts  5.24 us (2%)
    all_to_all x4, waiting for transfers between devices, exchange(): lax.all_to_all(value, axis, split_axis=0, concat_axis=0, tiled=True, axis...  66.5 us
    all_to_all x4, starting transfers between devices, exchange(): lax.all_to_all(value, axis, split_axis=0, concat_axis=0, tiled=True, axis...  24.2 us
    all_to_all x1, blocking collectives, exchange(): lax.all_to_all(value, axis, split_axis=0, concat_axis=0, tiled=True, axis...  20.3 us
    pallas_call x1, Pallas kernels, weight_grad(): pl.pallas_call(functools.partial(weight_kernel, grad_scale), grid_spec=pl...  11.8 us
    pallas_call x1, Pallas kernels, token_part(): pl.pallas_call(token_kernel, grid_spec=pltpu.PrefetchScalarGridSpec(num_s...  9.79 us
    pallas_call x1, Pallas kernels, tables(): pl.pallas_call(table_kernel, grid=(count // steps,), in_specs=[pl.BlockSp...  9.17 us
    pallas_call x1, Pallas kernels, operator_first(): pl.pallas_call(functools.partial(operator_first_kernel, group, grad_scale...  7.57 us
    pallas_call x1, Pallas kernels, project_first(): pl.pallas_call(first_kernel, grid_spec=pltpu.PrefetchScalarGridSpec(num_s...  6.64 us
  transfers between devices with their start and end apart: 9, of which 5 were waited for; matrix products, arithmetic and copies ran while one was open for 3% of the time, Pallas kernels for 30%

profile of v2, /device:TPU:0, one launch (start us, length us, event | category | flops | bytes accessed | tf_op | source)
XLA Modules:
  0.0 220.9 jit_solution(1778459207175417450)
XLA Ops:
  7.2 0.0 copy-start
  7.2 1.6 copy-done
  8.8 0.1 constant_dynamic-slice_fusion.1
  8.8 0.6 copy.20
  9.4 0.0 copy-start.4
  9.5 0.0 copy-start.5
  9.5 1.5 copy.27
  11.0 8.0 %all-to-all-start = ((bf16[8,64,1024]{2,1,0:T(8,128)(2,1)}), bf16[8,64,1024]{2,1,0:T(8,128)(2,1)S(1)}, u32[]{:S(2)}, u32[]{:S(2)}) async-start(bf16[8,64,1024]{2,1,0:T(8,128)(2,1)} %bitcast.17), calls=%async_computation | async-start | bytes 2097152 | tf_op jit(solution)/shard_map/all_to_all | solution.py:618
  19.0 0.0 all-gather.5.cloned.1.call-start
  19.2 0.1 fusion.7
  19.2 0.7 copy.19
  19.9 5.8 %arrange_weight.1 = (bf16[3,384,1024]{2,1,0:T(8,128)(2,1)}, bf16[3,1024,384]{2,1,0:T(8,128)(2,1)}, bf16[3,128,1024]{2,1,0:T(8,128)(2,1)}, bf16[3,1024,128]{2,1,0:T(8,128)(2,1)}) custom-call(bf16[3,1024,512]{2,1,0:T(8,128)(2,1)} %bitcast.21), custom_call_target="tpu_custom_call" | custom-call | bytes 9437184 | tf_op jit(solution)/shard_map/arrange_weight/pallas_call | solution.py:97
  25.7 1.9 edge_rows.1.edge_ref
  27.6 0.1 fusion.5
  27.7 2.5 %fusion.11 = (f32[16,1,1024]{2,1,0:T(1,128)}, f32[16,1,1024]{2,1,0:T(1,128)}) fusion(f32[16,1,1024]{2,0,1:T(8,128)S(1)} %fusion.5), kind=kLoop, calls=%fused_computation.31 | loop fusion | flops 16384 | bytes 196608 | tf_op jit(solution)/shard_map/sin | solution.py:120
  30.2 1.9 fusion.3
  32.1 9.2 %tables.1.table_ref = bf16[2,1024,1024]{2,1,0:T(8,128)(2,1)} custom-call(f32[16,1,1024]{2,1,0:T(1,128)} %get-tuple-element.71.cos_a_ref, f32[16,1,1024]{2,1,0:T(1,128)} %get-tuple-element.70.sin_a_ref, f32[64,1024]{1,0:T(8,128)} %get-tuple-element.73.cos_b_ref, f32[64,1024]{1,0:T(8,128)} %get-tuple-element.72.sin_b_ref), custom_call_target="tpu_custom_call" | custom-call | bytes 4194304 | tf_op jit(solution)/shard_map/tables/pallas_call | solution.py:131
  41.3 0.1 fusion.13
  41.4 0.6 pad_maximum_fusion.phase_ref
  42.0 0.0 all-to-all-done.mine_ref
  42.1 0.8 collective-permute-start.1
  42.8 2.0 collective-permute-done.theirs_ref
  44.8 6.6 %project_first.1 = (bf16[8,160,1024]{2,1,0:T(8,128)(2,1)}, bf16[1024,1024]{1,0:T(8,128)(2,1)}) custom-call(s32[1]{0:T(128)} %bitcast.core_ref, bf16[8,64,1024]{2,1,0:T(8,128)(2,1)} %copy-done.2, bf16[8,64,1024]{2,1,0:T(8,128)(2,1)} %collective-permute-done.theirs_ref, bf16[3,384,1024]{2,1,0:T(8,128)(2,1)} %get-tuple-element.42.weight_ref, ...), custom_call_target="tpu_custom_call" | custom-call | flops 2415919104 | bytes 8912896 | tf_op jit(solution)/shard_map/project_first/pallas_call | solution.py:178
  51.5 0.7 copy-done.3
  52.2 0.0 all-gather.5.cloned.1.call-update
  52.2 7.2 %all-to-all-start.1 = ((bf16[8,160,1024]{2,1,0:T(8,128)(2,1)}), bf16[8,160,1024]{2,1,0:T(8,128)(2,1)}, u32[]{:S(2)}, u32[]{:S(2)}) async-start(bf16[8,160,1024]{2,1,0:T(8,128)(2,1)} %get-tuple-element.45), calls=%async_computation.1 | async-start | bytes 5242880 | tf_op jit(solution)/shard_map/all_to_all | solution.py:618
  59.4 0.0 all-gather.7.cloned.1.call-start
  59.4 5.1 %project_rest.1 = bf16[8,3,16,1024]{3,2,1,0:T(8,128)(2,1)} custom-call(bf16[1024,1024]{1,0:T(8,128)(2,1)} %get-tuple-element.46.spread_ref.tokens_ref, bf16[3,128,1024]{2,1,0:T(8,128)(2,1)} %get-tuple-element.47.weight_ref), custom_call_target="tpu_custom_call" | custom-call | flops 805306368 | bytes 3670016 | tf_op jit(solution)/shard_map/project_rest/pallas_call | solution.py:208
  64.5 29.4 %all-to-all-done.1.parts_ref = bf16[8,160,1024]{2,1,0:T(8,128)(2,1)} async-done(((bf16[8,160,1024]{2,1,0:T(8,128)(2,1)}), bf16[8,160,1024]{2,1,0:T(8,128)(2,1)}, u32[]{:S(2)}, u32[]{:S(2)}) %all-to-all-start.1) | async-done | bytes 2621472 | tf_op jit(solution)/shard_map/all_to_all | solution.py:618
  93.9 7.6 %operator_first.1 = (bf16[144,1024]{1,0:T(8,128)(2,1)}, bf16[96,1024]{1,0:T(8,128)(2,1)}, bf16[128,1024]{1,0:T(8,128)(2,1)}) custom-call(bf16[8,160,1024]{2,1,0:T(8,128)(2,1)} %all-to-all-done.1.parts_ref, f32[64,10]{1,0:T(8,128)} %bitcast.23, f32[2,1024]{1,0:T(2,128)} %pad_maximum_fusion.phase_ref, bf16[2,1024,1024]{2,1,0:T(8,128)(2,1)} %tables.1.table_ref), custom_call_target="tpu_custom_call" | custom-call | flops 2415919104 | bytes 6815744 | tf_op jit(solution)/shard_map/operator_first/pallas_call | solution.py:398
  101.5 0.0 all-gather.5.cloned.1.call-done
  101.5 0.0 all-gather.7.cloned.1.call-update
  101.5 20.3 %all_to_all.25.parts_ref = bf16[8,3,16,1024]{3,2,1,0:T(8,128)(2,1)} all-to-all(bf16[8,3,16,1024]{3,2,1,0:T(8,128)(2,1)S(1)} %copy-done.1), channel_id=1, replica_groups=mesh['seq'=8,'chan'=8,'dp'=2] {'seq'}, dimensions={0} | all-to-all | bytes 1572864 | tf_op jit(solution)/shard_map/all_to_all | solution.py:618
  121.9 6.6 %operator_last.1 = bf16[16,64,1024]{2,1,0:T(8,128)(2,1)} custom-call(bf16[8,3,16,1024]{3,2,1,0:T(8,128)(2,1)} %all_to_all.25.parts_ref, f32[64,10]{1,0:T(8,128)} %bitcast.24, f32[2,1024]{1,0:T(2,128)} %pad_maximum_fusion.phase_ref, bf16[2,1024,1024]{2,1,0:T(8,128)(2,1)} %tables.1.table_ref, bf16[96,1024]{1,0:T(8,128)(2,1)} %get-tuple-element.56.outs_ref, ...), custom_call_target="tpu_custom_call" | custom-call | flops 805306368 | bytes 4980736 | tf_op jit(solution)/shard_map/operator_last/pallas_call | solution.py:442
  128.4 4.6 %all-to-all-start.3 = ((bf16[16,64,1024]{2,1,0:T(8,128)(2,1)}), bf16[16,64,1024]{2,1,0:T(8,128)(2,1)}, u32[]{:S(2)}, u32[]{:S(2)}) async-start(bf16[16,64,1024]{2,1,0:T(8,128)(2,1)} %operator_last.1), calls=%async_computation.3 | async-start | bytes 4194304 | tf_op jit(solution)/shard_map/all_to_all | solution.py:618
  133.1 0.6 pad_add_fusion.pos_ref
  133.7 4.1 %turn_tokens.1.own_ref = bf16[1024,1024]{1,0:T(8,128)(2,1)} custom-call(bf16[1024,1024]{1,0:T(8,128)(2,1)} %get-tuple-element.46.spread_ref.tokens_ref), custom_call_target="tpu_custom_call" | custom-call | bytes 4194304 | tf_op jit(solution)/shard_map/turn_tokens/pallas_call | solution.py:233
  137.8 4.2 %turn_shares.1.other_ref = bf16[1024,1024]{1,0:T(8,128)(2,1)} custom-call(bf16[4,2,8,16,1024]{4,3,2,1,0:T(8,128)(2,1)} %bitcast.22), custom_call_target="tpu_custom_call" | custom-call | bytes 4194304 | tf_op jit(solution)/shard_map/turn_shares/pallas_call | solution.py:259
  142.0 33.5 %all-to-all-done.3 = bf16[16,64,1024]{2,1,0:T(8,128)(2,1)} async-done(((bf16[16,64,1024]{2,1,0:T(8,128)(2,1)}), bf16[16,64,1024]{2,1,0:T(8,128)(2,1)}, u32[]{:S(2)}, u32[]{:S(2)}) %all-to-all-start.3) | async-done | bytes 2097184 | tf_op jit(solution)/shard_map/all_to_all | solution.py:618
  175.5 2.6 %finish.1 = (bf16[1,128,512]{2,1,0:T(8,128)(2,1)}, f32[128,512]{1,0:T(8,128)}) custom-call(s32[2]{0:T(128)} %pad_add_fusion.pos_ref, bf16[8,2,4,16,1024]{4,3,2,1,0:T(8,128)(2,1)} %bitcast.8.own_ref.other_ref.refs_3_.refs_2_, bf16[8,2,4,16,1024]{4,3,2,1,0:T(8,128)(2,1)} %bitcast.8.own_ref.other_ref.refs_3_.refs_2_), custom_call_target="tpu_custom_call" | custom-call | bytes 1048576 | tf_op jit(solution)/shard_map/finish/pallas_call | solution.py:593
  178.1 9.8 %token_part.1 = (bf16[512,1024]{1,0:T(8,128)(2,1)}, bf16[512,1024]{1,0:T(8,128)(2,1)}) custom-call(s32[2]{0:T(128)} %pad_add_fusion.pos_ref, bf16[3,4,2,128,384]{4,3,2,1,0:T(8,128)(2,1)} %bitcast.29, bf16[8,2,3,48,1024]{4,3,2,1,0:T(8,128)(2,1)} %bitcast.26, bf16[3,4,2,128,128]{4,3,2,1,0:T(8,128)(2,1)} %bitcast.30, ...), custom_call_target="tpu_custom_call" | custom-call | flops 3221225472 | bytes 8388608 | tf_op jit(solution)/shard_map/token_part/pallas_call | solution.py:490
  187.8 0.0 collective-permute-start.2
  187.9 2.9 %collective-permute-done.2 = bf16[512,1024]{1,0:T(8,128)(2,1)S(1)} collective-permute-done((bf16[512,1024]{1,0:T(8,128)(2,1)}, bf16[512,1024]{1,0:T(8,128)(2,1)S(1)}, u32[]{:S(2)}, u32[]{:S(2)}) %collective-permute-start.2) | collective-permute-done | bytes 1048608 | tf_op jit(solution)/shard_map/ppermute | solution.py:691
  190.7 2.6 %add_convert_fusion = bf16[512,1024]{1,0:T(8,128)(2,1)} fusion(bf16[512,1024]{1,0:T(8,128)(2,1)S(1)} %collective-permute-done.2, bf16[512,1024]{1,0:T(8,128)(2,1)} %get-tuple-element.65), kind=kLoop, calls=%fused_computation | loop fusion | flops 2097152 | bytes 3145728 | tf_op jit(solution)/shard_map/convert_element_type | solution.py:692
  193.3 4.4 %all-to-all-start.4 = ((bf16[4,128,1024]{2,1,0:T(8,128)(2,1)}), bf16[4,128,1024]{2,1,0:T(8,128)(2,1)S(1)}, u32[]{:S(2)}, u32[]{:S(2)}) async-start(bf16[4,128,1024]{2,1,0:T(8,128)(2,1)} %bitcast.18), calls=%async_computation.4 | async-start | bytes 2097152 | tf_op jit(solution)/shard_map/all_to_all | solution.py:618
  197.7 11.8 %weight_grad.1 = bf16[3,1024,512]{2,1,0:T(8,128)(2,1)} custom-call(s32[2]{0:T(128)} %pad_add_fusion.pos_ref, bf16[1024,1024]{1,0:T(8,128)(2,1)} %turn_tokens.1.own_ref, bf16[1024,1024]{1,0:T(8,128)(2,1)} %turn_shares.1.other_ref, bf16[8,2,3,48,1024]{4,3,2,1,0:T(8,128)(2,1)} %bitcast.27, bf16[8,2,3,48,1024]{4,3,2,1,0:T(8,128)(2,1)} %bitcast.28, ...), custom_call_target="tpu_custom_call" | custom-call | flops 6442450944 | bytes 13631488 | tf_op jit(solution)/shard_map/weight_grad/pallas_call | solution.py:535
  209.6 3.6 %all-to-all-done.4.parts_ref = bf16[4,128,1024]{2,1,0:T(8,128)(2,1)S(1)} async-done(((bf16[4,128,1024]{2,1,0:T(8,128)(2,1)}), bf16[4,128,1024]{2,1,0:T(8,128)(2,1)S(1)}, u32[]{:S(2)}, u32[]{:S(2)}) %all-to-all-start.4) | async-done | bytes 1048608 | tf_op jit(solution)/shard_map/all_to_all | solution.py:618
  213.1 0.9 token_total.1
  (15 shorter events, 0.1 us)
Async XLA Ops:
  7.2 1.6 copy-start
  9.4 9.7 %copy-start.4 = (f32[3,3,512]{2,1,0:T(4,128)S(1)}, f32[3,3,512]{2,1,0:T(4,128)}, u32[]{:S(2)}) copy-start(f32[3,3,512]{2,1,0:T(4,128)} %param.8) | copy-start | bytes 55300
  9.5 9.7 %copy-start.5 = (f32[512]{0:T(512)S(1)}, f32[512]{0:T(512)}, u32[]{:S(2)}) copy-start(f32[512]{0:T(512)} %param.10) | copy-start | bytes 6148
  11.0 31.0 %all-to-all-start = ((bf16[8,64,1024]{2,1,0:T(8,128)(2,1)}), bf16[8,64,1024]{2,1,0:T(8,128)(2,1)S(1)}, u32[]{:S(2)}, u32[]{:S(2)}) async-start(bf16[8,64,1024]{2,1,0:T(8,128)(2,1)} %bitcast.17), calls=%async_computation | async-start | bytes 2097152 | tf_op jit(solution)/shard_map/all_to_all | solution.py:618
  19.0 82.4 %all-gather.5.cloned.1.call-start = ((), (), s32[]{:S(2)}) async-start(), calls=%async_computation.5 | async-start | bytes 2359296 | tf_op jit(solution)/shard_map/all_gather | solution.py:668
  42.0 2.8 %copy-start.2 = (bf16[8,64,1024]{2,1,0:T(8,128)(2,1)}, bf16[8,64,1024]{2,1,0:T(8,128)(2,1)S(1)}, u32[]{:S(2)}) copy-start(bf16[8,64,1024]{2,1,0:T(8,128)(2,1)S(1)} %all-to-all-done.mine_ref) | copy-start | bytes 3145732
  42.0 2.8 %collective-permute-start = (bf16[8,64,1024]{2,1,0:T(8,128)(2,1)S(1)}, bf16[8,64,1024]{2,1,0:T(8,128)(2,1)}, u32[]{:S(2)}, u32[]{:S(2)}) collective-permute-start(bf16[8,64,1024]{2,1,0:T(8,128)(2,1)S(1)} %all-to-all-done.mine_ref), channel_id=1, source_target_pairs={{0,2},{2,0},{4,6},{6,4},{8,10},{10,8},{12,14},{14,12},{1,3},{3,1},... | collective-permute-start | bytes 3145736 | tf_op jit(solution)/shard_map/ppermute | solution.py:663
  42.1 9.4 %collective-permute-start.1 = (bf16[8,16,1024]{2,1,0:T(8,128)(2,1)S(1)}, bf16[8,16,1024]{2,1,0:T(8,128)(2,1)S(1)}, u32[]{:S(2)}, u32[]{:S(2)}) collective-permute-start(bf16[8,16,1024]{2,1,0:T(8,128)(2,1)S(1)} %constant_dynamic-slice_fusion), channel_id=1, source_target_pairs={{0,1},{1,0},{2,3},{3,2},{4,5},{5,4},{6,7},{7,6},{8,9},{9,8},{10,11... | collective-permute-start | bytes 786440 | tf_op jit(solution)/shard_map/ppermute | solution.py:666
  51.5 0.7 copy-start.3
  52.2 41.7 %all-to-all-start.1 = ((bf16[8,160,1024]{2,1,0:T(8,128)(2,1)}), bf16[8,160,1024]{2,1,0:T(8,128)(2,1)}, u32[]{:S(2)}, u32[]{:S(2)}) async-start(bf16[8,160,1024]{2,1,0:T(8,128)(2,1)} %get-tuple-element.45), calls=%async_computation.1 | async-start | bytes 5242880 | tf_op jit(solution)/shard_map/all_to_all | solution.py:618
  59.4 118.7 %all-gather.7.cloned.1.call-start = ((), (), s32[]{:S(2)}) async-start(), calls=%async_computation.6 | async-start | bytes 5013504 | tf_op jit(solution)/shard_map/all_gather | solution.py:677
  64.5 37.0 %copy-start.1 = (bf16[8,3,16,1024]{3,2,1,0:T(8,128)(2,1)S(1)}, bf16[8,3,16,1024]{3,2,1,0:T(8,128)(2,1)}, u32[]{:S(2)}) copy-start(bf16[8,3,16,1024]{3,2,1,0:T(8,128)(2,1)} %project_rest.1) | copy-start | bytes 2359300
  128.4 47.0 %all-to-all-start.3 = ((bf16[16,64,1024]{2,1,0:T(8,128)(2,1)}), bf16[16,64,1024]{2,1,0:T(8,128)(2,1)}, u32[]{:S(2)}, u32[]{:S(2)}) async-start(bf16[16,64,1024]{2,1,0:T(8,128)(2,1)} %operator_last.1), calls=%async_computation.3 | async-start | bytes 4194304 | tf_op jit(solution)/shard_map/all_to_all | solution.py:618
  187.8 2.9 %collective-permute-start.2 = (bf16[512,1024]{1,0:T(8,128)(2,1)}, bf16[512,1024]{1,0:T(8,128)(2,1)S(1)}, u32[]{:S(2)}, u32[]{:S(2)}) collective-permute-start(bf16[512,1024]{1,0:T(8,128)(2,1)} %get-tuple-element.66), channel_id=1, source_target_pairs={{0,2},{2,0},{4,6},{6,4},{8,10},{10,8},{12,14},{14,12},{1,3},{3,1},... | collective-permute-start | bytes 3145736 | tf_op jit(solution)/shard_map/ppermute | solution.py:691
  193.3 19.8 %all-to-all-start.4 = ((bf16[4,128,1024]{2,1,0:T(8,128)(2,1)}), bf16[4,128,1024]{2,1,0:T(8,128)(2,1)S(1)}, u32[]{:S(2)}, u32[]{:S(2)}) async-start(bf16[4,128,1024]{2,1,0:T(8,128)(2,1)} %bitcast.18), calls=%async_computation.4 | async-start | bytes 2097152 | tf_op jit(solution)/shard_map/all_to_all | solution.py:618
Sparse Core Ops, SparseCore 0:
  52.3 26.7 all-gather.4
  101.6 72.9 all-gather.6

commit v3 on v2

v3 whole, which is shorter than its diff:
```python
import functools
import math

import jax
import jax.numpy as jnp
from jax import lax
from jax.experimental import pallas as pl
from jax.experimental.pallas import tpu as pltpu
from jax.sharding import PartitionSpec as P

BF = jnp.bfloat16
F32 = jnp.float32
VMEM_BYTES = 60 << 20
NT = (((1,), (1,)), ((), ()))
NN = (((1,), (0,)), ((), ()))


def params(limit=VMEM_BYTES):
    return pltpu.CompilerParams(vmem_limit_bytes=limit)


def cost(flops, bytes_accessed):
    return pl.CostEstimate(flops=flops, bytes_accessed=bytes_accessed, transcendentals=0)


def kept(shape, dtype=BF):
    return pltpu.HBM(shape, dtype)


def matmul(left, right, dims):
    return lax.dot_general(left, right, dims, preferred_element_type=F32)


def split(value):
    high = value.astype(BF)
    return high, (value - high.astype(F32)).astype(BF)


def edge_kernel(pos_ref, cot_ref, filter_ref, out_ref):
    slabs = out_ref.shape[0]
    chans = filter_ref.shape[1] // slabs
    high, low = split(jnp.transpose(filter_ref[...]))
    taps = jnp.where(pos_ref[0] == 0, high.astype(F32), low.astype(F32)).astype(BF)
    cot = jnp.transpose(cot_ref[0].astype(F32)).astype(BF)
    for slab in range(slabs):
        part = slice(slab * chans, (slab + 1) * chans)
        fold(out_ref.at[slab], 0, jnp.concatenate([cot[part], taps[part]], axis=0))


def fold(out_ref, first, value):
    rows, block_len = value.shape
    count = rows * block_len // out_ref.shape[1]
    for pos in range(rows // count):
        out_ref[first : first + count, pos * block_len : (pos + 1) * block_len] = value[
            pos * count : (pos + 1) * count
        ]


def unfold(value, block_len):
    return jnp.concatenate(
        [value[:, at : at + block_len] for at in range(0, value.shape[1], block_len)], axis=0
    )


def edge_rows(pos, cotangent, long_filter, slabs, lanes):
    _, tok_rows, chan_cols = cotangent.shape
    full = pl.BlockSpec(memory_space=pltpu.VMEM)
    return pl.pallas_call(
        edge_kernel,
        in_specs=[pl.BlockSpec(memory_space=pltpu.SMEM), full, full],
        out_shape=kept((slabs, 2 * tok_rows * chan_cols // slabs // lanes, lanes)),
        compiler_params=params(),
        cost_estimate=cost(0, 8 * tok_rows * chan_cols),
        name="edge_rows",
    )(pos, cotangent, long_filter)


def flip_kernel(weight_ref, out_ref):
    out_ref[0] = jnp.transpose(weight_ref[0])


def flip_weight(weight):
    streams, slab_rows, chan_cols = weight.shape
    half = chan_cols // 2
    return pl.pallas_call(
        flip_kernel,
        grid=(streams, 2),
        in_specs=[pl.BlockSpec((1, slab_rows, half), lambda i, j: (i, 0, j))],
        out_specs=pl.BlockSpec((1, half, slab_rows), lambda i, j: (i, j, 0)),
        out_shape=kept((streams, chan_cols, slab_rows)),
        compiler_params=params(),
        cost_estimate=cost(0, 4 * weight.size),
        name="flip_weight",
    )(weight)


def table_kernel(cos_a_ref, sin_a_ref, cos_b_ref, sin_b_ref, out_ref):
    cos_a = cos_a_ref[0]
    sin_a = sin_a_ref[0]
    cos_b = cos_b_ref[...]
    sin_b = sin_b_ref[...]
    out_ref[0] = (cos_a * cos_b - sin_a * sin_b).astype(BF)
    out_ref[1] = (sin_a * cos_b + cos_a * sin_b).astype(BF)


def angle(product, period):
    phases = 2.0 * math.pi / period * (product % period).astype(F32)
    return jnp.cos(phases), jnp.sin(phases)


def tables(odd):
    steps = 64
    count = odd.shape[1]
    period = 8 * count
    base = jnp.arange(count // steps, dtype=jnp.int32)[:, None] * (2 * steps)
    fine = 2 * jnp.arange(steps, dtype=jnp.int32)[:, None] + 1
    cos_a, sin_a = angle(base * odd, period)
    cos_b, sin_b = angle(fine * odd, period)
    return pl.pallas_call(
        table_kernel,
        grid=(count // steps,),
        in_specs=[
            pl.BlockSpec((1, 1, count), lambda i: (i, 0, 0)),
            pl.BlockSpec((1, 1, count), lambda i: (i, 0, 0)),
            pl.BlockSpec((steps, count), lambda i: (0, 0)),
            pl.BlockSpec((steps, count), lambda i: (0, 0)),
        ],
        out_specs=pl.BlockSpec((2, steps, count), lambda i: (0, i, 0)),
        out_shape=jax.ShapeDtypeStruct((2, count, count), BF),
        compiler_params=params(),
        cost_estimate=cost(0, 4 * count * count),
        name="tables",
    )(cos_a[:, None], sin_a[:, None], cos_b, sin_b)


def project_kernel(core_ref, mine_ref, theirs_ref, weight_ref, edge_ref, out_ref, spread_ref):
    blocks, half, _ = mine_ref.shape
    core = core_ref[0]
    step = pl.program_id(0)

    @pl.when(step == 0)
    def _():
        for block in range(blocks):
            base = 2 * block * half
            spread_ref[pl.ds(pl.multiple_of(base + core * half, half), half)] = mine_ref[block]
            spread_ref[pl.ds(pl.multiple_of(base + (1 - core) * half, half), half)] = theirs_ref[block]
        out_ref[:, out_ref.shape[1] - edge_ref.shape[1] :] = edge_ref[...]

    slabs, _, positions = out_ref.shape
    chans = weight_ref.shape[1] // slabs
    result = matmul(weight_ref[0], spread_ref[...], NT).astype(BF).reshape(slabs, chans, positions)
    out_ref[:, pl.ds(pl.multiple_of(step * chans, chans), chans)] = result


def project(core, mine, theirs, weight, edge):
    blocks, half, width = mine.shape
    streams, rows, _ = weight.shape
    slabs, edge_len, positions = edge.shape
    out_dims = (slabs, streams * rows // slabs + edge_len, positions)
    return pl.pallas_call(
        project_kernel,
        grid_spec=pltpu.PrefetchScalarGridSpec(
            num_scalar_prefetch=1,
            grid=(streams,),
            in_specs=[
                pl.BlockSpec(mine.shape, lambda i, core: (0, 0, 0)),
                pl.BlockSpec(mine.shape, lambda i, core: (0, 0, 0)),
                pl.BlockSpec((1, rows, width), lambda i, core: (i, 0, 0)),
                pl.BlockSpec(edge.shape, lambda i, core: (0, 0, 0)),
            ],
            out_specs=[
                pl.BlockSpec(out_dims, lambda i, core: (0, 0, 0)),
                pl.BlockSpec((positions, width), lambda i, core: (0, 0)),
            ],
        ),
        out_shape=(kept(out_dims), kept((positions, width))),
        compiler_params=params(),
        cost_estimate=cost(
            2 * positions * width * streams * rows,
            2 * (2 * positions * width + weight.size + positions * streams * rows),
        ),
        name="project",
    )(core, mine, theirs, weight, edge)


def turn_kernel(tokens_ref, out_ref):
    out_ref[...] = jnp.transpose(tokens_ref[...])


def turn_tokens(tokens):
    positions, width = tokens.shape
    part = width // 4
    return pl.pallas_call(
        turn_kernel,
        grid=(4,),
        in_specs=[pl.BlockSpec((positions, part), lambda i: (0, i))],
        out_specs=pl.BlockSpec((part, positions), lambda i: (i, 0)),
        out_shape=kept((width, positions)),
        compiler_params=params(),
        cost_estimate=cost(0, 4 * tokens.size),
        name="turn_tokens",
    )(tokens)


def turn_shares_kernel(tokens_ref, out_ref, spread_ref):
    chips, cores, blocks, rows, _ = tokens_ref.shape
    for block in range(blocks):
        for core in range(cores):
            for chip in range(chips):
                base = ((block * cores + core) * chips + chip) * rows
                spread_ref[base : base + rows] = tokens_ref[chip, core, block]
    out_ref[...] = jnp.transpose(spread_ref[...])


def turn_shares(tokens):
    chips, cores, blocks, rows, width = tokens.shape
    positions = chips * cores * blocks * rows
    part = width // 4
    return pl.pallas_call(
        turn_shares_kernel,
        grid=(4,),
        in_specs=[pl.BlockSpec((chips, cores, blocks, rows, part), lambda i: (0, 0, 0, 0, i))],
        out_specs=pl.BlockSpec((part, positions), lambda i: (i, 0)),
        out_shape=kept((width, positions)),
        scratch_shapes=[pltpu.VMEM((positions, part), BF)],
        compiler_params=params(),
        cost_estimate=cost(0, 4 * tokens.size),
        name="turn_shares",
    )(tokens)


def delayed(value, steps):
    if steps == 0:
        return value
    lane = lax.broadcasted_iota(jnp.int32, value.shape, 1)
    return jnp.where(lane < steps, 0.0, pltpu.roll(value, steps, 1))


def advanced(value, steps):
    if steps == 0:
        return value
    lanes = value.shape[1]
    lane = lax.broadcasted_iota(jnp.int32, value.shape, 1)
    return jnp.where(lane >= lanes - steps, 0.0, pltpu.roll(value, lanes - steps, 1))


def transform(value, table):
    rows = value.shape[0]
    result = matmul(jnp.concatenate(split(value), axis=0), table, NN)
    return result[:rows] + result[rows:]


def operator_kernel(grad_scale, parts_ref, taps_ref, phase_ref, table_ref, grads_ref, out_ref, held_ref, sem):
    copy = pltpu.make_async_copy(table_ref, held_ref, sem)
    copy.start()
    devices, _, positions = parts_ref.shape
    block_len = out_ref.shape[2]
    batches = 2
    chans = taps_ref.shape[0]
    streams = grads_ref.shape[0] // (batches * chans)
    taps_len = (taps_ref.shape[1] - 1) // streams
    sources = devices // batches
    all_taps = jnp.concatenate([taps_ref[...]] * batches, axis=0)

    def tap(stream, pos):
        column = stream * taps_len + pos
        return all_taps[:, column : column + 1]

    def summed(batch, row):
        total = parts_ref[batch, row : row + chans].astype(F32)
        for source in range(1, sources):
            total = total + parts_ref[source * batches + batch, row : row + chans].astype(F32)
        return total

    def edge(batch):
        return jnp.concatenate(
            [
                unfold(parts_ref[source * batches + batch, streams * chans :], block_len).astype(F32)
                for source in range(sources)
            ],
            axis=1,
        )

    filtered = []
    for stream in range(streams):
        total = jnp.concatenate([summed(batch, stream * chans) for batch in range(batches)], axis=0)
        acc = tap(stream, 0) * total
        for pos in range(1, taps_len):
            acc = acc + tap(stream, pos) * delayed(total, pos)
        filtered.append(acc)
    query, key, value = filtered
    skip = all_taps[:, streams * taps_len : streams * taps_len + 1]
    edges = [edge(batch) for batch in range(batches)]
    cot = jnp.concatenate([rows[:chans] for rows in edges], axis=0)
    long_filter = edges[0][chans:] + edges[1][chans:]
    gated = key * value
    d_conv = cot * query
    stacked = jnp.concatenate([gated, d_conv, long_filter], axis=0)
    copy.wait()
    cos_all = transform(stacked, held_ref[0])
    sin_all = transform(stacked, held_ref[1])
    rows = batches * chans
    g_cos, d_cos, h_cos = cos_all[:rows], cos_all[rows : 2 * rows], cos_all[2 * rows :]
    g_sin, d_sin, h_sin = sin_all[:rows], sin_all[rows : 2 * rows], sin_all[2 * rows :]
    cos_phase = phase_ref[0:1]
    sin_phase = phase_ref[1:2]
    h_real = jnp.concatenate([h_cos * cos_phase + h_sin * sin_phase] * batches, axis=0)
    h_imag = jnp.concatenate([h_cos * sin_phase - h_sin * cos_phase] * batches, axis=0)
    conv_real = g_cos * h_real + g_sin * h_imag
    conv_imag = g_cos * h_imag - g_sin * h_real
    back_real = h_real * d_cos - h_imag * d_sin
    back_imag = -(h_real * d_sin + h_imag * d_cos)
    corr_real = g_cos * d_cos + g_sin * d_sin
    corr_imag = g_sin * d_cos - g_cos * d_sin
    corr_real = corr_real[:chans] + corr_real[chans:]
    corr_imag = corr_imag[:chans] + corr_imag[chans:]
    lag_real = corr_real * cos_phase + corr_imag * sin_phase
    lag_imag = corr_imag * cos_phase - corr_real * sin_phase
    real_all = jnp.concatenate([conv_real, back_real, lag_real], axis=0)
    imag_all = jnp.concatenate([conv_imag, back_imag, lag_imag], axis=0)
    result = transform(real_all, held_ref[0]) - transform(imag_all, held_ref[1])
    scale = 1.0 / positions
    conv_out = result[:rows] * scale + skip * gated
    d_gated = result[rows : 2 * rows] * scale + skip * d_conv
    filter_part = (result[2 * rows :] * (scale * grad_scale)).astype(BF)
    hyena_out = (query * conv_out).astype(BF)
    for device in range(devices):
        batch = device % batches
        lanes = slice(device // batches * block_len, (device // batches + 1) * block_len)
        out_ref[device, :chans] = hyena_out[batch * chans : (batch + 1) * chans, lanes]
        out_ref[device, chans:] = filter_part[:, lanes]
    for stream, grad in enumerate((cot * conv_out, d_gated * value, d_gated * key)):
        acc = tap(stream, 0) * grad
        for pos in range(1, taps_len):
            acc = acc + tap(stream, pos) * advanced(grad, pos)
        acc = acc.astype(BF)
        for batch in range(batches):
            row = (batch * streams + stream) * chans
            grads_ref[row : row + chans] = acc[batch * chans : (batch + 1) * chans]


def operator(parts, taps, phase, table, grad_scale, streams, block_len):
    devices, _, positions = parts.shape
    chans = taps.shape[0]
    rows = devices * block_len // positions * streams * chans
    full = pl.BlockSpec(memory_space=pltpu.VMEM)
    return pl.pallas_call(
        functools.partial(operator_kernel, grad_scale),
        in_specs=[full, full, full, pl.BlockSpec(memory_space=pl.ANY)],
        out_shape=(kept((rows, positions)), kept((devices, 2 * chans, block_len))),
        scratch_shapes=[pltpu.VMEM(table.shape, BF), pltpu.SemaphoreType.DMA],
        compiler_params=params(),
        cost_estimate=cost(8 * rows * positions * positions, 2 * (parts.size + table.size)),
        name="operator",
    )(parts, taps, phase, table)


def token_kernel(pos_ref, weight_ref, grads_ref, sent_ref, held_ref):
    streams, chips, _, rows, cols = weight_ref.shape
    positions = sent_ref.shape[1]
    weight = jnp.concatenate(
        [weight_ref[stream, :, 0].reshape(chips * rows, cols) for stream in range(streams)], axis=1
    )
    grads = jnp.concatenate(
        [grads_ref[:, 0, stream].reshape(cols, positions) for stream in range(streams)], axis=0
    )
    total = matmul(weight, grads, NN).astype(BF)

    @pl.when(pl.program_id(0) == 0)
    def _():
        sent_ref[...] = total

    @pl.when(pl.program_id(0) == 1)
    def _():
        held_ref[...] = total


def token_part(pos, weight, grads, chan_count):
    streams, slab_rows, cols = weight.shape
    slabs, _, _, chans, positions = grads.shape
    rows = slab_rows // chan_count
    return pl.pallas_call(
        token_kernel,
        grid_spec=pltpu.PrefetchScalarGridSpec(
            num_scalar_prefetch=1,
            grid=(2,),
            in_specs=[
                pl.BlockSpec(
                    (streams, chan_count // 2, 1, rows, cols),
                    lambda j, pos: (0, 0, jnp.where(j == 0, 1 - pos[1], pos[1]), 0, 0),
                ),
                pl.BlockSpec((slabs, 1, streams, chans, positions), lambda j, pos: (0, pos[0], 0, 0, 0)),
            ],
            out_specs=[pl.BlockSpec((slab_rows // 2, positions), lambda j, pos: (0, 0))] * 2,
        ),
        out_shape=(kept((slab_rows // 2, positions)), kept((slab_rows // 2, positions))),
        compiler_params=params(),
        cost_estimate=cost(2 * weight.size * positions, 8 * slab_rows * positions),
        name="token_part",
    )(pos, weight.reshape(streams, chan_count // 2, 2, rows, cols), grads)


def pair_kernel(held_ref, received_ref, out_ref):
    out_ref[...] = (held_ref[...].astype(F32) + received_ref[...].astype(F32)).astype(BF)


def pair_sum(held, received):
    rows, positions = held.shape
    block = pl.BlockSpec((rows // 4, positions), lambda i: (i, 0))
    return pl.pallas_call(
        pair_kernel,
        grid=(4,),
        in_specs=[block, block],
        out_specs=block,
        out_shape=kept((rows, positions)),
        compiler_params=params(24 << 20),
        cost_estimate=cost(0, 6 * held.size),
        name="pair_sum",
    )(held, received)


def weight_kernel(grad_scale, pos_ref, own_ref, other_ref, own_grads_ref, other_grads_ref, out_ref):
    chan_cols = out_ref.shape[2]
    positions = own_ref.shape[1]
    own = own_grads_ref[...].reshape(chan_cols, positions)
    other = other_grads_ref[...].reshape(chan_cols, positions)
    total = matmul(own_ref[...], own, NT) + matmul(other_ref[...], other, NT)
    out_ref[0] = (total * grad_scale).astype(BF)


def weight_grad(pos, own, other, grads, grad_scale):
    slabs, _, streams, chans, positions = grads.shape
    slab_rows = own.shape[0]
    chan_cols = slabs * chans
    block = (slabs, 1, 1, chans, positions)
    return pl.pallas_call(
        functools.partial(weight_kernel, grad_scale),
        grid_spec=pltpu.PrefetchScalarGridSpec(
            num_scalar_prefetch=1,
            grid=(streams,),
            in_specs=[
                pl.BlockSpec(own.shape, lambda i, pos: (0, 0)),
                pl.BlockSpec(own.shape, lambda i, pos: (0, 0)),
                pl.BlockSpec(block, lambda i, pos: (0, pos[0], i, 0, 0)),
                pl.BlockSpec(block, lambda i, pos: (0, 1 - pos[0], i, 0, 0)),
            ],
            out_specs=pl.BlockSpec((1, slab_rows, chan_cols), lambda i, pos: (i, 0, 0)),
        ),
        out_shape=jax.ShapeDtypeStruct((streams, slab_rows, chan_cols), BF),
        compiler_params=params(),
        cost_estimate=cost(
            4 * streams * slab_rows * chan_cols * positions,
            2 * (2 * own.size + grads.size + streams * slab_rows * chan_cols),
        ),
        name="weight_grad",
    )(pos, own, other, grads, grads)


def total_kernel(parts_ref, out_ref):
    total = parts_ref[0].astype(F32)
    for pos in range(1, parts_ref.shape[0]):
        total = total + parts_ref[pos].astype(F32)
    out_ref[0] = jnp.transpose(total).astype(BF)


def token_total(parts):
    _, rows, positions = parts.shape
    return pl.pallas_call(
        total_kernel,
        out_shape=jax.ShapeDtypeStruct((1, positions, rows), BF),
        compiler_params=params(24 << 20),
        cost_estimate=cost(0, 2 * parts.size),
        name="token_total",
    )(parts)


def finish_kernel(parts_ref, out_ref, filter_ref):
    slabs, rows, block_len = parts_ref.shape
    chans = rows // 2
    hyena = parts_ref[:, :chans].astype(F32).reshape(slabs * chans, block_len)
    filters = parts_ref[:, chans:].astype(F32).reshape(slabs * chans, block_len)
    out_ref[0] = jnp.transpose(hyena).astype(BF)
    filter_ref[...] = jnp.transpose(filters)


def finish(parts):
    slabs, rows, block_len = parts.shape
    chan_cols = slabs * rows // 2
    return pl.pallas_call(
        finish_kernel,
        out_shape=(
            jax.ShapeDtypeStruct((1, block_len, chan_cols), BF),
            jax.ShapeDtypeStruct((block_len, chan_cols), F32),
        ),
        compiler_params=params(24 << 20),
        cost_estimate=cost(0, 4 * parts.size),
        name="finish",
    )(parts)


def exchange(value, axis, groups=None):
    return lax.all_to_all(
        value, axis, split_axis=0, concat_axis=0, tiled=True, axis_index_groups=groups
    )


def local(tokens, in_weight, short_taps, long_filter, skip_gain, cotangent):
    seq_count = lax.axis_size("seq")
    dp_count = lax.axis_size("dp")
    dp_pos = lax.axis_index("dp").astype(jnp.int32)
    slab_pos = lax.axis_index("seq").astype(jnp.int32) * dp_count + dp_pos
    chan_count = lax.axis_size("chan")
    chan_pos = lax.axis_index("chan").astype(jnp.int32)
    core = chan_pos % 2
    pos = jnp.stack([dp_pos, core])
    tok_rows = tokens.shape[1]
    slab_rows = in_weight.shape[0]
    chan_cols = in_weight.shape[2]
    streams, taps_len = short_taps.shape[:2]
    positions = seq_count * tok_rows
    slabs = seq_count * dp_count
    chans = chan_cols // slabs
    half = tok_rows // 2
    share = tok_rows // chan_count
    chips = chan_count // 2
    grad_scale = 1.0 / math.sqrt(dp_count * positions)
    cores = [(i, i ^ 1) for i in range(chan_count)]
    weight = jnp.transpose(in_weight, (1, 0, 2))

    mine = lax.dynamic_slice_in_dim(tokens[0], core * half, half, 0)
    mine = jnp.transpose(mine.reshape(half, seq_count, slab_rows), (1, 0, 2))
    mine, edge, flipped = lax.optimization_barrier(
        (
            exchange(mine, "seq"),
            edge_rows(pos, cotangent, long_filter, slabs, positions),
            flip_weight(weight),
        )
    )
    theirs = lax.ppermute(mine, "chan", cores)
    parts, spread = project(core[None], mine, theirs, flipped, edge)

    shares = lax.dynamic_slice_in_dim(mine, chan_pos // 2 * share, share, 1)
    shares = lax.ppermute(shares, "dp", [(0, 1), (1, 0)])
    odd = 2 * jnp.arange(positions, dtype=jnp.int32)[None] + 1
    parts, shares, odd, short_taps = lax.optimization_barrier((parts, shares, odd, short_taps))
    shares = lax.all_gather(shares, "chan", axis=0)
    shares = shares.reshape(chips, 2, seq_count, share, slab_rows)
    taps = jnp.concatenate([short_taps.reshape(streams * taps_len, chan_cols), skip_gain[None]])
    taps = jnp.transpose(lax.dynamic_slice_in_dim(taps, slab_pos * chans, chans, 1))
    parts, table, taps, phase, own = lax.optimization_barrier(
        (
            exchange(parts, ("seq", "dp")),
            tables(odd),
            taps,
            jnp.concatenate(angle(odd, 8 * positions)),
            turn_tokens(spread),
        )
    )

    grads, outs = operator(parts, taps, phase, table, grad_scale, streams, tok_rows)
    grads, shares = lax.optimization_barrier((grads, shares))
    grads = lax.all_gather(grads, ("seq", "dp"), axis=0)
    finished = finish(exchange(outs, ("seq", "dp")))
    grads, finished, other = lax.optimization_barrier((grads, finished, turn_shares(shares)))
    hyena_out, grad_filter = finished

    grads = grads.reshape(slabs, dp_count, streams, chans, positions)
    sent, held = token_part(pos, weight, grads, chan_count)
    token_block = pair_sum(held, lax.ppermute(sent, "chan", cores))
    token_block = exchange(
        token_block.reshape(chips, -1, positions),
        "chan",
        [[chip * 2 + side for chip in range(chips)] for side in range(2)],
    )
    grad_tokens = token_total(token_block)
    grad_weight = weight_grad(pos, own, other, grads, grad_scale)
    return (hyena_out, grad_tokens, jnp.transpose(grad_weight, (1, 0, 2)), grad_filter)


def solution(mesh):
    placed = (
        P("dp", "seq", None),
        P("seq", None, "chan"),
        P(None, None, "chan"),
        P("seq", "chan"),
        P("chan"),
        P("dp", "seq", "chan"),
    )
    return jax.shard_map(
        local,
        mesh=mesh,
        in_specs=placed,
        out_specs=(
            P("dp", "seq", "chan"),
            P("dp", None, ("seq", "chan")),
            P("seq", None, "chan"),
            P("seq", "chan"),
        ),
        check_vma=False,
    )
```

time: 222 us -> 216 us (0.973)
  waiting for transfers between devices: 71.4 us -> 93 us
  Pallas kernels: 76.1 us -> 64.5 us
  starting transfers between devices: 25.1 us -> 17.6 us
  blocking collectives: 20.3 us -> 13.2 us
  other arithmetic: 8.55 us -> 5.95 us
    all_gather x1, waiting for transfers between devices: 0.01 us -> 42.1 us  [local(): grads = lax.all_gather(grads, ('seq', 'dp'), axis=0)]
    all_to_all x4 -> x3, waiting for transfers between devices: 66.5 us -> 45.9 us  [exchange(): lax.all_to_all(value, axis, split_axis=0, concat_axis=0, tiled=True, axis...]
    pallas_call x7 -> x6, Pallas kernels: 36.1 us -> 26 us  [the longest x1 8.14 us: operator(): pl.pallas_call(functools.partial(operator_kernel, grad_scale), in_specs=[...]
    all_to_all x4 -> x3, starting transfers between devices: 24.2 us -> 16.8 us  [exchange(): lax.all_to_all(value, axis, split_axis=0, concat_axis=0, tiled=True, axis...]
    all_to_all x1, blocking collectives: 20.3 us -> 13.2 us  [exchange(): lax.all_to_all(value, axis, split_axis=0, concat_axis=0, tiled=True, axis...]
    convert_element_type x1 -> x0, other arithmetic: 2.61 us -> none  [local(): token_block = (held.astype(F32) + received.astype(F32)).astype(BF)]
    sin x3 -> x2, other arithmetic: 4.54 us -> 4.41 us  [angle(): return (jnp.cos(phases), jnp.sin(phases))]
  transfers between devices with their start and end apart: 9 -> 8, of which waited for: 5 -> 6; matrix products, arithmetic and copies ran while one was open for 3% -> 3% of each run, Pallas kernels for 30% -> 25%
where the time goes in v3:
time: 216 us; the launch traced here: 215 us
  waiting for transfers between devices  93 us (43%)
  Pallas kernels  64.5 us (30%)
  starting transfers between devices  17.6 us (8%)
  between operations  14.2 us (7%)
  blocking collectives  13.2 us (6%)
  local copies, waits for them, and re-layouts  6.61 us (3%)
  other arithmetic  5.95 us (3%)
    all_to_all x3, waiting for transfers between devices, exchange(): lax.all_to_all(value, axis, split_axis=0, concat_axis=0, tiled=True, axis...  45.9 us
    all_gather x1, waiting for transfers between devices, local(): grads = lax.all_gather(grads, ('seq', 'dp'), axis=0)  42.1 us
    all_to_all x3, starting transfers between devices, exchange(): lax.all_to_all(value, axis, split_axis=0, concat_axis=0, tiled=True, axis...  16.8 us
    all_to_all x1, blocking collectives, exchange(): lax.all_to_all(value, axis, split_axis=0, concat_axis=0, tiled=True, axis...  13.2 us
    pallas_call x1, Pallas kernels, weight_grad(): pl.pallas_call(functools.partial(weight_kernel, grad_scale), grid_spec=pl...  11.7 us
    pallas_call x1, Pallas kernels, tables(): pl.pallas_call(table_kernel, grid=(count // steps,), in_specs=[pl.BlockSp...  9.2 us
    pallas_call x1, Pallas kernels, token_part(): pl.pallas_call(token_kernel, grid_spec=pltpu.PrefetchScalarGridSpec(num_s...  8.28 us
    pallas_call x1, Pallas kernels, operator(): pl.pallas_call(functools.partial(operator_kernel, grad_scale), in_specs=[...  8.14 us
  transfers between devices with their start and end apart: 8, of which 6 were waited for; matrix products, arithmetic and copies ran while one was open for 3% of the time, Pallas kernels for 25%

profile of v3, /device:TPU:0, one launch (start us, length us, event | category | flops | bytes accessed | tf_op | source)
XLA Modules:
  0.0 215.0 jit_solution(13926098562151449732)
XLA Ops:
  7.2 0.0 copy-start
  7.2 1.6 copy-done
  8.8 0.1 constant_dynamic-slice_fusion.1
  8.8 0.6 copy.20
  9.4 1.6 copy.27
  11.0 8.0 %all-to-all-start = ((bf16[8,64,1024]{2,1,0:T(8,128)(2,1)}), bf16[8,64,1024]{2,1,0:T(8,128)(2,1)S(1)}, u32[]{:S(2)}, u32[]{:S(2)}) async-start(bf16[8,64,1024]{2,1,0:T(8,128)(2,1)} %bitcast.18), calls=%async_computation | async-start | bytes 2097152 | tf_op jit(solution)/shard_map/all_to_all | solution.py:502
  19.1 0.0 all-gather.5.cloned.1.call-start
  19.1 5.7 %flip_weight.1.weight_ref = bf16[3,512,1024]{2,1,0:T(8,128)(2,1)} custom-call(bf16[3,1024,512]{2,1,0:T(8,128)(2,1)} %bitcast.22), custom_call_target="tpu_custom_call" | custom-call | bytes 6291456 | tf_op jit(solution)/shard_map/flip_weight/pallas_call | solution.py:85
  24.8 0.6 pad_add_fusion.pos_ref
  25.4 1.9 edge_rows.1.edge_ref
  27.3 8.9 %all-to-all-done.mine_ref = bf16[8,64,1024]{2,1,0:T(8,128)(2,1)S(1)} async-done(((bf16[8,64,1024]{2,1,0:T(8,128)(2,1)}), bf16[8,64,1024]{2,1,0:T(8,128)(2,1)S(1)}, u32[]{:S(2)}, u32[]{:S(2)}) %all-to-all-start) | async-done | bytes 1048608 | tf_op jit(solution)/shard_map/all_to_all | solution.py:502
  36.3 0.0 collective-permute-start
  36.3 0.8 collective-permute-start.1
  37.1 2.0 collective-permute-done.theirs_ref
  39.1 7.7 %project.1 = (bf16[16,104,1024]{2,1,0:T(8,128)(2,1)}, bf16[1024,1024]{1,0:T(8,128)(2,1)}) custom-call(s32[1]{0:T(128)} %bitcast.core_ref, bf16[8,64,1024]{2,1,0:T(8,128)(2,1)} %copy-done.2, bf16[8,64,1024]{2,1,0:T(8,128)(2,1)} %collective-permute-done.theirs_ref, bf16[3,512,1024]{2,1,0:T(8,128)(2,1)} %flip_weight.1.weight_ref, ...), custom_call_target="tpu_custom_call" | custom-call | flops 3221225472 | bytes 10485760 | tf_op jit(solution)/shard_map/project/pallas_call | solution.py:160
  46.7 0.0 collective-permute-done.1
  46.8 0.7 copy-done.3
  47.5 0.0 all-gather.5.cloned.1.call-update
  47.5 0.0 copy-start.4
  47.5 0.0 copy-start.5
  47.5 4.5 %all-to-all-start.1 = ((bf16[16,104,1024]{2,1,0:T(8,128)(2,1)}), bf16[16,104,1024]{2,1,0:T(8,128)(2,1)}, u32[]{:S(2)}, u32[]{:S(2)}) async-start(bf16[16,104,1024]{2,1,0:T(8,128)(2,1)} %get-tuple-element.34), calls=%async_computation.1 | async-start | bytes 6815744 | tf_op jit(solution)/shard_map/all_to_all | solution.py:502
  52.0 0.0 all-gather.7.cloned.1.call-start
  52.1 0.1 fusion.13
  52.2 0.1 sin.18
  52.4 0.1 fusion.7
  52.5 0.7 copy.19
  53.2 4.2 %turn_tokens.1.own_ref = bf16[1024,1024]{1,0:T(8,128)(2,1)} custom-call(bf16[1024,1024]{1,0:T(8,128)(2,1)} %get-tuple-element.37.tokens_ref), custom_call_target="tpu_custom_call" | custom-call | bytes 4194304 | tf_op jit(solution)/shard_map/turn_tokens/pallas_call | solution.py:193
  57.4 0.1 fusion.5
  57.5 2.5 %fusion.11 = (f32[16,1,1024]{2,1,0:T(1,128)}, f32[16,1,1024]{2,1,0:T(1,128)}) fusion(f32[16,1,1024]{2,0,1:T(8,128)S(1)} %fusion.5), kind=kLoop, calls=%fused_computation.30 | loop fusion | flops 16384 | bytes 196608 | tf_op jit(solution)/shard_map/sin | solution.py:108
  60.0 1.9 fusion.3
  61.9 9.2 %tables.1.table_ref = bf16[2,1024,1024]{2,1,0:T(8,128)(2,1)} custom-call(f32[16,1,1024]{2,1,0:T(1,128)} %get-tuple-element.59.cos_a_ref, f32[16,1,1024]{2,1,0:T(1,128)} %get-tuple-element.58.sin_a_ref, f32[64,1024]{1,0:T(8,128)} %get-tuple-element.61.cos_b_ref, f32[64,1024]{1,0:T(8,128)} %get-tuple-element.60.sin_b_ref), custom_call_target="tpu_custom_call" | custom-call | bytes 4194304 | tf_op jit(solution)/shard_map/tables/pallas_call | solution.py:119
  71.1 0.6 pad_maximum_fusion.phase_ref
  71.7 33.3 %all-to-all-done.1.parts_ref = bf16[16,104,1024]{2,1,0:T(8,128)(2,1)} async-done(((bf16[16,104,1024]{2,1,0:T(8,128)(2,1)}), bf16[16,104,1024]{2,1,0:T(8,128)(2,1)}, u32[]{:S(2)}, u32[]{:S(2)}) %all-to-all-start.1) | async-done | bytes 3407904 | tf_op jit(solution)/shard_map/all_to_all | solution.py:502
  105.0 8.1 %operator.1 = (bf16[192,1024]{1,0:T(8,128)(2,1)}, bf16[16,64,128]{2,1,0:T(8,128)(2,1)}) custom-call(bf16[16,104,1024]{2,1,0:T(8,128)(2,1)} %all-to-all-done.1.parts_ref, f32[32,10]{1,0:T(8,128)} %bitcast.25, f32[2,1024]{1,0:T(2,128)} %pad_maximum_fusion.phase_ref, bf16[2,1024,1024]{2,1,0:T(8,128)(2,1)} %tables.1.table_ref), custom_call_target="tpu_custom_call" | custom-call | flops 1610612736 | bytes 7602176 | tf_op jit(solution)/shard_map/operator/pallas_call | solution.py:347
  113.1 0.0 all-gather.5.cloned.1.call-done
  113.2 0.0 all-gather.7.cloned.1.call-update
  113.2 13.2 %all_to_all.20.parts_ref = bf16[16,64,128]{2,1,0:T(8,128)(2,1)S(1)} all-to-all(bf16[16,64,128]{2,1,0:T(8,128)(2,1)} %get-tuple-element.45), channel_id=1, replica_groups=mesh['seq'=8,'chan'=8,'dp'=2] {'seq','dp'}, dimensions={0} | all-to-all | bytes 524288 | tf_op jit(solution)/shard_map/all_to_all | solution.py:502
  126.4 0.9 finish.1
  127.2 4.2 %turn_shares.1.other_ref = bf16[1024,1024]{1,0:T(8,128)(2,1)} custom-call(bf16[4,2,8,16,1024]{4,3,2,1,0:T(8,128)(2,1)} %bitcast.24), custom_call_target="tpu_custom_call" | custom-call | bytes 4194304 | tf_op jit(solution)/shard_map/turn_shares/pallas_call | solution.py:219
  131.4 42.1 %all-gather.7.cloned.1.call-done = bf16[3072,1024]{1,0:T(8,128)(2,1)} async-done(((bf16[192,1024]{1,0:T(8,128)(2,1)}), bf16[3072,1024]{1,0:T(8,128)(2,1)}) %all-gather.7.cloned.1.call-update) | async-done | bytes 6291472 | tf_op jit(solution)/shard_map/all_gather | solution.py:562
  173.6 8.3 %token_part.1 = (bf16[512,1024]{1,0:T(8,128)(2,1)}, bf16[512,1024]{1,0:T(8,128)(2,1)}) custom-call(s32[2]{0:T(128)} %pad_add_fusion.pos_ref, bf16[3,4,2,128,512]{4,3,2,1,0:T(8,128)(2,1)} %bitcast.23, bf16[16,2,3,32,1024]{4,3,2,1,0:T(8,128)(2,1)} %bitcast.29), custom_call_target="tpu_custom_call" | custom-call | flops 3221225472 | bytes 8388608 | tf_op jit(solution)/shard_map/token_part/pallas_call | solution.py:382
  181.8 2.9 %collective-permute-done.2.received_ref = bf16[512,1024]{1,0:T(8,128)(2,1)S(1)} collective-permute-done((bf16[512,1024]{1,0:T(8,128)(2,1)}, bf16[512,1024]{1,0:T(8,128)(2,1)S(1)}, u32[]{:S(2)}, u32[]{:S(2)}) %collective-permute-start.2) | collective-permute-done | bytes 1048608 | tf_op jit(solution)/shard_map/ppermute | solution.py:569
  184.7 1.2 copy-done.1
  185.9 1.7 pair_sum.1
  187.6 4.2 %all-to-all-start.3 = ((bf16[4,128,1024]{2,1,0:T(8,128)(2,1)}), bf16[4,128,1024]{2,1,0:T(8,128)(2,1)S(1)}, u32[]{:S(2)}, u32[]{:S(2)}) async-start(bf16[4,128,1024]{2,1,0:T(8,128)(2,1)} %bitcast.19), calls=%async_computation.3 | async-start | bytes 2097152 | tf_op jit(solution)/shard_map/all_to_all | solution.py:502
  191.9 11.7 %weight_grad.1 = bf16[3,1024,512]{2,1,0:T(8,128)(2,1)} custom-call(s32[2]{0:T(128)} %pad_add_fusion.pos_ref, bf16[1024,1024]{1,0:T(8,128)(2,1)} %turn_tokens.1.own_ref, bf16[1024,1024]{1,0:T(8,128)(2,1)} %turn_shares.1.other_ref, bf16[16,2,3,32,1024]{4,3,2,1,0:T(8,128)(2,1)} %bitcast.30, bf16[16,2,3,32,1024]{4,3,2,1,0:T(8,128)(2,1)} %bitcast.31), custom_call_target="tpu_custom_call" | custom-call | flops 6442450944 | bytes 13631488 | tf_op jit(solution)/shard_map/weight_grad/pallas_call | solution.py:436
  203.6 3.7 %all-to-all-done.3.parts_ref = bf16[4,128,1024]{2,1,0:T(8,128)(2,1)S(1)} async-done(((bf16[4,128,1024]{2,1,0:T(8,128)(2,1)}), bf16[4,128,1024]{2,1,0:T(8,128)(2,1)S(1)}, u32[]{:S(2)}, u32[]{:S(2)}) %all-to-all-start.3) | async-done | bytes 1048608 | tf_op jit(solution)/shard_map/all_to_all | solution.py:502
  207.3 0.9 token_total.1
  (12 shorter events, 0.1 us)
Async XLA Ops:
  7.2 1.6 copy-start
  11.0 25.2 %all-to-all-start = ((bf16[8,64,1024]{2,1,0:T(8,128)(2,1)}), bf16[8,64,1024]{2,1,0:T(8,128)(2,1)S(1)}, u32[]{:S(2)}, u32[]{:S(2)}) async-start(bf16[8,64,1024]{2,1,0:T(8,128)(2,1)} %bitcast.18), calls=%async_computation | async-start | bytes 2097152 | tf_op jit(solution)/shard_map/all_to_all | solution.py:502
  19.1 94.1 %all-gather.5.cloned.1.call-start = ((), (), s32[]{:S(2)}) async-start(), calls=%async_computation.4 | async-start | bytes 2359296 | tf_op jit(solution)/shard_map/all_gather | solution.py:546
  36.3 2.8 %copy-start.2 = (bf16[8,64,1024]{2,1,0:T(8,128)(2,1)}, bf16[8,64,1024]{2,1,0:T(8,128)(2,1)S(1)}, u32[]{:S(2)}) copy-start(bf16[8,64,1024]{2,1,0:T(8,128)(2,1)S(1)} %all-to-all-done.mine_ref) | copy-start | bytes 3145732
  36.3 2.8 %collective-permute-start = (bf16[8,64,1024]{2,1,0:T(8,128)(2,1)S(1)}, bf16[8,64,1024]{2,1,0:T(8,128)(2,1)}, u32[]{:S(2)}, u32[]{:S(2)}) collective-permute-start(bf16[8,64,1024]{2,1,0:T(8,128)(2,1)S(1)} %all-to-all-done.mine_ref), channel_id=1, source_target_pairs={{0,2},{2,0},{4,6},{6,4},{8,10},{10,8},{12,14},{14,12},{1,3},{3,1},... | collective-permute-start | bytes 3145736 | tf_op jit(solution)/shard_map/ppermute | solution.py:539
  36.3 10.4 %collective-permute-start.1 = (bf16[8,16,1024]{2,1,0:T(8,128)(2,1)S(1)}, bf16[8,16,1024]{2,1,0:T(8,128)(2,1)S(1)}, u32[]{:S(2)}, u32[]{:S(2)}) collective-permute-start(bf16[8,16,1024]{2,1,0:T(8,128)(2,1)S(1)} %constant_dynamic-slice_fusion), channel_id=1, source_target_pairs={{0,1},{1,0},{2,3},{3,2},{4,5},{5,4},{6,7},{7,6},{8,9},{9,8},{10,11... | collective-permute-start | bytes 786440 | tf_op jit(solution)/shard_map/ppermute | solution.py:543
  46.8 0.7 copy-start.3
  47.5 4.9 %copy-start.4 = (f32[3,3,512]{2,1,0:T(4,128)S(1)}, f32[3,3,512]{2,1,0:T(4,128)}, u32[]{:S(2)}) copy-start(f32[3,3,512]{2,1,0:T(4,128)} %param.8) | copy-start | bytes 55300
  47.5 4.9 %copy-start.5 = (f32[512]{0:T(512)S(1)}, f32[512]{0:T(512)}, u32[]{:S(2)}) copy-start(f32[512]{0:T(512)} %param.10) | copy-start | bytes 6148
  47.5 57.5 %all-to-all-start.1 = ((bf16[16,104,1024]{2,1,0:T(8,128)(2,1)}), bf16[16,104,1024]{2,1,0:T(8,128)(2,1)}, u32[]{:S(2)}, u32[]{:S(2)}) async-start(bf16[16,104,1024]{2,1,0:T(8,128)(2,1)} %get-tuple-element.34), calls=%async_computation.1 | async-start | bytes 6815744 | tf_op jit(solution)/shard_map/all_to_all | solution.py:502
  52.0 121.5 %all-gather.7.cloned.1.call-start = ((), (), s32[]{:S(2)}) async-start(), calls=%async_computation.5 | async-start | bytes 6684672 | tf_op jit(solution)/shard_map/all_gather | solution.py:562
  181.8 2.9 %collective-permute-start.2 = (bf16[512,1024]{1,0:T(8,128)(2,1)}, bf16[512,1024]{1,0:T(8,128)(2,1)S(1)}, u32[]{:S(2)}, u32[]{:S(2)}) collective-permute-start(bf16[512,1024]{1,0:T(8,128)(2,1)} %get-tuple-element.52), channel_id=1, source_target_pairs={{0,2},{2,0},{4,6},{6,4},{8,10},{10,8},{12,14},{14,12},{1,3},{3,1},... | collective-permute-start | bytes 3145736 | tf_op jit(solution)/shard_map/ppermute | solution.py:569
  184.7 1.2 copy-start.1
  187.6 19.6 %all-to-all-start.3 = ((bf16[4,128,1024]{2,1,0:T(8,128)(2,1)}), bf16[4,128,1024]{2,1,0:T(8,128)(2,1)S(1)}, u32[]{:S(2)}, u32[]{:S(2)}) async-start(bf16[4,128,1024]{2,1,0:T(8,128)(2,1)} %bitcast.19), calls=%async_computation.3 | async-start | bytes 2097152 | tf_op jit(solution)/shard_map/all_to_all | solution.py:502
Sparse Core Ops, SparseCore 0:
  47.6 22.2 all-gather.4
  113.3 60.1 all-gather.6

commit v4 on v3

--- a/solution.py
+++ b/solution.py
@@ -3,6 +3,7 @@
 
 import jax
 import jax.numpy as jnp
+import numpy as np
 from jax import lax
 from jax.experimental import pallas as pl
 from jax.experimental.pallas import tpu as pltpu
@@ -25,6 +26,10 @@
 
 def kept(shape, dtype=BF):
     return pltpu.HBM(shape, dtype)
+
+
+def stay(value):
+    return pltpu.with_memory_space_constraint(value, pltpu.HBM)
 
 
 def matmul(left, right, dims):
@@ -94,112 +99,144 @@
     )(weight)
 
 
-def table_kernel(cos_a_ref, sin_a_ref, cos_b_ref, sin_b_ref, out_ref):
-    cos_a = cos_a_ref[0]
-    sin_a = sin_a_ref[0]
-    cos_b = cos_b_ref[...]
-    sin_b = sin_b_ref[...]
-    out_ref[0] = (cos_a * cos_b - sin_a * sin_b).astype(BF)
-    out_ref[1] = (sin_a * cos_b + cos_a * sin_b).astype(BF)
-
-
-def angle(product, period):
-    phases = 2.0 * math.pi / period * (product % period).astype(F32)
-    return jnp.cos(phases), jnp.sin(phases)
-
-
-def tables(odd):
-    steps = 64
-    count = odd.shape[1]
-    period = 8 * count
-    base = jnp.arange(count // steps, dtype=jnp.int32)[:, None] * (2 * steps)
-    fine = 2 * jnp.arange(steps, dtype=jnp.int32)[:, None] + 1
-    cos_a, sin_a = angle(base * odd, period)
-    cos_b, sin_b = angle(fine * odd, period)
-    return pl.pallas_call(
-        table_kernel,
-        grid=(count // steps,),
-        in_specs=[
-            pl.BlockSpec((1, 1, count), lambda i: (i, 0, 0)),
-            pl.BlockSpec((1, 1, count), lambda i: (i, 0, 0)),
-            pl.BlockSpec((steps, count), lambda i: (0, 0)),
-            pl.BlockSpec((steps, count), lambda i: (0, 0)),
-        ],
-        out_specs=pl.BlockSpec((2, steps, count), lambda i: (0, i, 0)),
-        out_shape=jax.ShapeDtypeStruct((2, count, count), BF),
+BLOCKS = 4
+
+
+def block_angle(residue, block):
+    return math.pi * (2 * residue + 1) * block / (2 * BLOCKS)
+
+
+def frequencies(count, residue):
+    steps = 2 * BLOCKS * np.arange(count // (2 * BLOCKS))
+    return steps + residue, steps + 2 * BLOCKS - 1 - residue
+
+
+def transform_tables(count):
+    width = count // BLOCKS
+    tables, phases = [], []
+    for residue in range(BLOCKS):
+        columns, rows = [], []
+        for side, freq in zip((1.0, -1.0), frequencies(count, residue)):
+            angles = math.pi / (4 * count) * (2 * np.arange(width)[:, None] + 1) * (2 * freq[None] + 1)
+            cos, sin = np.cos(angles), np.sin(angles)
+            columns += [np.concatenate([cos, side * sin]), np.concatenate([-sin, side * cos])]
+            rows.append(math.pi / (4 * count) * (2 * freq + 1))
+        tables.append(np.concatenate(columns, axis=1))
+        rows = np.concatenate(rows)
+        phases += [np.cos(rows), np.sin(rows)]
+    return jnp.asarray(np.stack(tables), BF), jnp.asarray(np.stack(phases), F32)
+
+
+def cut_kernel(pos_ref, tokens_ref, out_ref, sems):
+    slabs, half, width = out_ref.shape
+    start = pl.multiple_of(pos_ref[1] * half, half)
+    copies = [
+        pltpu.make_async_copy(
+            tokens_ref.at[0, pl.ds(start, half), slice(slab * width, (slab + 1) * width)],
+            out_ref.at[slab],
+            sems.at[slab],
+        )
+        for slab in range(slabs)
+    ]
+    for copy in copies:
+        copy.start()
+    for copy in copies:
+        copy.wait()
+
+
+def cut_tokens(pos, tokens, slabs):
+    _, rows, width = tokens.shape
+    return pl.pallas_call(
+        cut_kernel,
+        in_specs=[pl.BlockSpec(memory_space=pltpu.SMEM), pl.BlockSpec(memory_space=pl.ANY)],
+        out_specs=pl.BlockSpec(memory_space=pl.ANY),
+        out_shape=kept((slabs, rows // 2, width // slabs)),
+        scratch_shapes=[pltpu.SemaphoreType.DMA((slabs,))],
         compiler_params=params(),
-        cost_estimate=cost(0, 4 * count * count),
-        name="tables",
-    )(cos_a[:, None], sin_a[:, None], cos_b, sin_b)
-
-
-def project_kernel(core_ref, mine_ref, theirs_ref, weight_ref, edge_ref, out_ref, spread_ref):
+        cost_estimate=cost(0, 2 * tokens.size),
+        name="cut_tokens",
+    )(pos, tokens)
+
+
+def in_order(core, mine_ref, theirs_ref, spread_ref):
     blocks, half, _ = mine_ref.shape
-    core = core_ref[0]
+    for block in range(blocks):
+        base = 2 * block * half
+        spread_ref[pl.ds(pl.multiple_of(base + core * half, half), half)] = mine_ref[block]
+        spread_ref[pl.ds(pl.multiple_of(base + (1 - core) * half, half), half)] = theirs_ref[block]
+
+
+def project_kernel(pos_ref, mine_ref, theirs_ref, weight_ref, edge_ref, out_ref, spread_ref):
     step = pl.program_id(0)
+    last = pl.num_programs(0) - 1
 
     @pl.when(step == 0)
     def _():
-        for block in range(blocks):
-            base = 2 * block * half
-            spread_ref[pl.ds(pl.multiple_of(base + core * half, half), half)] = mine_ref[block]
-            spread_ref[pl.ds(pl.multiple_of(base + (1 - core) * half, half), half)] = theirs_ref[block]
-        out_ref[:, out_ref.shape[1] - edge_ref.shape[1] :] = edge_ref[...]
-
-    slabs, _, positions = out_ref.shape
-    chans = weight_ref.shape[1] // slabs
-    result = matmul(weight_ref[0], spread_ref[...], NT).astype(BF).reshape(slabs, chans, positions)
-    out_ref[:, pl.ds(pl.multiple_of(step * chans, chans), chans)] = result
-
-
-def project(core, mine, theirs, weight, edge):
+        in_order(pos_ref[1], mine_ref, theirs_ref, spread_ref)
+
+    @pl.when(step < last)
+    def _():
+        result = matmul(weight_ref[0], spread_ref[...], NT).astype(BF)
+        out_ref[...] = result.reshape(out_ref.shape)
+
+    @pl.when(step == last)
+    def _():
+        out_ref[:, : edge_ref.shape[1]] = edge_ref[...]
+
+
+def project(pos, mine, theirs, weight, edge):
     blocks, half, width = mine.shape
     streams, rows, _ = weight.shape
     slabs, edge_len, positions = edge.shape
-    out_dims = (slabs, streams * rows // slabs + edge_len, positions)
+    chans = rows // slabs
     return pl.pallas_call(
         project_kernel,
         grid_spec=pltpu.PrefetchScalarGridSpec(
             num_scalar_prefetch=1,
-            grid=(streams,),
+            grid=(streams + 1,),
             in_specs=[
-                pl.BlockSpec(mine.shape, lambda i, core: (0, 0, 0)),
-                pl.BlockSpec(mine.shape, lambda i, core: (0, 0, 0)),
-                pl.BlockSpec((1, rows, width), lambda i, core: (i, 0, 0)),
-                pl.BlockSpec(edge.shape, lambda i, core: (0, 0, 0)),
+                pl.BlockSpec(memory_space=pltpu.VMEM),
+                pl.BlockSpec(memory_space=pltpu.VMEM),
+                pl.BlockSpec((1, rows, width), lambda i, pos: (jnp.minimum(i, streams - 1), 0, 0)),
+                pl.BlockSpec(edge.shape, lambda i, pos: (0, 0, 0)),
             ],
-            out_specs=[
-                pl.BlockSpec(out_dims, lambda i, core: (0, 0, 0)),
-                pl.BlockSpec((positions, width), lambda i, core: (0, 0)),
-            ],
-        ),
-        out_shape=(kept(out_dims), kept((positions, width))),
-        compiler_params=params(),
+            out_specs=pl.BlockSpec((slabs, chans, positions), lambda i, pos: (0, i, 0)),
+            scratch_shapes=[pltpu.VMEM((positions, width), BF)],
+        ),
+        out_shape=kept((slabs, streams * chans + edge_len, positions)),
+        compiler_params=params(36 << 20),
         cost_estimate=cost(
             2 * positions * width * streams * rows,
-            2 * (2 * positions * width + weight.size + positions * streams * rows),
+            2 * (positions * width + weight.size + positions * streams * rows),
         ),
         name="project",
-    )(core, mine, theirs, weight, edge)
-
-
-def turn_kernel(tokens_ref, out_ref):
-    out_ref[...] = jnp.transpose(tokens_ref[...])
-
-
-def turn_tokens(tokens):
-    positions, width = tokens.shape
+    )(pos, mine, theirs, stay(weight), stay(edge))
+
+
+def turn_kernel(pos_ref, mine_ref, theirs_ref, out_ref, spread_ref):
+    in_order(pos_ref[1], mine_ref, theirs_ref, spread_ref)
+    out_ref[...] = jnp.transpose(spread_ref[...])
+
+
+def turn_tokens(pos, mine, theirs):
+    blocks, half, width = mine.shape
+    positions = 2 * blocks * half
     part = width // 4
+    block = pl.BlockSpec((blocks, half, part), lambda i, pos: (0, 0, i))
     return pl.pallas_call(
         turn_kernel,
-        grid=(4,),
-        in_specs=[pl.BlockSpec((positions, part), lambda i: (0, i))],
-        out_specs=pl.BlockSpec((part, positions), lambda i: (i, 0)),
+        grid_spec=pltpu.PrefetchScalarGridSpec(
+            num_scalar_prefetch=1,
+            grid=(4,),
+            in_specs=[block, block],
+            out_specs=pl.BlockSpec((part, positions), lambda i, pos: (i, 0)),
+            scratch_shapes=[pltpu.VMEM((positions, part), BF)],
+        ),
         out_shape=kept((width, positions)),
         compiler_params=params(),
-        cost_estimate=cost(0, 4 * tokens.size),
+        cost_estimate=cost(0, 4 * positions * width),
         name="turn_tokens",
-    )(tokens)
+    )(pos, mine, theirs)
 
 
 def turn_shares_kernel(tokens_ref, out_ref, spread_ref):
@@ -244,10 +281,42 @@
     return jnp.where(lane >= lanes - steps, 0.0, pltpu.roll(value, lanes - steps, 1))
 
 
-def transform(value, table):
+def two_part(value, table, dims):
     rows = value.shape[0]
-    result = matmul(jnp.concatenate(split(value), axis=0), table, NN)
+    result = matmul(jnp.concatenate(split(value), axis=0), table, dims)
     return result[:rows] + result[rows:]
+
+
+def spectrum(value, residue, table):
+    width = value.shape[1] // BLOCKS
+    parts = [value[:, block * width : (block + 1) * width] for block in range(BLOCKS)]
+    real = parts[0]
+    imag = None
+    for block in range(1, BLOCKS):
+        angle = block_angle(residue, block)
+        real = real + parts[block] * math.cos(angle)
+        term = parts[block] * -math.sin(angle)
+        imag = term if imag is None else imag + term
+    result = two_part(jnp.concatenate([real, imag], axis=1), table, NN)
+    steps = result.shape[1] // 4
+    quarter = [result[:, i * steps : (i + 1) * steps] for i in range(4)]
+    return jnp.concatenate([quarter[0], quarter[2]], axis=1), jnp.concatenate(
+        [quarter[1], quarter[3]], axis=1
+    )
+
+
+def from_spectrum(real, imag, residue, table, totals):
+    steps = real.shape[1] // 2
+    value = jnp.concatenate(
+        [real[:, :steps], imag[:, :steps], real[:, steps:], imag[:, steps:]], axis=1
+    )
+    result = two_part(value, table, NT)
+    width = result.shape[1] // 2
+    even, odd = result[:, :width], result[:, width:]
+    for block in range(BLOCKS):
+        angle = block_angle(residue, block)
+        term = even if block == 0 else even * math.cos(angle) - odd * math.sin(angle)
+        totals[block] = term if totals[block] is None else totals[block] + term
 
 
 def operator_kernel(grad_scale, parts_ref, taps_ref, phase_ref, table_ref, grads_ref, out_ref, held_ref, sem):
@@ -296,29 +365,35 @@
     gated = key * value
     d_conv = cot * query
     stacked = jnp.concatenate([gated, d_conv, long_filter], axis=0)
+    rows = batches * chans
+    totals = [None] * BLOCKS
     copy.wait()
-    cos_all = transform(stacked, held_ref[0])
-    sin_all = transform(stacked, held_ref[1])
-    rows = batches * chans
-    g_cos, d_cos, h_cos = cos_all[:rows], cos_all[rows : 2 * rows], cos_all[2 * rows :]
-    g_sin, d_sin, h_sin = sin_all[:rows], sin_all[rows : 2 * rows], sin_all[2 * rows :]
-    cos_phase = phase_ref[0:1]
-    sin_phase = phase_ref[1:2]
-    h_real = jnp.concatenate([h_cos * cos_phase + h_sin * sin_phase] * batches, axis=0)
-    h_imag = jnp.concatenate([h_cos * sin_phase - h_sin * cos_phase] * batches, axis=0)
-    conv_real = g_cos * h_real + g_sin * h_imag
-    conv_imag = g_cos * h_imag - g_sin * h_real
-    back_real = h_real * d_cos - h_imag * d_sin
-    back_imag = -(h_real * d_sin + h_imag * d_cos)
-    corr_real = g_cos * d_cos + g_sin * d_sin
-    corr_imag = g_sin * d_cos - g_cos * d_sin
-    corr_real = corr_real[:chans] + corr_real[chans:]
-    corr_imag = corr_imag[:chans] + corr_imag[chans:]
-    lag_real = corr_real * cos_phase + corr_imag * sin_phase
-    lag_imag = corr_imag * cos_phase - corr_real * sin_phase
-    real_all = jnp.concatenate([conv_real, back_real, lag_real], axis=0)
-    imag_all = jnp.concatenate([conv_imag, back_imag, lag_imag], axis=0)
-    result = transform(real_all, held_ref[0]) - transform(imag_all, held_ref[1])
+    for residue in range(BLOCKS):
+        cos_all, sin_all = spectrum(stacked, residue, held_ref[residue])
+        g_real, d_real, h_real = cos_all[:rows], cos_all[rows : 2 * rows], cos_all[2 * rows :]
+        g_imag, d_imag, h_imag = sin_all[:rows], sin_all[rows : 2 * rows], sin_all[2 * rows :]
+        cos_phase = phase_ref[2 * residue : 2 * residue + 1]
+        sin_phase = phase_ref[2 * residue + 1 : 2 * residue + 2]
+        f_real = jnp.concatenate([h_real * cos_phase - h_imag * sin_phase] * batches, axis=0)
+        f_imag = jnp.concatenate([h_real * sin_phase + h_imag * cos_phase] * batches, axis=0)
+        conv_real = g_real * f_real - g_imag * f_imag
+        conv_imag = g_real * f_imag + g_imag * f_real
+        back_real = f_real * d_real + f_imag * d_imag
+        back_imag = f_real * d_imag - f_imag * d_real
+        corr_real = g_real * d_real + g_imag * d_imag
+        corr_imag = g_real * d_imag - g_imag * d_real
+        corr_real = corr_real[:chans] + corr_real[chans:]
+        corr_imag = corr_imag[:chans] + corr_imag[chans:]
+        lag_real = corr_real * cos_phase + corr_imag * sin_phase
+        lag_imag = corr_imag * cos_phase - corr_real * sin_phase
+        from_spectrum(
+            jnp.concatenate([conv_real, back_real, lag_real], axis=0),
+            jnp.concatenate([conv_imag, back_imag, lag_imag], axis=0),
+            residue,
+            held_ref[residue],
+            totals,
+        )
+    result = jnp.concatenate(totals, axis=1)
     scale = 1.0 / positions
     conv_out = result[:rows] * scale + skip * gated
     d_gated = result[rows : 2 * rows] * scale + skip * d_conv
@@ -349,55 +424,47 @@
         in_specs=[full, full, full, pl.BlockSpec(memory_space=pl.ANY)],
         out_shape=(kept((rows, positions)), kept((devices, 2 * chans, block_len))),
         scratch_shapes=[pltpu.VMEM(table.shape, BF), pltpu.SemaphoreType.DMA],
-        compiler_params=params(),
+        compiler_params=params(40 << 20),
         cost_estimate=cost(8 * rows * positions * positions, 2 * (parts.size + table.size)),
         name="operator",
-    )(parts, taps, phase, table)
+    )(parts, taps, phase, stay(table))
 
 
 def token_kernel(pos_ref, weight_ref, grads_ref, sent_ref, held_ref):
     streams, chips, _, rows, cols = weight_ref.shape
     positions = sent_ref.shape[1]
-    weight = jnp.concatenate(
-        [weight_ref[stream, :, 0].reshape(chips * rows, cols) for stream in range(streams)], axis=1
-    )
-    grads = jnp.concatenate(
-        [grads_ref[:, 0, stream].reshape(cols, positions) for stream in range(streams)], axis=0
-    )
-    total = matmul(weight, grads, NN).astype(BF)
-
-    @pl.when(pl.program_id(0) == 0)
-    def _():
-        sent_ref[...] = total
-
-    @pl.when(pl.program_id(0) == 1)
-    def _():
-        held_ref[...] = total
+    grads = [grads_ref[:, 0, stream].reshape(cols, positions) for stream in range(streams)]
+    for side, out_ref in ((1 - pos_ref[1], sent_ref), (pos_ref[1], held_ref)):
+        total = None
+        for stream in range(streams):
+            weight = weight_ref[stream, :, pl.ds(side, 1)].reshape(chips * rows, cols)
+            part = matmul(weight, grads[stream], NN)
+            total = part if total is None else total + part
+        out_ref[...] = total.astype(BF)
 
 
 def token_part(pos, weight, grads, chan_count):
     streams, slab_rows, cols = weight.shape
     slabs, _, _, chans, positions = grads.shape
     rows = slab_rows // chan_count
+    part = positions // 4
+    dims = (streams, chan_count // 2, 2, rows, cols)
     return pl.pallas_call(
         token_kernel,
         grid_spec=pltpu.PrefetchScalarGridSpec(
             num_scalar_prefetch=1,
-            grid=(2,),
+            grid=(4,),
             in_specs=[
-                pl.BlockSpec(
-                    (streams, chan_count // 2, 1, rows, cols),
-                    lambda j, pos: (0, 0, jnp.where(j == 0, 1 - pos[1], pos[1]), 0, 0),
-                ),
-                pl.BlockSpec((slabs, 1, streams, chans, positions), lambda j, pos: (0, pos[0], 0, 0, 0)),
+                pl.BlockSpec(dims, lambda j, pos: (0, 0, 0, 0, 0)),
+                pl.BlockSpec((slabs, 1, streams, chans, part), lambda j, pos: (0, pos[0], 0, 0, j)),
             ],
-            out_specs=[pl.BlockSpec((slab_rows // 2, positions), lambda j, pos: (0, 0))] * 2,
+            out_specs=[pl.BlockSpec((slab_rows // 2, part), lambda j, pos: (0, j))] * 2,
         ),
         out_shape=(kept((slab_rows // 2, positions)), kept((slab_rows // 2, positions))),
         compiler_params=params(),
         cost_estimate=cost(2 * weight.size * positions, 8 * slab_rows * positions),
         name="token_part",
-    )(pos, weight.reshape(streams, chan_count // 2, 2, rows, cols), grads)
+    )(pos, weight.reshape(dims), grads)
 
 
 def pair_kernel(held_ref, received_ref, out_ref):
@@ -405,18 +472,14 @@
 
 
 def pair_sum(held, received):
-    rows, positions = held.shape
-    block = pl.BlockSpec((rows // 4, positions), lambda i: (i, 0))
     return pl.pallas_call(
         pair_kernel,
-        grid=(4,),
-        in_specs=[block, block],
-        out_specs=block,
-        out_shape=kept((rows, positions)),
+        in_specs=[pl.BlockSpec(memory_space=pltpu.VMEM)] * 2,
+        out_shape=kept(held.shape),
         compiler_params=params(24 << 20),
         cost_estimate=cost(0, 6 * held.size),
         name="pair_sum",
-    )(held, received)
+    )(stay(held), received)
 
 
 def weight_kernel(grad_scale, pos_ref, own_ref, other_ref, own_grads_ref, other_grads_ref, out_ref):
@@ -527,41 +590,33 @@
     cores = [(i, i ^ 1) for i in range(chan_count)]
     weight = jnp.transpose(in_weight, (1, 0, 2))
 
-    mine = lax.dynamic_slice_in_dim(tokens[0], core * half, half, 0)
-    mine = jnp.transpose(mine.reshape(half, seq_count, slab_rows), (1, 0, 2))
     mine, edge, flipped = lax.optimization_barrier(
         (
-            exchange(mine, "seq"),
+            exchange(cut_tokens(pos, tokens, seq_count), "seq"),
             edge_rows(pos, cotangent, long_filter, slabs, positions),
             flip_weight(weight),
         )
     )
     theirs = lax.ppermute(mine, "chan", cores)
-    parts, spread = project(core[None], mine, theirs, flipped, edge)
+    parts = project(pos, mine, theirs, flipped, edge)
 
     shares = lax.dynamic_slice_in_dim(mine, chan_pos // 2 * share, share, 1)
     shares = lax.ppermute(shares, "dp", [(0, 1), (1, 0)])
-    odd = 2 * jnp.arange(positions, dtype=jnp.int32)[None] + 1
-    parts, shares, odd, short_taps = lax.optimization_barrier((parts, shares, odd, short_taps))
+    parts, shares, short_taps = lax.optimization_barrier((parts, shares, short_taps))
     shares = lax.all_gather(shares, "chan", axis=0)
     shares = shares.reshape(chips, 2, seq_count, share, slab_rows)
     taps = jnp.concatenate([short_taps.reshape(streams * taps_len, chan_cols), skip_gain[None]])
     taps = jnp.transpose(lax.dynamic_slice_in_dim(taps, slab_pos * chans, chans, 1))
-    parts, table, taps, phase, own = lax.optimization_barrier(
-        (
-            exchange(parts, ("seq", "dp")),
-            tables(odd),
-            taps,
-            jnp.concatenate(angle(odd, 8 * positions)),
-            turn_tokens(spread),
-        )
-    )
+    table, phase = transform_tables(positions)
+    parts, taps = lax.optimization_barrier((exchange(parts, ("seq", "dp")), taps))
 
     grads, outs = operator(parts, taps, phase, table, grad_scale, streams, tok_rows)
-    grads, shares = lax.optimization_barrier((grads, shares))
+    grads, shares, mine, theirs = lax.optimization_barrier((grads, shares, mine, theirs))
     grads = lax.all_gather(grads, ("seq", "dp"), axis=0)
     finished = finish(exchange(outs, ("seq", "dp")))
-    grads, finished, other = lax.optimization_barrier((grads, finished, turn_shares(shares)))
+    grads, finished, own, other = lax.optimization_barrier(
+        (grads, finished, turn_tokens(pos, mine, theirs), turn_shares(shares))
+    )
     hyena_out, grad_filter = finished
 
     grads = grads.reshape(slabs, dp_count, streams, chans, positions)

time: 216 us -> 242 us (1.12)
  Pallas kernels: 64.5 us -> 87.5 us
  waiting for transfers between devices: 93 us -> 108 us
  local copies, waits for them, and re-layouts: 6.61 us -> 0.85 us
  other arithmetic: 5.95 us -> 0.7 us
    pallas_call x3, Pallas kernels: 15.1 us -> 41 us  [the longest x1 33.6 us: cut_tokens(): pl.pallas_call(cut_kernel, in_specs=[pl.BlockSpec(memory_space=pltpu.SMEM...]
    all_to_all x3, waiting for transfers between devices: 45.9 us -> 65.9 us  [exchange(): lax.all_to_all(value, axis, split_axis=0, concat_axis=0, tiled=True, axis...]
    all_gather x1, waiting for transfers between devices: 42.1 us -> 37.2 us  [local(): grads = lax.all_gather(grads, ('seq', 'dp'), axis=0)]
    sin x2 -> x0, other arithmetic: 4.41 us -> none  [angle(): return (jnp.cos(phases), jnp.sin(phases))]
    unnamed x14 -> x15, local copies, waits for them, and re-layouts: 4.79 us -> 0.82 us
  transfers between devices with their start and end apart: 8 -> 8, of which waited for: 6 -> 6; matrix products, arithmetic and copies ran while one was open for 3% -> 0% of each run, Pallas kernels for 25% -> 18%
where the time goes in v4:
time: 242 us; the launch traced here: 241 us
  waiting for transfers between devices  108 us (45%)
  Pallas kernels  87.5 us (36%)
  starting transfers between devices  17 us (7%)
  between operations  14.2 us (6%)
  blocking collectives  13.2 us (5%)
    all_to_all x3, waiting for transfers between devices, exchange(): lax.all_to_all(value, axis, split_axis=0, concat_axis=0, tiled=True, axis...  65.9 us
    all_gather x1, waiting for transfers between devices, local(): grads = lax.all_gather(grads, ('seq', 'dp'), axis=0)  37.2 us
    pallas_call x1, Pallas kernels, cut_tokens(): pl.pallas_call(cut_kernel, in_specs=[pl.BlockSpec(memory_space=pltpu.SMEM...  33.6 us
    all_to_all x3, starting transfers between devices, exchange(): lax.all_to_all(value, axis, split_axis=0, concat_axis=0, tiled=True, axis...  16.2 us
    all_to_all x1, blocking collectives, exchange(): lax.all_to_all(value, axis, split_axis=0, concat_axis=0, tiled=True, axis...  13.2 us
    pallas_call x1, Pallas kernels, weight_grad(): pl.pallas_call(functools.partial(weight_kernel, grad_scale), grid_spec=pl...  11.7 us
    pallas_call x1, Pallas kernels, token_part(): pl.pallas_call(token_kernel, grid_spec=pltpu.PrefetchScalarGridSpec(num_s...  8.04 us
    pallas_call x1, Pallas kernels, project(): pl.pallas_call(project_kernel, grid_spec=pltpu.PrefetchScalarGridSpec(num...  7.26 us
  transfers between devices with their start and end apart: 8, of which 6 were waited for; matrix products, arithmetic and copies ran while one was open for 0% of the time, Pallas kernels for 18%

profile of v4, /device:TPU:0, one launch (start us, length us, event | category | flops | bytes accessed | tf_op | source)
XLA Modules:
  0.0 241.3 jit_solution(2922177506640266342)
XLA Ops:
  7.2 0.6 pad_add_fusion.pos_ref
  7.8 33.6 %cut_tokens.1 = bf16[8,64,1024]{2,1,0:T(8,128)(2,1)} custom-call(s32[2]{0:T(128)} %pad_add_fusion.pos_ref, bf16[1,128,8192]{2,1,0:T(8,128)(2,1)} %tokens_ref.1), custom_call_target="tpu_custom_call" | custom-call | bytes 2097152 | tf_op jit(solution)/shard_map/cut_tokens/pallas_call | solution.py:149
  41.4 8.0 %all-to-all-start = ((bf16[8,64,1024]{2,1,0:T(8,128)(2,1)}), bf16[8,64,1024]{2,1,0:T(8,128)(2,1)S(1)}, u32[]{:S(2)}, u32[]{:S(2)}) async-start(bf16[8,64,1024]{2,1,0:T(8,128)(2,1)} %cut_tokens.1), calls=%async_computation | async-start | bytes 2097152 | tf_op jit(solution)/shard_map/all_to_all | solution.py:565
  49.4 0.0 all-gather.5.cloned.1.call-start
  49.5 0.0 copy-start.2
  49.5 5.7 %flip_weight.1.weight_ref = bf16[3,512,1024]{2,1,0:T(8,128)(2,1)} custom-call(bf16[3,1024,512]{2,1,0:T(8,128)(2,1)} %bitcast.14), custom_call_target="tpu_custom_call" | custom-call | bytes 6291456 | tf_op jit(solution)/shard_map/flip_weight/pallas_call | solution.py:90
  55.2 1.9 edge_rows.1.edge_ref
  57.1 9.5 %all-to-all-done.mine_ref = bf16[8,64,1024]{2,1,0:T(8,128)(2,1)S(1)} async-done(((bf16[8,64,1024]{2,1,0:T(8,128)(2,1)}), bf16[8,64,1024]{2,1,0:T(8,128)(2,1)S(1)}, u32[]{:S(2)}, u32[]{:S(2)}) %all-to-all-start) | async-done | bytes 1048608 | tf_op jit(solution)/shard_map/all_to_all | solution.py:565
  66.6 0.0 copy-start
  66.6 0.0 collective-permute-start
  66.7 0.8 collective-permute-start.1
  67.4 1.9 collective-permute-done.theirs_ref
  69.3 0.0 copy-done.2
  69.3 0.0 copy-start.1
  69.3 7.3 %project.1 = bf16[16,104,1024]{2,1,0:T(8,128)(2,1)} custom-call(s32[2]{0:T(128)S(1)} %copy-done.2, bf16[8,64,1024]{2,1,0:T(8,128)(2,1)S(1)} %all-to-all-done.mine_ref, bf16[8,64,1024]{2,1,0:T(8,128)(2,1)S(1)} %collective-permute-done.theirs_ref, bf16[3,512,1024]{2,1,0:T(8,128)(2,1)} %flip_weight.1.weight_ref, bf16[16,8,1024]{2,1,0:T(8,128)(2,1)} %edge_rows.1.edge_ref), custom_call_target="tpu_custom_call" | custom-call | flops 3221225472 | bytes 8388608 | tf_op jit(solution)/shard_map/project/pallas_call | solution.py:192
  76.6 0.0 copy-done
  76.6 0.0 copy-done.1
  76.6 0.0 collective-permute-done.1
  76.6 0.0 copy-start.4
  76.6 0.7 copy-done.4
  77.3 0.0 all-gather.5.cloned.1.call-update
  77.3 0.0 copy-start.5
  77.3 0.0 copy-start.6
  77.3 0.0 copy-start.3
  77.3 3.9 %all-to-all-start.1 = ((bf16[16,104,1024]{2,1,0:T(8,128)(2,1)}), bf16[16,104,1024]{2,1,0:T(8,128)(2,1)S(1)}, u32[]{:S(2)}, u32[]{:S(2)}) async-start(bf16[16,104,1024]{2,1,0:T(8,128)(2,1)} %project.1), calls=%async_computation.1 | async-start | bytes 6815744 | tf_op jit(solution)/shard_map/all_to_all | solution.py:565
  81.2 0.0 all-gather.7.cloned.1.call-start
  81.3 0.0 copy-done.5
  81.3 0.0 copy-done.6
  81.3 0.1 fusion
  81.4 0.1 copy.16
  81.5 52.7 %all-to-all-done.1.parts_ref = bf16[16,104,1024]{2,1,0:T(8,128)(2,1)S(1)} async-done(((bf16[16,104,1024]{2,1,0:T(8,128)(2,1)}), bf16[16,104,1024]{2,1,0:T(8,128)(2,1)S(1)}, u32[]{:S(2)}, u32[]{:S(2)}) %all-to-all-start.1) | async-done | bytes 3407904 | tf_op jit(solution)/shard_map/all_to_all | solution.py:565
  134.2 0.0 copy-done.3
  134.2 6.0 %operator.1 = (bf16[192,1024]{1,0:T(8,128)(2,1)}, bf16[16,64,128]{2,1,0:T(8,128)(2,1)}) custom-call(bf16[16,104,1024]{2,1,0:T(8,128)(2,1)S(1)} %all-to-all-done.1.parts_ref, f32[32,10]{1,0:T(8,128)S(1)} %bitcast.12, f32[8,256]{1,0:T(8,128)S(1)} %copy-done.3, bf16[4,512,512]{2,1,0:T(8,128)(2,1)} %constant.49.clone.table_ref), custom_call_target="tpu_custom_call" | custom-call | flops 1610612736 | bytes 5505024 | tf_op jit(solution)/shard_map/operator/pallas_call | solution.py:422
  140.2 0.0 all-gather.5.cloned.1.call-done
  140.2 0.0 all-gather.7.cloned.1.call-update
  140.2 13.2 %all_to_all.20.parts_ref = bf16[16,64,128]{2,1,0:T(8,128)(2,1)S(1)} all-to-all(bf16[16,64,128]{2,1,0:T(8,128)(2,1)} %get-tuple-element.37), channel_id=1, replica_groups=mesh['seq'=8,'chan'=8,'dp'=2] {'seq','dp'}, dimensions={0} | all-to-all | bytes 524288 | tf_op jit(solution)/shard_map/all_to_all | solution.py:565
  153.4 0.9 finish.1
  154.2 4.2 %turn_shares.1.other_ref = bf16[1024,1024]{1,0:T(8,128)(2,1)} custom-call(bf16[4,2,8,16,1024]{4,3,2,1,0:T(8,128)(2,1)} %bitcast.16), custom_call_target="tpu_custom_call" | custom-call | bytes 4194304 | tf_op jit(solution)/shard_map/turn_shares/pallas_call | solution.py:256
  158.4 4.9 %turn_tokens.1.own_ref = bf16[1024,1024]{1,0:T(8,128)(2,1)} custom-call(s32[2]{0:T(128)} %pad_add_fusion.pos_ref, bf16[8,64,1024]{2,1,0:T(8,128)(2,1)} %copy-done, bf16[8,64,1024]{2,1,0:T(8,128)(2,1)} %copy-done.1), custom_call_target="tpu_custom_call" | custom-call | bytes 4194304 | tf_op jit(solution)/shard_map/turn_tokens/pallas_call | solution.py:226
  163.4 37.2 %all-gather.7.cloned.1.call-done = bf16[3072,1024]{1,0:T(8,128)(2,1)} async-done(((bf16[192,1024]{1,0:T(8,128)(2,1)}), bf16[3072,1024]{1,0:T(8,128)(2,1)}) %all-gather.7.cloned.1.call-update) | async-done | bytes 6291472 | tf_op jit(solution)/shard_map/all_gather | solution.py:615
  200.6 8.0 %token_part.1 = (bf16[512,1024]{1,0:T(8,128)(2,1)}, bf16[512,1024]{1,0:T(8,128)(2,1)}) custom-call(s32[2]{0:T(128)} %pad_add_fusion.pos_ref, bf16[3,4,2,128,512]{4,3,2,1,0:T(8,128)(2,1)} %bitcast.15, bf16[16,2,3,32,1024]{4,3,2,1,0:T(8,128)(2,1)} %bitcast.18), custom_call_target="tpu_custom_call" | custom-call | flops 3221225472 | bytes 8388608 | tf_op jit(solution)/shard_map/token_part/pallas_call | solution.py:452
  208.6 0.0 collective-permute-start.2
  208.6 2.9 %collective-permute-done.2.received_ref = bf16[512,1024]{1,0:T(8,128)(2,1)S(1)} collective-permute-done((bf16[512,1024]{1,0:T(8,128)(2,1)}, bf16[512,1024]{1,0:T(8,128)(2,1)S(1)}, u32[]{:S(2)}, u32[]{:S(2)}) %collective-permute-start.2) | collective-permute-done | bytes 1048608 | tf_op jit(solution)/shard_map/ppermute | solution.py:624
  211.5 2.4 %pair_sum.1 = bf16[512,1024]{1,0:T(8,128)(2,1)} custom-call(bf16[512,1024]{1,0:T(8,128)(2,1)} %get-tuple-element.45.held_ref, bf16[512,1024]{1,0:T(8,128)(2,1)S(1)} %collective-permute-done.2.received_ref), custom_call_target="tpu_custom_call" | custom-call | bytes 3145728 | tf_op jit(solution)/shard_map/pair_sum/pallas_call | solution.py:475
  213.9 4.2 %all-to-all-start.3 = ((bf16[4,128,1024]{2,1,0:T(8,128)(2,1)}), bf16[4,128,1024]{2,1,0:T(8,128)(2,1)S(1)}, u32[]{:S(2)}, u32[]{:S(2)}) async-start(bf16[4,128,1024]{2,1,0:T(8,128)(2,1)} %bitcast.13), calls=%async_computation.3 | async-start | bytes 2097152 | tf_op jit(solution)/shard_map/all_to_all | solution.py:565
  218.2 11.7 %weight_grad.1 = bf16[3,1024,512]{2,1,0:T(8,128)(2,1)} custom-call(s32[2]{0:T(128)} %pad_add_fusion.pos_ref, bf16[1024,1024]{1,0:T(8,128)(2,1)} %turn_tokens.1.own_ref, bf16[1024,1024]{1,0:T(8,128)(2,1)} %turn_shares.1.other_ref, bf16[16,2,3,32,1024]{4,3,2,1,0:T(8,128)(2,1)} %bitcast.19, bf16[16,2,3,32,1024]{4,3,2,1,0:T(8,128)(2,1)} %bitcast.20), custom_call_target="tpu_custom_call" | custom-call | flops 6442450944 | bytes 13631488 | tf_op jit(solution)/shard_map/weight_grad/pallas_call | solution.py:499
  229.9 3.7 %all-to-all-done.3.parts_ref = bf16[4,128,1024]{2,1,0:T(8,128)(2,1)S(1)} async-done(((bf16[4,128,1024]{2,1,0:T(8,128)(2,1)}), bf16[4,128,1024]{2,1,0:T(8,128)(2,1)S(1)}, u32[]{:S(2)}, u32[]{:S(2)}) %all-to-all-start.3) | async-done | bytes 1048608 | tf_op jit(solution)/shard_map/all_to_all | solution.py:565
  233.6 0.9 token_total.1
  (2 shorter events, 0.0 us)
Async XLA Ops:
  41.4 25.2 %all-to-all-start = ((bf16[8,64,1024]{2,1,0:T(8,128)(2,1)}), bf16[8,64,1024]{2,1,0:T(8,128)(2,1)S(1)}, u32[]{:S(2)}, u32[]{:S(2)}) async-start(bf16[8,64,1024]{2,1,0:T(8,128)(2,1)} %cut_tokens.1), calls=%async_computation | async-start | bytes 2097152 | tf_op jit(solution)/shard_map/all_to_all | solution.py:565
  49.4 90.8 %all-gather.5.cloned.1.call-start = ((), (), s32[]{:S(2)}) async-start(), calls=%async_computation.4 | async-start | bytes 2359296 | tf_op jit(solution)/shard_map/all_gather | solution.py:606
  49.5 19.8 %copy-start.2 = (s32[2]{0:T(128)S(1)}, s32[2]{0:T(128)}, u32[]{:S(2)}) copy-start(s32[2]{0:T(128)} %pad_add_fusion.pos_ref) | copy-start | bytes 28
  66.6 9.9 %copy-start = (bf16[8,64,1024]{2,1,0:T(8,128)(2,1)}, bf16[8,64,1024]{2,1,0:T(8,128)(2,1)S(1)}, u32[]{:S(2)}) copy-start(bf16[8,64,1024]{2,1,0:T(8,128)(2,1)S(1)} %all-to-all-done.mine_ref) | copy-start | bytes 3145732
  66.6 2.7 %collective-permute-start = (bf16[8,64,1024]{2,1,0:T(8,128)(2,1)S(1)}, bf16[8,64,1024]{2,1,0:T(8,128)(2,1)S(1)}, u32[]{:S(2)}, u32[]{:S(2)}) collective-permute-start(bf16[8,64,1024]{2,1,0:T(8,128)(2,1)S(1)} %all-to-all-done.mine_ref), channel_id=1, source_target_pairs={{0,2},{2,0},{4,6},{6,4},{8,10},{10,8},{12,14},{14,12},{1,3},{3,1},... | collective-permute-start | bytes 3145736 | tf_op jit(solution)/shard_map/ppermute | solution.py:600
  66.7 9.9 %collective-permute-start.1 = (bf16[8,16,1024]{2,1,0:T(8,128)(2,1)S(1)}, bf16[8,16,1024]{2,1,0:T(8,128)(2,1)S(1)}, u32[]{:S(2)}, u32[]{:S(2)}) collective-permute-start(bf16[8,16,1024]{2,1,0:T(8,128)(2,1)S(1)} %constant_dynamic-slice_fusion), channel_id=1, source_target_pairs={{0,1},{1,0},{2,3},{3,2},{4,5},{5,4},{6,7},{7,6},{8,9},{9,8},{10,11... | collective-permute-start | bytes 786440 | tf_op jit(solution)/shard_map/ppermute | solution.py:604
  69.3 7.3 %copy-start.1 = (bf16[8,64,1024]{2,1,0:T(8,128)(2,1)}, bf16[8,64,1024]{2,1,0:T(8,128)(2,1)S(1)}, u32[]{:S(2)}) copy-start(bf16[8,64,1024]{2,1,0:T(8,128)(2,1)S(1)} %collective-permute-done.theirs_ref) | copy-start | bytes 3145732
  76.6 0.7 copy-start.4
  77.3 4.0 %copy-start.5 = (f32[3,3,512]{2,1,0:T(4,128)S(1)}, f32[3,3,512]{2,1,0:T(4,128)}, u32[]{:S(2)}) copy-start(f32[3,3,512]{2,1,0:T(4,128)} %param.10) | copy-start | bytes 55300
  77.3 4.0 %copy-start.6 = (f32[512]{0:T(512)S(1)}, f32[512]{0:T(512)}, u32[]{:S(2)}) copy-start(f32[512]{0:T(512)} %param.12) | copy-start | bytes 6148
  77.3 56.9 %copy-start.3 = (f32[8,256]{1,0:T(8,128)S(1)}, f32[8,256]{1,0:T(8,128)}, u32[]{:S(2)}) copy-start(f32[8,256]{1,0:T(8,128)} %constant.50.clone.phase_ref) | copy-start | bytes 24580
  77.3 56.8 %all-to-all-start.1 = ((bf16[16,104,1024]{2,1,0:T(8,128)(2,1)}), bf16[16,104,1024]{2,1,0:T(8,128)(2,1)S(1)}, u32[]{:S(2)}, u32[]{:S(2)}) async-start(bf16[16,104,1024]{2,1,0:T(8,128)(2,1)} %project.1), calls=%async_computation.1 | async-start | bytes 6815744 | tf_op jit(solution)/shard_map/all_to_all | solution.py:565
  81.2 119.3 %all-gather.7.cloned.1.call-start = ((), (), s32[]{:S(2)}) async-start(), calls=%async_computation.5 | async-start | bytes 6684672 | tf_op jit(solution)/shard_map/all_gather | solution.py:615
  208.6 2.9 %collective-permute-start.2 = (bf16[512,1024]{1,0:T(8,128)(2,1)}, bf16[512,1024]{1,0:T(8,128)(2,1)S(1)}, u32[]{:S(2)}, u32[]{:S(2)}) collective-permute-start(bf16[512,1024]{1,0:T(8,128)(2,1)} %get-tuple-element.46), channel_id=1, source_target_pairs={{0,2},{2,0},{4,6},{6,4},{8,10},{10,8},{12,14},{14,12},{1,3},{3,1},... | collective-permute-start | bytes 3145736 | tf_op jit(solution)/shard_map/ppermute | solution.py:624
  213.9 19.6 %all-to-all-start.3 = ((bf16[4,128,1024]{2,1,0:T(8,128)(2,1)}), bf16[4,128,1024]{2,1,0:T(8,128)(2,1)S(1)}, u32[]{:S(2)}, u32[]{:S(2)}) async-start(bf16[4,128,1024]{2,1,0:T(8,128)(2,1)} %bitcast.13), calls=%async_computation.3 | async-start | bytes 2097152 | tf_op jit(solution)/shard_map/all_to_all | solution.py:565
Sparse Core Ops, SparseCore 0:
  77.4 22.2 all-gather.4
  140.4 60.1 all-gather.6

commit v5 on v4

--- a/solution.py
+++ b/solution.py
@@ -41,11 +41,10 @@
     return high, (value - high.astype(F32)).astype(BF)
 
 
-def edge_kernel(pos_ref, cot_ref, filter_ref, out_ref):
+def edge_kernel(cot_ref, filter_ref, out_ref):
     slabs = out_ref.shape[0]
     chans = filter_ref.shape[1] // slabs
-    high, low = split(jnp.transpose(filter_ref[...]))
-    taps = jnp.where(pos_ref[0] == 0, high.astype(F32), low.astype(F32)).astype(BF)
+    taps = jnp.transpose(filter_ref[...]).astype(BF)
     cot = jnp.transpose(cot_ref[0].astype(F32)).astype(BF)
     for slab in range(slabs):
         part = slice(slab * chans, (slab + 1) * chans)
@@ -67,17 +66,17 @@
     )
 
 
-def edge_rows(pos, cotangent, long_filter, slabs, lanes):
+def edge_rows(cotangent, long_filter, slabs, lanes):
     _, tok_rows, chan_cols = cotangent.shape
     full = pl.BlockSpec(memory_space=pltpu.VMEM)
     return pl.pallas_call(
         edge_kernel,
-        in_specs=[pl.BlockSpec(memory_space=pltpu.SMEM), full, full],
+        in_specs=[full, full],
         out_shape=kept((slabs, 2 * tok_rows * chan_cols // slabs // lanes, lanes)),
         compiler_params=params(),
         cost_estimate=cost(0, 8 * tok_rows * chan_cols),
         name="edge_rows",
-    )(pos, cotangent, long_filter)
+    )(cotangent, long_filter)
 
 
 def flip_kernel(weight_ref, out_ref):
@@ -127,31 +126,24 @@
     return jnp.asarray(np.stack(tables), BF), jnp.asarray(np.stack(phases), F32)
 
 
-def cut_kernel(pos_ref, tokens_ref, out_ref, sems):
-    slabs, half, width = out_ref.shape
-    start = pl.multiple_of(pos_ref[1] * half, half)
-    copies = [
-        pltpu.make_async_copy(
-            tokens_ref.at[0, pl.ds(start, half), slice(slab * width, (slab + 1) * width)],
-            out_ref.at[slab],
-            sems.at[slab],
-        )
-        for slab in range(slabs)
-    ]
-    for copy in copies:
-        copy.start()
-    for copy in copies:
-        copy.wait()
+def cut_kernel(pos_ref, tokens_ref, out_ref):
+    slabs, _, width = out_ref.shape
+    for slab in range(slabs):
+        out_ref[slab] = tokens_ref[0, :, slab * width : (slab + 1) * width]
 
 
 def cut_tokens(pos, tokens, slabs):
     _, rows, width = tokens.shape
+    dims = (slabs, rows // 2, width // slabs)
     return pl.pallas_call(
         cut_kernel,
-        in_specs=[pl.BlockSpec(memory_space=pltpu.SMEM), pl.BlockSpec(memory_space=pl.ANY)],
-        out_specs=pl.BlockSpec(memory_space=pl.ANY),
-        out_shape=kept((slabs, rows // 2, width // slabs)),
-        scratch_shapes=[pltpu.SemaphoreType.DMA((slabs,))],
+        grid_spec=pltpu.PrefetchScalarGridSpec(
+            num_scalar_prefetch=1,
+            grid=(1,),
+            in_specs=[pl.BlockSpec((1, rows // 2, width), lambda i, pos: (0, pos[1], 0))],
+            out_specs=pl.BlockSpec(dims, lambda i, pos: (0, 0, 0)),
+        ),
+        out_shape=kept(dims),
         compiler_params=params(),
         cost_estimate=cost(0, 2 * tokens.size),
         name="cut_tokens",
@@ -322,50 +314,43 @@
 def operator_kernel(grad_scale, parts_ref, taps_ref, phase_ref, table_ref, grads_ref, out_ref, held_ref, sem):
     copy = pltpu.make_async_copy(table_ref, held_ref, sem)
     copy.start()
-    devices, _, positions = parts_ref.shape
+    sources, _, positions = parts_ref.shape
     block_len = out_ref.shape[2]
-    batches = 2
     chans = taps_ref.shape[0]
-    streams = grads_ref.shape[0] // (batches * chans)
+    streams = grads_ref.shape[0] // chans
     taps_len = (taps_ref.shape[1] - 1) // streams
-    sources = devices // batches
-    all_taps = jnp.concatenate([taps_ref[...]] * batches, axis=0)
 
     def tap(stream, pos):
         column = stream * taps_len + pos
-        return all_taps[:, column : column + 1]
-
-    def summed(batch, row):
-        total = parts_ref[batch, row : row + chans].astype(F32)
+        return taps_ref[:, column : column + 1]
+
+    def summed(row):
+        total = parts_ref[0, row : row + chans].astype(F32)
         for source in range(1, sources):
-            total = total + parts_ref[source * batches + batch, row : row + chans].astype(F32)
+            total = total + parts_ref[source, row : row + chans].astype(F32)
         return total
-
-    def edge(batch):
-        return jnp.concatenate(
-            [
-                unfold(parts_ref[source * batches + batch, streams * chans :], block_len).astype(F32)
-                for source in range(sources)
-            ],
-            axis=1,
-        )
 
     filtered = []
     for stream in range(streams):
-        total = jnp.concatenate([summed(batch, stream * chans) for batch in range(batches)], axis=0)
+        total = summed(stream * chans)
         acc = tap(stream, 0) * total
         for pos in range(1, taps_len):
             acc = acc + tap(stream, pos) * delayed(total, pos)
         filtered.append(acc)
     query, key, value = filtered
-    skip = all_taps[:, streams * taps_len : streams * taps_len + 1]
-    edges = [edge(batch) for batch in range(batches)]
-    cot = jnp.concatenate([rows[:chans] for rows in edges], axis=0)
-    long_filter = edges[0][chans:] + edges[1][chans:]
+    skip = taps_ref[:, streams * taps_len : streams * taps_len + 1]
+    edge = jnp.concatenate(
+        [
+            unfold(parts_ref[source, streams * chans :], block_len).astype(F32)
+            for source in range(sources)
+        ],
+        axis=1,
+    )
+    cot, long_filter = edge[:chans], edge[chans:]
     gated = key * value
     d_conv = cot * query
     stacked = jnp.concatenate([gated, d_conv, long_filter], axis=0)
-    rows = batches * chans
+    rows = chans
     totals = [None] * BLOCKS
     copy.wait()
     for residue in range(BLOCKS):
@@ -374,16 +359,14 @@
         g_imag, d_imag, h_imag = sin_all[:rows], sin_all[rows : 2 * rows], sin_all[2 * rows :]
         cos_phase = phase_ref[2 * residue : 2 * residue + 1]
         sin_phase = phase_ref[2 * residue + 1 : 2 * residue + 2]
-        f_real = jnp.concatenate([h_real * cos_phase - h_imag * sin_phase] * batches, axis=0)
-        f_imag = jnp.concatenate([h_real * sin_phase + h_imag * cos_phase] * batches, axis=0)
+        f_real = h_real * cos_phase - h_imag * sin_phase
+        f_imag = h_real * sin_phase + h_imag * cos_phase
         conv_real = g_real * f_real - g_imag * f_imag
         conv_imag = g_real * f_imag + g_imag * f_real
         back_real = f_real * d_real + f_imag * d_imag
         back_imag = f_real * d_imag - f_imag * d_real
         corr_real = g_real * d_real + g_imag * d_imag
         corr_imag = g_real * d_imag - g_imag * d_real
-        corr_real = corr_real[:chans] + corr_real[chans:]
-        corr_imag = corr_imag[:chans] + corr_imag[chans:]
         lag_real = corr_real * cos_phase + corr_imag * sin_phase
         lag_imag = corr_imag * cos_phase - corr_real * sin_phase
         from_spectrum(
@@ -399,30 +382,26 @@
     d_gated = result[rows : 2 * rows] * scale + skip * d_conv
     filter_part = (result[2 * rows :] * (scale * grad_scale)).astype(BF)
     hyena_out = (query * conv_out).astype(BF)
-    for device in range(devices):
-        batch = device % batches
-        lanes = slice(device // batches * block_len, (device // batches + 1) * block_len)
-        out_ref[device, :chans] = hyena_out[batch * chans : (batch + 1) * chans, lanes]
-        out_ref[device, chans:] = filter_part[:, lanes]
+    for block in range(sources):
+        lanes = slice(block * block_len, (block + 1) * block_len)
+        out_ref[block, :chans] = hyena_out[:, lanes]
+        out_ref[block, chans:] = filter_part[:, lanes]
     for stream, grad in enumerate((cot * conv_out, d_gated * value, d_gated * key)):
         acc = tap(stream, 0) * grad
         for pos in range(1, taps_len):
             acc = acc + tap(stream, pos) * advanced(grad, pos)
-        acc = acc.astype(BF)
-        for batch in range(batches):
-            row = (batch * streams + stream) * chans
-            grads_ref[row : row + chans] = acc[batch * chans : (batch + 1) * chans]
+        grads_ref[stream * chans : (stream + 1) * chans] = acc.astype(BF)
 
 
 def operator(parts, taps, phase, table, grad_scale, streams, block_len):
-    devices, _, positions = parts.shape
+    sources, _, positions = parts.shape
     chans = taps.shape[0]
-    rows = devices * block_len // positions * streams * chans
+    rows = streams * chans
     full = pl.BlockSpec(memory_space=pltpu.VMEM)
     return pl.pallas_call(
         functools.partial(operator_kernel, grad_scale),
         in_specs=[full, full, full, pl.BlockSpec(memory_space=pl.ANY)],
-        out_shape=(kept((rows, positions)), kept((devices, 2 * chans, block_len))),
+        out_shape=(kept((rows, positions)), kept((sources, 2 * chans, block_len))),
         scratch_shapes=[pltpu.VMEM(table.shape, BF), pltpu.SemaphoreType.DMA],
         compiler_params=params(40 << 20),
         cost_estimate=cost(8 * rows * positions * positions, 2 * (parts.size + table.size)),
@@ -537,17 +516,17 @@
     )(parts)
 
 
-def finish_kernel(parts_ref, out_ref, filter_ref):
-    slabs, rows, block_len = parts_ref.shape
+def finish_kernel(own_ref, other_ref, out_ref, filter_ref):
+    slabs, rows, block_len = own_ref.shape
     chans = rows // 2
-    hyena = parts_ref[:, :chans].astype(F32).reshape(slabs * chans, block_len)
-    filters = parts_ref[:, chans:].astype(F32).reshape(slabs * chans, block_len)
+    hyena = own_ref[:, :chans].astype(F32).reshape(slabs * chans, block_len)
+    filters = own_ref[:, chans:].astype(F32) + other_ref[...].astype(F32)
     out_ref[0] = jnp.transpose(hyena).astype(BF)
-    filter_ref[...] = jnp.transpose(filters)
-
-
-def finish(parts):
-    slabs, rows, block_len = parts.shape
+    filter_ref[...] = jnp.transpose(filters.reshape(slabs * chans, block_len))
+
+
+def finish(own, other):
+    slabs, rows, block_len = own.shape
     chan_cols = slabs * rows // 2
     return pl.pallas_call(
         finish_kernel,
@@ -556,9 +535,9 @@
             jax.ShapeDtypeStruct((block_len, chan_cols), F32),
         ),
         compiler_params=params(24 << 20),
-        cost_estimate=cost(0, 4 * parts.size),
+        cost_estimate=cost(0, 4 * own.size),
         name="finish",
-    )(parts)
+    )(own, other)
 
 
 def exchange(value, axis, groups=None):
@@ -571,7 +550,7 @@
     seq_count = lax.axis_size("seq")
     dp_count = lax.axis_size("dp")
     dp_pos = lax.axis_index("dp").astype(jnp.int32)
-    slab_pos = lax.axis_index("seq").astype(jnp.int32) * dp_count + dp_pos
+    seq_pos = lax.axis_index("seq").astype(jnp.int32)
     chan_count = lax.axis_size("chan")
     chan_pos = lax.axis_index("chan").astype(jnp.int32)
     core = chan_pos % 2
@@ -581,19 +560,19 @@
     chan_cols = in_weight.shape[2]
     streams, taps_len = short_taps.shape[:2]
     positions = seq_count * tok_rows
-    slabs = seq_count * dp_count
-    chans = chan_cols // slabs
+    chans = chan_cols // seq_count
     half = tok_rows // 2
     share = tok_rows // chan_count
     chips = chan_count // 2
     grad_scale = 1.0 / math.sqrt(dp_count * positions)
+    batches = [(0, 1), (1, 0)]
     cores = [(i, i ^ 1) for i in range(chan_count)]
     weight = jnp.transpose(in_weight, (1, 0, 2))
 
     mine, edge, flipped = lax.optimization_barrier(
         (
             exchange(cut_tokens(pos, tokens, seq_count), "seq"),
-            edge_rows(pos, cotangent, long_filter, slabs, positions),
+            edge_rows(cotangent, long_filter, seq_count, positions),
             flip_weight(weight),
         )
     )
@@ -601,25 +580,26 @@
     parts = project(pos, mine, theirs, flipped, edge)
 
     shares = lax.dynamic_slice_in_dim(mine, chan_pos // 2 * share, share, 1)
-    shares = lax.ppermute(shares, "dp", [(0, 1), (1, 0)])
+    shares = lax.ppermute(shares, "dp", batches)
     parts, shares, short_taps = lax.optimization_barrier((parts, shares, short_taps))
     shares = lax.all_gather(shares, "chan", axis=0)
     shares = shares.reshape(chips, 2, seq_count, share, slab_rows)
     taps = jnp.concatenate([short_taps.reshape(streams * taps_len, chan_cols), skip_gain[None]])
-    taps = jnp.transpose(lax.dynamic_slice_in_dim(taps, slab_pos * chans, chans, 1))
+    taps = jnp.transpose(lax.dynamic_slice_in_dim(taps, seq_pos * chans, chans, 1))
     table, phase = transform_tables(positions)
-    parts, taps = lax.optimization_barrier((exchange(parts, ("seq", "dp")), taps))
+    parts, taps = lax.optimization_barrier((exchange(parts, "seq"), taps))
 
     grads, outs = operator(parts, taps, phase, table, grad_scale, streams, tok_rows)
     grads, shares, mine, theirs = lax.optimization_barrier((grads, shares, mine, theirs))
     grads = lax.all_gather(grads, ("seq", "dp"), axis=0)
-    finished = finish(exchange(outs, ("seq", "dp")))
+    outs = exchange(outs, "seq")
+    finished = finish(outs, lax.ppermute(outs[:, chans:], "dp", batches))
     grads, finished, own, other = lax.optimization_barrier(
         (grads, finished, turn_tokens(pos, mine, theirs), turn_shares(shares))
     )
     hyena_out, grad_filter = finished
 
-    grads = grads.reshape(slabs, dp_count, streams, chans, positions)
+    grads = grads.reshape(seq_count, dp_count, streams, chans, positions)
     sent, held = token_part(pos, weight, grads, chan_count)
     token_block = pair_sum(held, lax.ppermute(sent, "chan", cores))
     token_block = exchange(

time: 242 us -> 200 us (0.83)
  Pallas kernels: 87.5 us -> 56.5 us
  waiting for transfers between devices: 108 us -> 97.4 us
    pallas_call x2, Pallas kernels: 35.5 us -> 4.82 us  [the longest x1 2.96 us: cut_tokens(): pl.pallas_call(cut_kernel, grid_spec=pltpu.PrefetchScalarGridSpec(num_sca...]
    all_to_all x3, waiting for transfers between devices: 65.9 us -> 56 us  [exchange(): lax.all_to_all(value, axis, split_axis=0, concat_axis=0, tiled=True, axis...]
    all_gather x1, waiting for transfers between devices: 37.2 us -> 30.4 us  [local(): grads = lax.all_gather(grads, ('seq', 'dp'), axis=0)]
    ppermute x1 -> x2, waiting for transfers between devices: 0.01 us -> 6.22 us  [the longest x1 6.22 us: local(): finished = finish(outs, lax.ppermute(outs[:, chans:], 'dp', batches))]
  transfers between devices with their start and end apart: 8 -> 9, of which waited for: 6 -> 7; matrix products, arithmetic and copies ran while one was open for 0% -> 0% of each run, Pallas kernels for 18% -> 21%
where the time goes in v5:
time: 200 us; the launch traced here: 199 us
  waiting for transfers between devices  97.4 us (49%)
  Pallas kernels  56.5 us (28%)
  starting transfers between devices  17.6 us (9%)
  between operations  14.2 us (7%)
  blocking collectives  12.2 us (6%)
    all_to_all x3, waiting for transfers between devices, exchange(): lax.all_to_all(value, axis, split_axis=0, concat_axis=0, tiled=True, axis...  56 us
    all_gather x1, waiting for transfers between devices, local(): grads = lax.all_gather(grads, ('seq', 'dp'), axis=0)  30.4 us
    all_to_all x3, starting transfers between devices, exchange(): lax.all_to_all(value, axis, split_axis=0, concat_axis=0, tiled=True, axis...  16.1 us
    all_to_all x1, blocking collectives, exchange(): lax.all_to_all(value, axis, split_axis=0, concat_axis=0, tiled=True, axis...  12.2 us
    pallas_call x1, Pallas kernels, weight_grad(): pl.pallas_call(functools.partial(weight_kernel, grad_scale), grid_spec=pl...  11.7 us
    pallas_call x1, Pallas kernels, token_part(): pl.pallas_call(token_kernel, grid_spec=pltpu.PrefetchScalarGridSpec(num_s...  8.03 us
    pallas_call x1, Pallas kernels, project(): pl.pallas_call(project_kernel, grid_spec=pltpu.PrefetchScalarGridSpec(num...  7.24 us
    ppermute x1, waiting for transfers between devices, local(): finished = finish(outs, lax.ppermute(outs[:, chans:], 'dp', batches))  6.22 us
  transfers between devices with their start and end apart: 9, of which 7 were waited for; matrix products, arithmetic and copies ran while one was open for 0% of the time, Pallas kernels for 21%

profile of v5, /device:TPU:0, one launch (start us, length us, event | category | flops | bytes accessed | tf_op | source)
XLA Modules:
  0.0 199.4 jit_solution(14548646043151121169)
XLA Ops:
  7.2 0.6 pad_add_fusion.pos_ref
  7.8 3.0 %cut_tokens.1 = bf16[8,64,1024]{2,1,0:T(8,128)(2,1)} custom-call(s32[2]{0:T(128)} %pad_add_fusion.pos_ref, bf16[1,128,8192]{2,1,0:T(8,128)(2,1)} %tokens_ref.1), custom_call_target="tpu_custom_call" | custom-call | bytes 2097152 | tf_op jit(solution)/shard_map/cut_tokens/pallas_call | solution.py:138
  10.7 8.0 %all-to-all-start = ((bf16[8,64,1024]{2,1,0:T(8,128)(2,1)}), bf16[8,64,1024]{2,1,0:T(8,128)(2,1)S(1)}, u32[]{:S(2)}, u32[]{:S(2)}) async-start(bf16[8,64,1024]{2,1,0:T(8,128)(2,1)} %cut_tokens.1), calls=%async_computation | async-start | bytes 2097152 | tf_op jit(solution)/shard_map/all_to_all | solution.py:544
  18.7 0.0 all-gather.5.cloned.1.call-start
  18.8 0.0 copy-start.2
  18.8 5.7 %flip_weight.1.weight_ref = bf16[3,512,1024]{2,1,0:T(8,128)(2,1)} custom-call(bf16[3,1024,512]{2,1,0:T(8,128)(2,1)} %bitcast.14), custom_call_target="tpu_custom_call" | custom-call | bytes 6291456 | tf_op jit(solution)/shard_map/flip_weight/pallas_call | solution.py:89
  24.5 1.9 edge_rows.1.edge_ref
  26.4 9.5 %all-to-all-done.mine_ref = bf16[8,64,1024]{2,1,0:T(8,128)(2,1)S(1)} async-done(((bf16[8,64,1024]{2,1,0:T(8,128)(2,1)}), bf16[8,64,1024]{2,1,0:T(8,128)(2,1)S(1)}, u32[]{:S(2)}, u32[]{:S(2)}) %all-to-all-start) | async-done | bytes 1048608 | tf_op jit(solution)/shard_map/all_to_all | solution.py:544
  36.0 0.0 collective-permute-start
  36.0 0.8 collective-permute-start.1
  36.7 1.9 collective-permute-done.theirs_ref
  38.6 0.0 copy-done.2
  38.6 7.2 %project.1 = bf16[8,208,1024]{2,1,0:T(8,128)(2,1)} custom-call(s32[2]{0:T(128)S(1)} %copy-done.2, bf16[8,64,1024]{2,1,0:T(8,128)(2,1)S(1)} %all-to-all-done.mine_ref, bf16[8,64,1024]{2,1,0:T(8,128)(2,1)S(1)} %collective-permute-done.theirs_ref, bf16[3,512,1024]{2,1,0:T(8,128)(2,1)} %flip_weight.1.weight_ref, bf16[8,16,1024]{2,1,0:T(8,128)(2,1)} %edge_rows.1.edge_ref), custom_call_target="tpu_custom_call" | custom-call | flops 3221225472 | bytes 8388608 | tf_op jit(solution)/shard_map/project/pallas_call | solution.py:184
  45.9 0.0 copy-done
  45.9 0.0 copy-done.1
  45.9 0.0 collective-permute-done.1
  45.9 0.0 copy-start.4
  45.9 0.7 copy-done.4
  46.6 0.0 all-gather.5.cloned.1.call-update
  46.6 0.0 copy-start.5
  46.6 0.0 copy-start.6
  46.6 0.0 copy-start.3
  46.6 3.8 %all-to-all-start.1 = ((bf16[8,208,1024]{2,1,0:T(8,128)(2,1)}), bf16[8,208,1024]{2,1,0:T(8,128)(2,1)S(1)}, u32[]{:S(2)}, u32[]{:S(2)}) async-start(bf16[8,208,1024]{2,1,0:T(8,128)(2,1)} %project.1), calls=%async_computation.1 | async-start | bytes 6815744 | tf_op jit(solution)/shard_map/all_to_all | solution.py:544
  50.5 0.0 all-gather.7.cloned.1.call-start
  50.5 0.0 copy-done.5
  50.5 0.0 copy-done.6
  50.5 0.1 fusion
  50.6 0.1 copy.16
  50.7 42.8 %all-to-all-done.1.parts_ref = bf16[8,208,1024]{2,1,0:T(8,128)(2,1)S(1)} async-done(((bf16[8,208,1024]{2,1,0:T(8,128)(2,1)}), bf16[8,208,1024]{2,1,0:T(8,128)(2,1)S(1)}, u32[]{:S(2)}, u32[]{:S(2)}) %all-to-all-start.1) | async-done | bytes 3407904 | tf_op jit(solution)/shard_map/all_to_all | solution.py:544
  93.5 0.0 copy-done.3
  93.5 5.7 %operator.1 = (bf16[192,1024]{1,0:T(8,128)(2,1)}, bf16[8,128,128]{2,1,0:T(8,128)(2,1)}) custom-call(bf16[8,208,1024]{2,1,0:T(8,128)(2,1)S(1)} %all-to-all-done.1.parts_ref, f32[64,10]{1,0:T(8,128)S(1)} %bitcast.12, f32[8,256]{1,0:T(8,128)S(1)} %copy-done.3, bf16[4,512,512]{2,1,0:T(8,128)(2,1)} %constant.47.clone.table_ref), custom_call_target="tpu_custom_call" | custom-call | flops 1610612736 | bytes 5505024 | tf_op jit(solution)/shard_map/operator/pallas_call | solution.py:401
  99.2 0.0 all-gather.5.cloned.1.call-done
  99.2 0.0 all-gather.7.cloned.1.call-update
  99.2 12.2 %all_to_all.20.own_ref = bf16[8,128,128]{2,1,0:T(8,128)(2,1)S(1)} all-to-all(bf16[8,128,128]{2,1,0:T(8,128)(2,1)} %get-tuple-element.37), channel_id=1, replica_groups=mesh['seq'=8,'chan'=8,'dp'=2] {'seq'}, dimensions={0} | all-to-all | bytes 524288 | tf_op jit(solution)/shard_map/all_to_all | solution.py:544
  111.4 0.7 collective-permute-start.2
  112.1 6.2 %collective-permute-done.2.other_ref = bf16[8,64,128]{2,1,0:T(8,128)(2,1)S(1)} collective-permute-done((bf16[8,64,128]{2,1,0:T(8,128)(2,1)S(1)}, bf16[8,64,128]{2,1,0:T(8,128)(2,1)S(1)}, u32[]{:S(2)}, u32[]{:S(2)}) %collective-permute-start.2) | collective-permute-done | bytes 131104 | tf_op jit(solution)/shard_map/ppermute | solution.py:596
  118.3 0.9 finish.1
  119.2 4.2 %turn_shares.1.other_ref = bf16[1024,1024]{1,0:T(8,128)(2,1)} custom-call(bf16[4,2,8,16,1024]{4,3,2,1,0:T(8,128)(2,1)} %bitcast.16), custom_call_target="tpu_custom_call" | custom-call | bytes 4194304 | tf_op jit(solution)/shard_map/turn_shares/pallas_call | solution.py:248
  123.4 4.9 %turn_tokens.1.own_ref = bf16[1024,1024]{1,0:T(8,128)(2,1)} custom-call(s32[2]{0:T(128)} %pad_add_fusion.pos_ref, bf16[8,64,1024]{2,1,0:T(8,128)(2,1)} %copy-done, bf16[8,64,1024]{2,1,0:T(8,128)(2,1)} %copy-done.1), custom_call_target="tpu_custom_call" | custom-call | bytes 4194304 | tf_op jit(solution)/shard_map/turn_tokens/pallas_call | solution.py:218
  128.3 30.4 %all-gather.7.cloned.1.call-done = bf16[3072,1024]{1,0:T(8,128)(2,1)} async-done(((bf16[192,1024]{1,0:T(8,128)(2,1)}), bf16[3072,1024]{1,0:T(8,128)(2,1)}) %all-gather.7.cloned.1.call-update) | async-done | bytes 6291472 | tf_op jit(solution)/shard_map/all_gather | solution.py:594
  158.7 8.0 %token_part.1 = (bf16[512,1024]{1,0:T(8,128)(2,1)}, bf16[512,1024]{1,0:T(8,128)(2,1)}) custom-call(s32[2]{0:T(128)} %pad_add_fusion.pos_ref, bf16[3,4,2,128,512]{4,3,2,1,0:T(8,128)(2,1)} %bitcast.15, bf16[8,2,3,64,1024]{4,3,2,1,0:T(8,128)(2,1)} %bitcast.18), custom_call_target="tpu_custom_call" | custom-call | flops 3221225472 | bytes 8388608 | tf_op jit(solution)/shard_map/token_part/pallas_call | solution.py:431
  166.7 0.0 collective-permute-start.3
  166.7 2.9 %collective-permute-done.3.received_ref = bf16[512,1024]{1,0:T(8,128)(2,1)S(1)} collective-permute-done((bf16[512,1024]{1,0:T(8,128)(2,1)}, bf16[512,1024]{1,0:T(8,128)(2,1)S(1)}, u32[]{:S(2)}, u32[]{:S(2)}) %collective-permute-start.3) | collective-permute-done | bytes 1048608 | tf_op jit(solution)/shard_map/ppermute | solution.py:604
  169.6 2.5 %pair_sum.1 = bf16[512,1024]{1,0:T(8,128)(2,1)} custom-call(bf16[512,1024]{1,0:T(8,128)(2,1)} %get-tuple-element.45.held_ref, bf16[512,1024]{1,0:T(8,128)(2,1)S(1)} %collective-permute-done.3.received_ref), custom_call_target="tpu_custom_call" | custom-call | bytes 3145728 | tf_op jit(solution)/shard_map/pair_sum/pallas_call | solution.py:454
  172.0 4.2 %all-to-all-start.3 = ((bf16[4,128,1024]{2,1,0:T(8,128)(2,1)}), bf16[4,128,1024]{2,1,0:T(8,128)(2,1)S(1)}, u32[]{:S(2)}, u32[]{:S(2)}) async-start(bf16[4,128,1024]{2,1,0:T(8,128)(2,1)} %bitcast.13), calls=%async_computation.3 | async-start | bytes 2097152 | tf_op jit(solution)/shard_map/all_to_all | solution.py:544
  176.3 11.7 %weight_grad.1 = bf16[3,1024,512]{2,1,0:T(8,128)(2,1)} custom-call(s32[2]{0:T(128)} %pad_add_fusion.pos_ref, bf16[1024,1024]{1,0:T(8,128)(2,1)} %turn_tokens.1.own_ref, bf16[1024,1024]{1,0:T(8,128)(2,1)} %turn_shares.1.other_ref, bf16[8,2,3,64,1024]{4,3,2,1,0:T(8,128)(2,1)} %bitcast.19, bf16[8,2,3,64,1024]{4,3,2,1,0:T(8,128)(2,1)} %bitcast.20), custom_call_target="tpu_custom_call" | custom-call | flops 6442450944 | bytes 13631488 | tf_op jit(solution)/shard_map/weight_grad/pallas_call | solution.py:478
  188.0 3.7 %all-to-all-done.3.parts_ref = bf16[4,128,1024]{2,1,0:T(8,128)(2,1)S(1)} async-done(((bf16[4,128,1024]{2,1,0:T(8,128)(2,1)}), bf16[4,128,1024]{2,1,0:T(8,128)(2,1)S(1)}, u32[]{:S(2)}, u32[]{:S(2)}) %all-to-all-start.3) | async-done | bytes 1048608 | tf_op jit(solution)/shard_map/all_to_all | solution.py:544
  191.7 0.9 token_total.1
  (5 shorter events, 0.0 us)
Async XLA Ops:
  10.7 25.2 %all-to-all-start = ((bf16[8,64,1024]{2,1,0:T(8,128)(2,1)}), bf16[8,64,1024]{2,1,0:T(8,128)(2,1)S(1)}, u32[]{:S(2)}, u32[]{:S(2)}) async-start(bf16[8,64,1024]{2,1,0:T(8,128)(2,1)} %cut_tokens.1), calls=%async_computation | async-start | bytes 2097152 | tf_op jit(solution)/shard_map/all_to_all | solution.py:544
  18.7 80.4 %all-gather.5.cloned.1.call-start = ((), (), s32[]{:S(2)}) async-start(), calls=%async_computation.4 | async-start | bytes 2359296 | tf_op jit(solution)/shard_map/all_gather | solution.py:585
  18.8 19.8 %copy-start.2 = (s32[2]{0:T(128)S(1)}, s32[2]{0:T(128)}, u32[]{:S(2)}) copy-start(s32[2]{0:T(128)} %pad_add_fusion.pos_ref) | copy-start | bytes 28
  36.0 9.9 %copy-start = (bf16[8,64,1024]{2,1,0:T(8,128)(2,1)}, bf16[8,64,1024]{2,1,0:T(8,128)(2,1)S(1)}, u32[]{:S(2)}) copy-start(bf16[8,64,1024]{2,1,0:T(8,128)(2,1)S(1)} %all-to-all-done.mine_ref) | copy-start | bytes 3145732
  36.0 2.7 %collective-permute-start = (bf16[8,64,1024]{2,1,0:T(8,128)(2,1)S(1)}, bf16[8,64,1024]{2,1,0:T(8,128)(2,1)S(1)}, u32[]{:S(2)}, u32[]{:S(2)}) collective-permute-start(bf16[8,64,1024]{2,1,0:T(8,128)(2,1)S(1)} %all-to-all-done.mine_ref), channel_id=1, source_target_pairs={{0,2},{2,0},{4,6},{6,4},{8,10},{10,8},{12,14},{14,12},{1,3},{3,1},... | collective-permute-start | bytes 3145736 | tf_op jit(solution)/shard_map/ppermute | solution.py:579
  36.0 9.9 %collective-permute-start.1 = (bf16[8,16,1024]{2,1,0:T(8,128)(2,1)S(1)}, bf16[8,16,1024]{2,1,0:T(8,128)(2,1)S(1)}, u32[]{:S(2)}, u32[]{:S(2)}) collective-permute-start(bf16[8,16,1024]{2,1,0:T(8,128)(2,1)S(1)} %constant_dynamic-slice_fusion), channel_id=1, source_target_pairs={{0,1},{1,0},{2,3},{3,2},{4,5},{5,4},{6,7},{7,6},{8,9},{9,8},{10,11... | collective-permute-start | bytes 786440 | tf_op jit(solution)/shard_map/ppermute | solution.py:583
  38.6 7.3 %copy-start.1 = (bf16[8,64,1024]{2,1,0:T(8,128)(2,1)}, bf16[8,64,1024]{2,1,0:T(8,128)(2,1)S(1)}, u32[]{:S(2)}) copy-start(bf16[8,64,1024]{2,1,0:T(8,128)(2,1)S(1)} %collective-permute-done.theirs_ref) | copy-start | bytes 3145732
  45.9 0.7 copy-start.4
  46.6 3.9 %copy-start.5 = (f32[3,3,512]{2,1,0:T(4,128)S(1)}, f32[3,3,512]{2,1,0:T(4,128)}, u32[]{:S(2)}) copy-start(f32[3,3,512]{2,1,0:T(4,128)} %param.10) | copy-start | bytes 55300
  46.6 3.9 %copy-start.6 = (f32[512]{0:T(512)S(1)}, f32[512]{0:T(512)}, u32[]{:S(2)}) copy-start(f32[512]{0:T(512)} %param.12) | copy-start | bytes 6148
  46.6 46.9 %copy-start.3 = (f32[8,256]{1,0:T(8,128)S(1)}, f32[8,256]{1,0:T(8,128)}, u32[]{:S(2)}) copy-start(f32[8,256]{1,0:T(8,128)} %constant.48.clone.phase_ref) | copy-start | bytes 24580
  46.6 46.9 %all-to-all-start.1 = ((bf16[8,208,1024]{2,1,0:T(8,128)(2,1)}), bf16[8,208,1024]{2,1,0:T(8,128)(2,1)S(1)}, u32[]{:S(2)}, u32[]{:S(2)}) async-start(bf16[8,208,1024]{2,1,0:T(8,128)(2,1)} %project.1), calls=%async_computation.1 | async-start | bytes 6815744 | tf_op jit(solution)/shard_map/all_to_all | solution.py:544
  50.5 108.2 %all-gather.7.cloned.1.call-start = ((), (), s32[]{:S(2)}) async-start(), calls=%async_computation.5 | async-start | bytes 6684672 | tf_op jit(solution)/shard_map/all_gather | solution.py:594
  111.4 6.9 %collective-permute-start.2 = (bf16[8,64,128]{2,1,0:T(8,128)(2,1)S(1)}, bf16[8,64,128]{2,1,0:T(8,128)(2,1)S(1)}, u32[]{:S(2)}, u32[]{:S(2)}) collective-permute-start(bf16[8,64,128]{2,1,0:T(8,128)(2,1)S(1)} %slice.4), channel_id=1, source_target_pairs={{0,1},{1,0},{2,3},{3,2},{4,5},{5,4},{6,7},{7,6},{8,9},{9,8},{10,11... | collective-permute-start | bytes 393224 | tf_op jit(solution)/shard_map/ppermute | solution.py:596
  166.7 2.9 %collective-permute-start.3 = (bf16[512,1024]{1,0:T(8,128)(2,1)}, bf16[512,1024]{1,0:T(8,128)(2,1)S(1)}, u32[]{:S(2)}, u32[]{:S(2)}) collective-permute-start(bf16[512,1024]{1,0:T(8,128)(2,1)} %get-tuple-element.46), channel_id=1, source_target_pairs={{0,2},{2,0},{4,6},{6,4},{8,10},{10,8},{12,14},{14,12},{1,3},{3,1},... | collective-permute-start | bytes 3145736 | tf_op jit(solution)/shard_map/ppermute | solution.py:604
  172.0 19.6 %all-to-all-start.3 = ((bf16[4,128,1024]{2,1,0:T(8,128)(2,1)}), bf16[4,128,1024]{2,1,0:T(8,128)(2,1)S(1)}, u32[]{:S(2)}, u32[]{:S(2)}) async-start(bf16[4,128,1024]{2,1,0:T(8,128)(2,1)} %bitcast.13), calls=%async_computation.3 | async-start | bytes 2097152 | tf_op jit(solution)/shard_map/all_to_all | solution.py:544
Sparse Core Ops, SparseCore 0:
  46.7 22.2 all-gather.4
  99.3 59.2 all-gather.6

commit v6 on v5

--- a/solution.py
+++ b/solution.py
@@ -126,13 +126,13 @@
     return jnp.asarray(np.stack(tables), BF), jnp.asarray(np.stack(phases), F32)
 
 
-def cut_kernel(pos_ref, tokens_ref, out_ref):
+def cut_kernel(core_ref, tokens_ref, out_ref):
     slabs, _, width = out_ref.shape
     for slab in range(slabs):
         out_ref[slab] = tokens_ref[0, :, slab * width : (slab + 1) * width]
 
 
-def cut_tokens(pos, tokens, slabs):
+def cut_tokens(core, tokens, slabs):
     _, rows, width = tokens.shape
     dims = (slabs, rows // 2, width // slabs)
     return pl.pallas_call(
@@ -140,14 +140,14 @@
         grid_spec=pltpu.PrefetchScalarGridSpec(
             num_scalar_prefetch=1,
             grid=(1,),
-            in_specs=[pl.BlockSpec((1, rows // 2, width), lambda i, pos: (0, pos[1], 0))],
-            out_specs=pl.BlockSpec(dims, lambda i, pos: (0, 0, 0)),
+            in_specs=[pl.BlockSpec((1, rows // 2, width), lambda i, core: (0, core[0], 0))],
+            out_specs=pl.BlockSpec(dims, lambda i, core: (0, 0, 0)),
         ),
         out_shape=kept(dims),
         compiler_params=params(),
         cost_estimate=cost(0, 2 * tokens.size),
         name="cut_tokens",
-    )(pos, tokens)
+    )(core, tokens)
 
 
 def in_order(core, mine_ref, theirs_ref, spread_ref):
@@ -409,41 +409,66 @@
     )(parts, taps, phase, stay(table))
 
 
+def near_kernel(weight_ref, out_ref, sem):
+    copy = pltpu.make_async_copy(weight_ref, out_ref, sem)
+    copy.start()
+    copy.wait()
+
+
+def near_weight(weight):
+    return pl.pallas_call(
+        near_kernel,
+        in_specs=[pl.BlockSpec(memory_space=pltpu.HBM)],
+        out_specs=pl.BlockSpec(memory_space=pltpu.VMEM),
+        out_shape=pltpu.VMEM(weight.shape, weight.dtype),
+        scratch_shapes=[pltpu.SemaphoreType.DMA],
+        compiler_params=params(16 << 20),
+        cost_estimate=cost(0, 4 * weight.size),
+        name="near_weight",
+    )(stay(weight))
+
+
 def token_kernel(pos_ref, weight_ref, grads_ref, sent_ref, held_ref):
     streams, chips, _, rows, cols = weight_ref.shape
-    positions = sent_ref.shape[1]
-    grads = [grads_ref[:, 0, stream].reshape(cols, positions) for stream in range(streams)]
-    for side, out_ref in ((1 - pos_ref[1], sent_ref), (pos_ref[1], held_ref)):
+    part = sent_ref.shape[1]
+    grads = [grads_ref[:, 0, stream].reshape(cols, part) for stream in range(streams)]
+    lanes = pl.ds(pl.multiple_of(pl.program_id(0) * part, part), part)
+    for own in (False, True):
         total = None
+        side = pos_ref[1] if own else 1 - pos_ref[1]
         for stream in range(streams):
             weight = weight_ref[stream, :, pl.ds(side, 1)].reshape(chips * rows, cols)
-            part = matmul(weight, grads[stream], NN)
-            total = part if total is None else total + part
-        out_ref[...] = total.astype(BF)
-
-
-def token_part(pos, weight, grads, chan_count):
-    streams, slab_rows, cols = weight.shape
+            term = matmul(weight, grads[stream], NN)
+            total = term if total is None else total + term
+        if own:
+            held_ref[:, lanes] = total.astype(BF)
+        else:
+            sent_ref[...] = total.astype(BF)
+
+
+def token_part(pos, weight, grads):
+    streams, chips, cores, rows, cols = weight.shape
     slabs, _, _, chans, positions = grads.shape
-    rows = slab_rows // chan_count
     part = positions // 4
-    dims = (streams, chan_count // 2, 2, rows, cols)
     return pl.pallas_call(
         token_kernel,
         grid_spec=pltpu.PrefetchScalarGridSpec(
             num_scalar_prefetch=1,
             grid=(4,),
             in_specs=[
-                pl.BlockSpec(dims, lambda j, pos: (0, 0, 0, 0, 0)),
+                pl.BlockSpec(memory_space=pltpu.VMEM),
                 pl.BlockSpec((slabs, 1, streams, chans, part), lambda j, pos: (0, pos[0], 0, 0, j)),
             ],
-            out_specs=[pl.BlockSpec((slab_rows // 2, part), lambda j, pos: (0, j))] * 2,
-        ),
-        out_shape=(kept((slab_rows // 2, positions)), kept((slab_rows // 2, positions))),
-        compiler_params=params(),
-        cost_estimate=cost(2 * weight.size * positions, 8 * slab_rows * positions),
+            out_specs=[
+                pl.BlockSpec((chips * rows, part), lambda j, pos: (0, j)),
+                pl.BlockSpec(memory_space=pltpu.VMEM),
+            ],
+        ),
+        out_shape=(kept((chips * rows, positions)), pltpu.VMEM((chips * rows, positions), BF)),
+        compiler_params=params(40 << 20),
+        cost_estimate=cost(2 * weight.size * positions, 8 * chips * rows * positions),
         name="token_part",
-    )(pos, weight.reshape(dims), grads)
+    )(pos, weight, stay(grads))
 
 
 def pair_kernel(held_ref, received_ref, out_ref):
@@ -458,7 +483,7 @@
         compiler_params=params(24 << 20),
         cost_estimate=cost(0, 6 * held.size),
         name="pair_sum",
-    )(stay(held), received)
+    )(held, received)
 
 
 def weight_kernel(grad_scale, pos_ref, own_ref, other_ref, own_grads_ref, other_grads_ref, out_ref):
@@ -571,7 +596,7 @@
 
     mine, edge, flipped = lax.optimization_barrier(
         (
-            exchange(cut_tokens(pos, tokens, seq_count), "seq"),
+            exchange(cut_tokens(core[None], tokens, seq_count), "seq"),
             edge_rows(cotangent, long_filter, seq_count, positions),
             flip_weight(weight),
         )
@@ -594,13 +619,20 @@
     grads = lax.all_gather(grads, ("seq", "dp"), axis=0)
     outs = exchange(outs, "seq")
     finished = finish(outs, lax.ppermute(outs[:, chans:], "dp", batches))
-    grads, finished, own, other = lax.optimization_barrier(
-        (grads, finished, turn_tokens(pos, mine, theirs), turn_shares(shares))
-    )
+    own, other, near, finished = lax.optimization_barrier(
+        (
+            turn_tokens(pos, mine, theirs),
+            turn_shares(shares),
+            weight.reshape(streams, chips, 2, slab_rows // chan_count, chan_cols),
+            finished,
+        )
+    )
+    near = near_weight(near)
+    grads, finished, own, other = lax.optimization_barrier((grads, finished, own, other))
     hyena_out, grad_filter = finished
 
     grads = grads.reshape(seq_count, dp_count, streams, chans, positions)
-    sent, held = token_part(pos, weight, grads, chan_count)
+    sent, held = token_part(pos, near, grads)
     token_block = pair_sum(held, lax.ppermute(sent, "chan", cores))
     token_block = exchange(
         token_block.reshape(chips, -1, positions),

time: 200 us -> 197 us (0.985)
  waiting for transfers between devices: 97.4 us -> 94.9 us
    all_gather x1, waiting for transfers between devices: 30.4 us -> 28 us  [local(): grads = lax.all_gather(grads, ('seq', 'dp'), axis=0)]
    pallas_call x0 -> x1, Pallas kernels: none -> 2.34 us  [near_weight(): pl.pallas_call(near_kernel, in_specs=[pl.BlockSpec(memory_space=pltpu.HBM...]
  transfers between devices with their start and end apart: 9 -> 9, of which waited for: 7 -> 7; matrix products, arithmetic and copies ran while one was open for 0% -> 0% of each run, Pallas kernels for 21% -> 23%
where the time goes in v6:
time: 197 us; the launch traced here: 196 us
  waiting for transfers between devices  94.9 us (48%)
  Pallas kernels  55.7 us (28%)
  starting transfers between devices  17.6 us (9%)
  between operations  14.2 us (7%)
  blocking collectives  12.2 us (6%)
    all_to_all x3, waiting for transfers between devices, exchange(): lax.all_to_all(value, axis, split_axis=0, concat_axis=0, tiled=True, axis...  56 us
    all_gather x1, waiting for transfers between devices, local(): grads = lax.all_gather(grads, ('seq', 'dp'), axis=0)  28 us
    all_to_all x3, starting transfers between devices, exchange(): lax.all_to_all(value, axis, split_axis=0, concat_axis=0, tiled=True, axis...  16.1 us
    all_to_all x1, blocking collectives, exchange(): lax.all_to_all(value, axis, split_axis=0, concat_axis=0, tiled=True, axis...  12.2 us
    pallas_call x1, Pallas kernels, weight_grad(): pl.pallas_call(functools.partial(weight_kernel, grad_scale), grid_spec=pl...  11.7 us
    pallas_call x1, Pallas kernels, project(): pl.pallas_call(project_kernel, grid_spec=pltpu.PrefetchScalarGridSpec(num...  7.24 us
    pallas_call x1, Pallas kernels, token_part(): pl.pallas_call(token_kernel, grid_spec=pltpu.PrefetchScalarGridSpec(num_s...  6.7 us
    ppermute x1, waiting for transfers between devices, local(): finished = finish(outs, lax.ppermute(outs[:, chans:], 'dp', batches))  6.22 us
  transfers between devices with their start and end apart: 9, of which 7 were waited for; matrix products, arithmetic and copies ran while one was open for 0% of the time, Pallas kernels for 23%

profile of v6, /device:TPU:0, one launch (start us, length us, event | category | flops | bytes accessed | tf_op | source)
XLA Modules:
  0.0 195.6 jit_solution(7589932133054166379)
XLA Ops:
  7.2 2.3 %cut_tokens.1 = bf16[8,64,1024]{2,1,0:T(8,128)(2,1)} custom-call(s32[1]{0:T(128)} %bitcast.1.core_ref, bf16[1,128,8192]{2,1,0:T(8,128)(2,1)} %tokens_ref.1), custom_call_target="tpu_custom_call" | custom-call | bytes 2097152 | tf_op jit(solution)/shard_map/cut_tokens/pallas_call | solution.py:138
  9.5 8.0 %all-to-all-start = ((bf16[8,64,1024]{2,1,0:T(8,128)(2,1)}), bf16[8,64,1024]{2,1,0:T(8,128)(2,1)S(1)}, u32[]{:S(2)}, u32[]{:S(2)}) async-start(bf16[8,64,1024]{2,1,0:T(8,128)(2,1)} %cut_tokens.1), calls=%async_computation | async-start | bytes 2097152 | tf_op jit(solution)/shard_map/all_to_all | solution.py:569
  17.5 0.0 all-gather.5.cloned.1.call-start
  17.6 5.7 %flip_weight.1.weight_ref = bf16[3,512,1024]{2,1,0:T(8,128)(2,1)} custom-call(bf16[3,1024,512]{2,1,0:T(8,128)(2,1)} %bitcast.13), custom_call_target="tpu_custom_call" | custom-call | bytes 6291456 | tf_op jit(solution)/shard_map/flip_weight/pallas_call | solution.py:89
  23.3 1.9 edge_rows.1.edge_ref
  25.2 9.6 %all-to-all-done.mine_ref = bf16[8,64,1024]{2,1,0:T(8,128)(2,1)S(1)} async-done(((bf16[8,64,1024]{2,1,0:T(8,128)(2,1)}), bf16[8,64,1024]{2,1,0:T(8,128)(2,1)S(1)}, u32[]{:S(2)}, u32[]{:S(2)}) %all-to-all-start) | async-done | bytes 1048608 | tf_op jit(solution)/shard_map/all_to_all | solution.py:569
  34.7 0.0 collective-permute-start
  34.7 0.1 pad_add_fusion.pos_ref
  34.8 0.8 collective-permute-start.1
  35.6 1.8 collective-permute-done.theirs_ref
  37.4 7.2 %project.1 = bf16[8,208,1024]{2,1,0:T(8,128)(2,1)} custom-call(s32[2]{0:T(128)S(1)} %pad_add_fusion.pos_ref, bf16[8,64,1024]{2,1,0:T(8,128)(2,1)S(1)} %all-to-all-done.mine_ref, bf16[8,64,1024]{2,1,0:T(8,128)(2,1)S(1)} %collective-permute-done.theirs_ref, bf16[3,512,1024]{2,1,0:T(8,128)(2,1)} %flip_weight.1.weight_ref, bf16[8,16,1024]{2,1,0:T(8,128)(2,1)} %edge_rows.1.edge_ref), custom_call_target="tpu_custom_call" | custom-call | flops 3221225472 | bytes 8388608 | tf_op jit(solution)/shard_map/project/pallas_call | solution.py:184
  44.6 0.0 copy-done
  44.6 0.0 copy-done.2
  44.6 0.0 copy-done.1
  44.6 0.0 collective-permute-done.1
  44.7 0.0 copy-start.5
  44.7 0.7 copy-done.5
  45.4 0.0 all-gather.5.cloned.1.call-update
  45.4 0.0 copy-start.6
  45.4 0.0 copy-start.7
  45.4 0.0 copy-start.4
  45.4 3.8 %all-to-all-start.1 = ((bf16[8,208,1024]{2,1,0:T(8,128)(2,1)}), bf16[8,208,1024]{2,1,0:T(8,128)(2,1)S(1)}, u32[]{:S(2)}, u32[]{:S(2)}) async-start(bf16[8,208,1024]{2,1,0:T(8,128)(2,1)} %project.1), calls=%async_computation.1 | async-start | bytes 6815744 | tf_op jit(solution)/shard_map/all_to_all | solution.py:569
  49.2 0.0 all-gather.7.cloned.1.call-start
  49.3 0.0 copy-done.6
  49.3 0.0 copy-done.7
  49.3 0.1 fusion
  49.4 0.1 copy.16
  49.5 42.8 %all-to-all-done.1.parts_ref = bf16[8,208,1024]{2,1,0:T(8,128)(2,1)S(1)} async-done(((bf16[8,208,1024]{2,1,0:T(8,128)(2,1)}), bf16[8,208,1024]{2,1,0:T(8,128)(2,1)S(1)}, u32[]{:S(2)}, u32[]{:S(2)}) %all-to-all-start.1) | async-done | bytes 3407904 | tf_op jit(solution)/shard_map/all_to_all | solution.py:569
  92.3 0.0 copy-done.4
  92.3 5.7 %operator.1 = (bf16[192,1024]{1,0:T(8,128)(2,1)}, bf16[8,128,128]{2,1,0:T(8,128)(2,1)}) custom-call(bf16[8,208,1024]{2,1,0:T(8,128)(2,1)S(1)} %all-to-all-done.1.parts_ref, f32[64,10]{1,0:T(8,128)S(1)} %bitcast.12, f32[8,256]{1,0:T(8,128)S(1)} %copy-done.4, bf16[4,512,512]{2,1,0:T(8,128)(2,1)} %constant.47.clone.table_ref), custom_call_target="tpu_custom_call" | custom-call | flops 1610612736 | bytes 5505024 | tf_op jit(solution)/shard_map/operator/pallas_call | solution.py:401
  98.0 0.0 all-gather.5.cloned.1.call-done
  98.0 0.0 all-gather.7.cloned.1.call-update
  98.0 12.2 %all_to_all.20.own_ref = bf16[8,128,128]{2,1,0:T(8,128)(2,1)S(1)} all-to-all(bf16[8,128,128]{2,1,0:T(8,128)(2,1)} %get-tuple-element.45), channel_id=1, replica_groups=mesh['seq'=8,'chan'=8,'dp'=2] {'seq'}, dimensions={0} | all-to-all | bytes 524288 | tf_op jit(solution)/shard_map/all_to_all | solution.py:569
  110.2 0.7 collective-permute-start.2
  110.9 6.2 %collective-permute-done.2.other_ref = bf16[8,64,128]{2,1,0:T(8,128)(2,1)S(1)} collective-permute-done((bf16[8,64,128]{2,1,0:T(8,128)(2,1)S(1)}, bf16[8,64,128]{2,1,0:T(8,128)(2,1)S(1)}, u32[]{:S(2)}, u32[]{:S(2)}) %collective-permute-start.2) | collective-permute-done | bytes 131104 | tf_op jit(solution)/shard_map/ppermute | solution.py:621
  117.1 0.9 finish.1
  118.0 4.2 %turn_shares.1.other_ref = bf16[1024,1024]{1,0:T(8,128)(2,1)} custom-call(bf16[4,2,8,16,1024]{4,3,2,1,0:T(8,128)(2,1)} %bitcast.16), custom_call_target="tpu_custom_call" | custom-call | bytes 4194304 | tf_op jit(solution)/shard_map/turn_shares/pallas_call | solution.py:248
  122.2 4.9 %turn_tokens.1.own_ref = bf16[1024,1024]{1,0:T(8,128)(2,1)} custom-call(s32[2]{0:T(128)} %copy-done.2, bf16[8,64,1024]{2,1,0:T(8,128)(2,1)} %copy-done, bf16[8,64,1024]{2,1,0:T(8,128)(2,1)} %copy-done.1), custom_call_target="tpu_custom_call" | custom-call | bytes 4194304 | tf_op jit(solution)/shard_map/turn_tokens/pallas_call | solution.py:218
  127.1 2.3 %near_weight.1.weight_ref = bf16[3,4,2,128,512]{4,3,2,1,0:T(8,128)(2,1)S(1)} custom-call(bf16[3,4,2,128,512]{4,3,2,1,0:T(8,128)(2,1)} %bitcast.14), custom_call_target="tpu_custom_call" | custom-call | bytes 6291456 | tf_op jit(solution)/shard_map/near_weight/pallas_call | solution.py:419
  129.5 28.0 %all-gather.7.cloned.1.call-done = bf16[3072,1024]{1,0:T(8,128)(2,1)} async-done(((bf16[192,1024]{1,0:T(8,128)(2,1)}), bf16[3072,1024]{1,0:T(8,128)(2,1)}) %all-gather.7.cloned.1.call-update) | async-done | bytes 6291472 | tf_op jit(solution)/shard_map/all_gather | solution.py:619
  157.4 6.7 %token_part.1 = (bf16[512,1024]{1,0:T(8,128)(2,1)}, bf16[512,1024]{1,0:T(8,128)(2,1)S(1)}) custom-call(s32[2]{0:T(128)S(1)} %copy-done.3, bf16[3,4,2,128,512]{4,3,2,1,0:T(8,128)(2,1)S(1)} %near_weight.1.weight_ref, bf16[8,2,3,64,1024]{4,3,2,1,0:T(8,128)(2,1)} %bitcast.18), custom_call_target="tpu_custom_call" | custom-call | flops 3221225472 | bytes 4194304 | tf_op jit(solution)/shard_map/token_part/pallas_call | solution.py:453
  164.1 0.0 collective-permute-start.3
  164.2 2.9 %collective-permute-done.3.received_ref = bf16[512,1024]{1,0:T(8,128)(2,1)S(1)} collective-permute-done((bf16[512,1024]{1,0:T(8,128)(2,1)}, bf16[512,1024]{1,0:T(8,128)(2,1)S(1)}, u32[]{:S(2)}, u32[]{:S(2)}) %collective-permute-start.3) | collective-permute-done | bytes 1048608 | tf_op jit(solution)/shard_map/ppermute | solution.py:636
  167.0 1.2 pair_sum.1
  168.2 4.2 %all-to-all-start.3 = ((bf16[4,128,1024]{2,1,0:T(8,128)(2,1)}), bf16[4,128,1024]{2,1,0:T(8,128)(2,1)S(1)}, u32[]{:S(2)}, u32[]{:S(2)}) async-start(bf16[4,128,1024]{2,1,0:T(8,128)(2,1)} %bitcast.15), calls=%async_computation.3 | async-start | bytes 2097152 | tf_op jit(solution)/shard_map/all_to_all | solution.py:569
  172.5 11.7 %weight_grad.1 = bf16[3,1024,512]{2,1,0:T(8,128)(2,1)} custom-call(s32[2]{0:T(128)} %copy-done.2, bf16[1024,1024]{1,0:T(8,128)(2,1)} %turn_tokens.1.own_ref, bf16[1024,1024]{1,0:T(8,128)(2,1)} %turn_shares.1.other_ref, bf16[8,2,3,64,1024]{4,3,2,1,0:T(8,128)(2,1)} %bitcast.19, bf16[8,2,3,64,1024]{4,3,2,1,0:T(8,128)(2,1)} %bitcast.20), custom_call_target="tpu_custom_call" | custom-call | flops 6442450944 | bytes 13631488 | tf_op jit(solution)/shard_map/weight_grad/pallas_call | solution.py:503
  184.2 3.7 %all-to-all-done.3.parts_ref = bf16[4,128,1024]{2,1,0:T(8,128)(2,1)S(1)} async-done(((bf16[4,128,1024]{2,1,0:T(8,128)(2,1)}), bf16[4,128,1024]{2,1,0:T(8,128)(2,1)S(1)}, u32[]{:S(2)}, u32[]{:S(2)}) %all-to-all-start.3) | async-done | bytes 1048608 | tf_op jit(solution)/shard_map/all_to_all | solution.py:569
  187.9 0.9 token_total.1
  (8 shorter events, 0.1 us)
Async XLA Ops:
  9.5 25.2 %all-to-all-start = ((bf16[8,64,1024]{2,1,0:T(8,128)(2,1)}), bf16[8,64,1024]{2,1,0:T(8,128)(2,1)S(1)}, u32[]{:S(2)}, u32[]{:S(2)}) async-start(bf16[8,64,1024]{2,1,0:T(8,128)(2,1)} %cut_tokens.1), calls=%async_computation | async-start | bytes 2097152 | tf_op jit(solution)/shard_map/all_to_all | solution.py:569
  17.5 80.5 %all-gather.5.cloned.1.call-start = ((), (), s32[]{:S(2)}) async-start(), calls=%async_computation.4 | async-start | bytes 2359296 | tf_op jit(solution)/shard_map/all_gather | solution.py:610
  34.7 9.9 %copy-start = (bf16[8,64,1024]{2,1,0:T(8,128)(2,1)}, bf16[8,64,1024]{2,1,0:T(8,128)(2,1)S(1)}, u32[]{:S(2)}) copy-start(bf16[8,64,1024]{2,1,0:T(8,128)(2,1)S(1)} %all-to-all-done.mine_ref) | copy-start | bytes 3145732
  34.7 2.7 %collective-permute-start = (bf16[8,64,1024]{2,1,0:T(8,128)(2,1)S(1)}, bf16[8,64,1024]{2,1,0:T(8,128)(2,1)S(1)}, u32[]{:S(2)}, u32[]{:S(2)}) collective-permute-start(bf16[8,64,1024]{2,1,0:T(8,128)(2,1)S(1)} %all-to-all-done.mine_ref), channel_id=1, source_target_pairs={{0,2},{2,0},{4,6},{6,4},{8,10},{10,8},{12,14},{14,12},{1,3},{3,1},... | collective-permute-start | bytes 3145736 | tf_op jit(solution)/shard_map/ppermute | solution.py:604
  34.8 9.8 %copy-start.2 = (s32[2]{0:T(128)}, s32[2]{0:T(128)S(1)}, u32[]{:S(2)}) copy-start(s32[2]{0:T(128)S(1)} %pad_add_fusion.pos_ref) | copy-start | bytes 28
  34.8 9.8 %collective-permute-start.1 = (bf16[8,16,1024]{2,1,0:T(8,128)(2,1)S(1)}, bf16[8,16,1024]{2,1,0:T(8,128)(2,1)S(1)}, u32[]{:S(2)}, u32[]{:S(2)}) collective-permute-start(bf16[8,16,1024]{2,1,0:T(8,128)(2,1)S(1)} %constant_dynamic-slice_fusion), channel_id=1, source_target_pairs={{0,1},{1,0},{2,3},{3,2},{4,5},{5,4},{6,7},{7,6},{8,9},{9,8},{10,11... | collective-permute-start | bytes 786440 | tf_op jit(solution)/shard_map/ppermute | solution.py:608
  37.4 7.3 %copy-start.1 = (bf16[8,64,1024]{2,1,0:T(8,128)(2,1)}, bf16[8,64,1024]{2,1,0:T(8,128)(2,1)S(1)}, u32[]{:S(2)}) copy-start(bf16[8,64,1024]{2,1,0:T(8,128)(2,1)S(1)} %collective-permute-done.theirs_ref) | copy-start | bytes 3145732
  44.7 0.7 copy-start.5
  45.4 3.9 %copy-start.6 = (f32[3,3,512]{2,1,0:T(4,128)S(1)}, f32[3,3,512]{2,1,0:T(4,128)}, u32[]{:S(2)}) copy-start(f32[3,3,512]{2,1,0:T(4,128)} %param.10) | copy-start | bytes 55300
  45.4 3.9 %copy-start.7 = (f32[512]{0:T(512)S(1)}, f32[512]{0:T(512)}, u32[]{:S(2)}) copy-start(f32[512]{0:T(512)} %param.12) | copy-start | bytes 6148
  45.4 46.9 %copy-start.4 = (f32[8,256]{1,0:T(8,128)S(1)}, f32[8,256]{1,0:T(8,128)}, u32[]{:S(2)}) copy-start(f32[8,256]{1,0:T(8,128)} %constant.48.clone.phase_ref) | copy-start | bytes 24580
  45.4 46.9 %all-to-all-start.1 = ((bf16[8,208,1024]{2,1,0:T(8,128)(2,1)}), bf16[8,208,1024]{2,1,0:T(8,128)(2,1)S(1)}, u32[]{:S(2)}, u32[]{:S(2)}) async-start(bf16[8,208,1024]{2,1,0:T(8,128)(2,1)} %project.1), calls=%async_computation.1 | async-start | bytes 6815744 | tf_op jit(solution)/shard_map/all_to_all | solution.py:569
  49.2 108.2 %all-gather.7.cloned.1.call-start = ((), (), s32[]{:S(2)}) async-start(), calls=%async_computation.5 | async-start | bytes 6684672 | tf_op jit(solution)/shard_map/all_gather | solution.py:619
  110.2 6.9 %collective-permute-start.2 = (bf16[8,64,128]{2,1,0:T(8,128)(2,1)S(1)}, bf16[8,64,128]{2,1,0:T(8,128)(2,1)S(1)}, u32[]{:S(2)}, u32[]{:S(2)}) collective-permute-start(bf16[8,64,128]{2,1,0:T(8,128)(2,1)S(1)} %slice.4), channel_id=1, source_target_pairs={{0,1},{1,0},{2,3},{3,2},{4,5},{5,4},{6,7},{7,6},{8,9},{9,8},{10,11... | collective-permute-start | bytes 393224 | tf_op jit(solution)/shard_map/ppermute | solution.py:621
  127.1 30.3 %copy-start.3 = (s32[2]{0:T(128)S(1)}, s32[2]{0:T(128)}, u32[]{:S(2)}) copy-start(s32[2]{0:T(128)} %copy-done.2) | copy-start | bytes 28
  164.1 2.9 %collective-permute-start.3 = (bf16[512,1024]{1,0:T(8,128)(2,1)}, bf16[512,1024]{1,0:T(8,128)(2,1)S(1)}, u32[]{:S(2)}, u32[]{:S(2)}) collective-permute-start(bf16[512,1024]{1,0:T(8,128)(2,1)} %get-tuple-element.56), channel_id=1, source_target_pairs={{0,2},{2,0},{4,6},{6,4},{8,10},{10,8},{12,14},{14,12},{1,3},{3,1},... | collective-permute-start | bytes 3145736 | tf_op jit(solution)/shard_map/ppermute | solution.py:636
  168.2 19.6 %all-to-all-start.3 = ((bf16[4,128,1024]{2,1,0:T(8,128)(2,1)}), bf16[4,128,1024]{2,1,0:T(8,128)(2,1)S(1)}, u32[]{:S(2)}, u32[]{:S(2)}) async-start(bf16[4,128,1024]{2,1,0:T(8,128)(2,1)} %bitcast.15), calls=%async_computation.3 | async-start | bytes 2097152 | tf_op jit(solution)/shard_map/all_to_all | solution.py:569
Sparse Core Ops, SparseCore 0:
  45.5 22.2 all-gather.4
  98.1 59.2 all-gather.6

commit v7 on v6

--- a/solution.py
+++ b/solution.py
@@ -34,11 +34,6 @@
 
 def matmul(left, right, dims):
     return lax.dot_general(left, right, dims, preferred_element_type=F32)
-
-
-def split(value):
-    high = value.astype(BF)
-    return high, (value - high.astype(F32)).astype(BF)
 
 
 def edge_kernel(cot_ref, filter_ref, out_ref):
@@ -126,10 +121,28 @@
     return jnp.asarray(np.stack(tables), BF), jnp.asarray(np.stack(phases), F32)
 
 
-def cut_kernel(core_ref, tokens_ref, out_ref):
-    slabs, _, width = out_ref.shape
+def cut_kernel(core_ref, tokens_ref, out_ref, held_ref, in_sems, out_sems):
+    slabs, half, width = held_ref.shape
+    start = pl.multiple_of(core_ref[0] * half, half)
+    inward = [
+        pltpu.make_async_copy(
+            tokens_ref.at[0, pl.ds(start, half), slice(slab * width, (slab + 1) * width)],
+            held_ref.at[slab],
+            in_sems.at[slab],
+        )
+        for slab in range(slabs)
+    ]
+    outward = [
+        pltpu.make_async_copy(held_ref.at[slab], out_ref.at[slab], out_sems.at[slab])
+        for slab in range(slabs)
+    ]
+    for copy in inward:
+        copy.start()
     for slab in range(slabs):
-        out_ref[slab] = tokens_ref[0, :, slab * width : (slab + 1) * width]
+        inward[slab].wait()
+        outward[slab].start()
+    for copy in outward:
+        copy.wait()
 
 
 def cut_tokens(core, tokens, slabs):
@@ -137,17 +150,18 @@
     dims = (slabs, rows // 2, width // slabs)
     return pl.pallas_call(
         cut_kernel,
-        grid_spec=pltpu.PrefetchScalarGridSpec(
-            num_scalar_prefetch=1,
-            grid=(1,),
-            in_specs=[pl.BlockSpec((1, rows // 2, width), lambda i, core: (0, core[0], 0))],
-            out_specs=pl.BlockSpec(dims, lambda i, core: (0, 0, 0)),
-        ),
+        in_specs=[pl.BlockSpec(memory_space=pltpu.SMEM), pl.BlockSpec(memory_space=pltpu.HBM)],
+        out_specs=pl.BlockSpec(memory_space=pltpu.HBM),
         out_shape=kept(dims),
+        scratch_shapes=[
+            pltpu.VMEM(dims, BF),
+            pltpu.SemaphoreType.DMA((slabs,)),
+            pltpu.SemaphoreType.DMA((slabs,)),
+        ],
         compiler_params=params(),
         cost_estimate=cost(0, 2 * tokens.size),
         name="cut_tokens",
-    )(core, tokens)
+    )(core, stay(tokens))
 
 
 def in_order(core, mine_ref, theirs_ref, spread_ref):
@@ -273,12 +287,6 @@
     return jnp.where(lane >= lanes - steps, 0.0, pltpu.roll(value, lanes - steps, 1))
 
 
-def two_part(value, table, dims):
-    rows = value.shape[0]
-    result = matmul(jnp.concatenate(split(value), axis=0), table, dims)
-    return result[:rows] + result[rows:]
-
-
 def spectrum(value, residue, table):
     width = value.shape[1] // BLOCKS
     parts = [value[:, block * width : (block + 1) * width] for block in range(BLOCKS)]
@@ -289,7 +297,7 @@
         real = real + parts[block] * math.cos(angle)
         term = parts[block] * -math.sin(angle)
         imag = term if imag is None else imag + term
-    result = two_part(jnp.concatenate([real, imag], axis=1), table, NN)
+    result = matmul(jnp.concatenate([real, imag], axis=1).astype(BF), table, NN)
     steps = result.shape[1] // 4
     quarter = [result[:, i * steps : (i + 1) * steps] for i in range(4)]
     return jnp.concatenate([quarter[0], quarter[2]], axis=1), jnp.concatenate(
@@ -302,7 +310,7 @@
     value = jnp.concatenate(
         [real[:, :steps], imag[:, :steps], real[:, steps:], imag[:, steps:]], axis=1
     )
-    result = two_part(value, table, NT)
+    result = matmul(value.astype(BF), table, NT)
     width = result.shape[1] // 2
     even, odd = result[:, :width], result[:, width:]
     for block in range(BLOCKS):

time: 197 us -> 196 us (level)
  transfers between devices with their start and end apart: 9 -> 9, of which waited for: 7 -> 7; matrix products, arithmetic and copies ran while one was open for 0% -> 0% of each run, Pallas kernels for 23% -> 22%
where the time goes in v7:
time: 196 us; the launch traced here: 195 us
  waiting for transfers between devices  95 us (48%)
  Pallas kernels  54.5 us (28%)
  starting transfers between devices  17.7 us (9%)
  between operations  14.2 us (7%)
  blocking collectives  12.2 us (6%)
    all_to_all x3, waiting for transfers between devices, exchange(): lax.all_to_all(value, axis, split_axis=0, concat_axis=0, tiled=True, axis...  56 us
    all_gather x1, waiting for transfers between devices, local(): grads = lax.all_gather(grads, ('seq', 'dp'), axis=0)  28 us
    all_to_all x3, starting transfers between devices, exchange(): lax.all_to_all(value, axis, split_axis=0, concat_axis=0, tiled=True, axis...  16.1 us
    all_to_all x1, blocking collectives, exchange(): lax.all_to_all(value, axis, split_axis=0, concat_axis=0, tiled=True, axis...  12.2 us
    pallas_call x1, Pallas kernels, weight_grad(): pl.pallas_call(functools.partial(weight_kernel, grad_scale), grid_spec=pl...  11.7 us
    pallas_call x1, Pallas kernels, project(): pl.pallas_call(project_kernel, grid_spec=pltpu.PrefetchScalarGridSpec(num...  7.25 us
    pallas_call x1, Pallas kernels, token_part(): pl.pallas_call(token_kernel, grid_spec=pltpu.PrefetchScalarGridSpec(num_s...  6.7 us
    ppermute x1, waiting for transfers between devices, local(): finished = finish(outs, lax.ppermute(outs[:, chans:], 'dp', batches))  6.22 us
  transfers between devices with their start and end apart: 9, of which 7 were waited for; matrix products, arithmetic and copies ran while one was open for 0% of the time, Pallas kernels for 22%

profile of v7, /device:TPU:0, one launch (start us, length us, event | category | flops | bytes accessed | tf_op | source)
XLA Modules:
  0.0 194.5 jit_solution(17588504790175320369)
XLA Ops:
  7.2 2.1 %cut_tokens.1 = bf16[8,64,1024]{2,1,0:T(8,128)(2,1)} custom-call(s32[1]{0:T(128)} %bitcast.1.core_ref, bf16[1,128,8192]{2,1,0:T(8,128)(2,1)} %tokens_ref.1), custom_call_target="tpu_custom_call" | custom-call | bytes 2097152 | tf_op jit(solution)/shard_map/cut_tokens/pallas_call | solution.py:151
  9.3 8.0 %all-to-all-start = ((bf16[8,64,1024]{2,1,0:T(8,128)(2,1)}), bf16[8,64,1024]{2,1,0:T(8,128)(2,1)S(1)}, u32[]{:S(2)}, u32[]{:S(2)}) async-start(bf16[8,64,1024]{2,1,0:T(8,128)(2,1)} %cut_tokens.1), calls=%async_computation | async-start | bytes 2097152 | tf_op jit(solution)/shard_map/all_to_all | solution.py:577
  17.3 0.0 all-gather.5.cloned.1.call-start
  17.4 5.7 %flip_weight.1.weight_ref = bf16[3,512,1024]{2,1,0:T(8,128)(2,1)} custom-call(bf16[3,1024,512]{2,1,0:T(8,128)(2,1)} %bitcast.13), custom_call_target="tpu_custom_call" | custom-call | bytes 6291456 | tf_op jit(solution)/shard_map/flip_weight/pallas_call | solution.py:84
  23.1 1.9 edge_rows.1.edge_ref
  25.0 9.6 %all-to-all-done.mine_ref = bf16[8,64,1024]{2,1,0:T(8,128)(2,1)S(1)} async-done(((bf16[8,64,1024]{2,1,0:T(8,128)(2,1)}), bf16[8,64,1024]{2,1,0:T(8,128)(2,1)S(1)}, u32[]{:S(2)}, u32[]{:S(2)}) %all-to-all-start) | async-done | bytes 1048608 | tf_op jit(solution)/shard_map/all_to_all | solution.py:577
  34.5 0.0 collective-permute-start
  34.5 0.1 pad_add_fusion.pos_ref
  34.6 0.8 collective-permute-start.1
  35.4 1.8 collective-permute-done.theirs_ref
  37.2 7.2 %project.1 = bf16[8,208,1024]{2,1,0:T(8,128)(2,1)} custom-call(s32[2]{0:T(128)S(1)} %pad_add_fusion.pos_ref, bf16[8,64,1024]{2,1,0:T(8,128)(2,1)S(1)} %all-to-all-done.mine_ref, bf16[8,64,1024]{2,1,0:T(8,128)(2,1)S(1)} %collective-permute-done.theirs_ref, bf16[3,512,1024]{2,1,0:T(8,128)(2,1)} %flip_weight.1.weight_ref, bf16[8,16,1024]{2,1,0:T(8,128)(2,1)} %edge_rows.1.edge_ref), custom_call_target="tpu_custom_call" | custom-call | flops 3221225472 | bytes 8388608 | tf_op jit(solution)/shard_map/project/pallas_call | solution.py:198
  44.5 0.0 copy-done
  44.5 0.0 copy-done.2
  44.5 0.0 copy-done.1
  44.5 0.0 collective-permute-done.1
  44.5 0.0 copy-start.5
  44.5 0.7 copy-done.5
  45.2 0.0 all-gather.5.cloned.1.call-update
  45.2 0.0 copy-start.6
  45.2 0.0 copy-start.7
  45.2 0.0 copy-start.4
  45.2 3.8 %all-to-all-start.1 = ((bf16[8,208,1024]{2,1,0:T(8,128)(2,1)}), bf16[8,208,1024]{2,1,0:T(8,128)(2,1)S(1)}, u32[]{:S(2)}, u32[]{:S(2)}) async-start(bf16[8,208,1024]{2,1,0:T(8,128)(2,1)} %project.1), calls=%async_computation.1 | async-start | bytes 6815744 | tf_op jit(solution)/shard_map/all_to_all | solution.py:577
  49.1 0.0 all-gather.7.cloned.1.call-start
  49.1 0.0 copy-done.6
  49.1 0.0 copy-done.7
  49.1 0.1 fusion
  49.2 0.1 copy.16
  49.3 42.8 %all-to-all-done.1.parts_ref = bf16[8,208,1024]{2,1,0:T(8,128)(2,1)S(1)} async-done(((bf16[8,208,1024]{2,1,0:T(8,128)(2,1)}), bf16[8,208,1024]{2,1,0:T(8,128)(2,1)S(1)}, u32[]{:S(2)}, u32[]{:S(2)}) %all-to-all-start.1) | async-done | bytes 3407904 | tf_op jit(solution)/shard_map/all_to_all | solution.py:577
  92.1 0.0 copy-done.4
  92.1 4.7 %operator.1 = (bf16[192,1024]{1,0:T(8,128)(2,1)}, bf16[8,128,128]{2,1,0:T(8,128)(2,1)}) custom-call(bf16[8,208,1024]{2,1,0:T(8,128)(2,1)S(1)} %all-to-all-done.1.parts_ref, f32[64,10]{1,0:T(8,128)S(1)} %bitcast.12, f32[8,256]{1,0:T(8,128)S(1)} %copy-done.4, bf16[4,512,512]{2,1,0:T(8,128)(2,1)} %constant.47.clone.table_ref), custom_call_target="tpu_custom_call" | custom-call | flops 1610612736 | bytes 5505024 | tf_op jit(solution)/shard_map/operator/pallas_call | solution.py:409
  96.8 0.0 all-gather.5.cloned.1.call-done
  96.9 0.0 all-gather.7.cloned.1.call-update
  96.9 12.2 %all_to_all.20.own_ref = bf16[8,128,128]{2,1,0:T(8,128)(2,1)S(1)} all-to-all(bf16[8,128,128]{2,1,0:T(8,128)(2,1)} %get-tuple-element.45), channel_id=1, replica_groups=mesh['seq'=8,'chan'=8,'dp'=2] {'seq'}, dimensions={0} | all-to-all | bytes 524288 | tf_op jit(solution)/shard_map/all_to_all | solution.py:577
  109.0 0.7 collective-permute-start.2
  109.8 6.2 %collective-permute-done.2.other_ref = bf16[8,64,128]{2,1,0:T(8,128)(2,1)S(1)} collective-permute-done((bf16[8,64,128]{2,1,0:T(8,128)(2,1)S(1)}, bf16[8,64,128]{2,1,0:T(8,128)(2,1)S(1)}, u32[]{:S(2)}, u32[]{:S(2)}) %collective-permute-start.2) | collective-permute-done | bytes 131104 | tf_op jit(solution)/shard_map/ppermute | solution.py:629
  116.0 0.9 finish.1
  116.9 4.2 %turn_shares.1.other_ref = bf16[1024,1024]{1,0:T(8,128)(2,1)} custom-call(bf16[4,2,8,16,1024]{4,3,2,1,0:T(8,128)(2,1)} %bitcast.16), custom_call_target="tpu_custom_call" | custom-call | bytes 4194304 | tf_op jit(solution)/shard_map/turn_shares/pallas_call | solution.py:262
  121.0 4.9 %turn_tokens.1.own_ref = bf16[1024,1024]{1,0:T(8,128)(2,1)} custom-call(s32[2]{0:T(128)} %copy-done.2, bf16[8,64,1024]{2,1,0:T(8,128)(2,1)} %copy-done, bf16[8,64,1024]{2,1,0:T(8,128)(2,1)} %copy-done.1), custom_call_target="tpu_custom_call" | custom-call | bytes 4194304 | tf_op jit(solution)/shard_map/turn_tokens/pallas_call | solution.py:232
  126.0 2.3 %near_weight.1.weight_ref = bf16[3,4,2,128,512]{4,3,2,1,0:T(8,128)(2,1)S(1)} custom-call(bf16[3,4,2,128,512]{4,3,2,1,0:T(8,128)(2,1)} %bitcast.14), custom_call_target="tpu_custom_call" | custom-call | bytes 6291456 | tf_op jit(solution)/shard_map/near_weight/pallas_call | solution.py:427
  128.3 28.0 %all-gather.7.cloned.1.call-done = bf16[3072,1024]{1,0:T(8,128)(2,1)} async-done(((bf16[192,1024]{1,0:T(8,128)(2,1)}), bf16[3072,1024]{1,0:T(8,128)(2,1)}) %all-gather.7.cloned.1.call-update) | async-done | bytes 6291472 | tf_op jit(solution)/shard_map/all_gather | solution.py:627
  156.3 6.7 %token_part.1 = (bf16[512,1024]{1,0:T(8,128)(2,1)}, bf16[512,1024]{1,0:T(8,128)(2,1)S(1)}) custom-call(s32[2]{0:T(128)S(1)} %copy-done.3, bf16[3,4,2,128,512]{4,3,2,1,0:T(8,128)(2,1)S(1)} %near_weight.1.weight_ref, bf16[8,2,3,64,1024]{4,3,2,1,0:T(8,128)(2,1)} %bitcast.18), custom_call_target="tpu_custom_call" | custom-call | flops 3221225472 | bytes 4194304 | tf_op jit(solution)/shard_map/token_part/pallas_call | solution.py:461
  163.0 0.0 collective-permute-start.3
  163.0 2.9 %collective-permute-done.3.received_ref = bf16[512,1024]{1,0:T(8,128)(2,1)S(1)} collective-permute-done((bf16[512,1024]{1,0:T(8,128)(2,1)}, bf16[512,1024]{1,0:T(8,128)(2,1)S(1)}, u32[]{:S(2)}, u32[]{:S(2)}) %collective-permute-start.3) | collective-permute-done | bytes 1048608 | tf_op jit(solution)/shard_map/ppermute | solution.py:644
  165.9 1.2 pair_sum.1
  167.1 4.2 %all-to-all-start.3 = ((bf16[4,128,1024]{2,1,0:T(8,128)(2,1)}), bf16[4,128,1024]{2,1,0:T(8,128)(2,1)S(1)}, u32[]{:S(2)}, u32[]{:S(2)}) async-start(bf16[4,128,1024]{2,1,0:T(8,128)(2,1)} %bitcast.15), calls=%async_computation.3 | async-start | bytes 2097152 | tf_op jit(solution)/shard_map/all_to_all | solution.py:577
  171.4 11.7 %weight_grad.1 = bf16[3,1024,512]{2,1,0:T(8,128)(2,1)} custom-call(s32[2]{0:T(128)} %copy-done.2, bf16[1024,1024]{1,0:T(8,128)(2,1)} %turn_tokens.1.own_ref, bf16[1024,1024]{1,0:T(8,128)(2,1)} %turn_shares.1.other_ref, bf16[8,2,3,64,1024]{4,3,2,1,0:T(8,128)(2,1)} %bitcast.19, bf16[8,2,3,64,1024]{4,3,2,1,0:T(8,128)(2,1)} %bitcast.20), custom_call_target="tpu_custom_call" | custom-call | flops 6442450944 | bytes 13631488 | tf_op jit(solution)/shard_map/weight_grad/pallas_call | solution.py:511
  183.1 3.7 %all-to-all-done.3.parts_ref = bf16[4,128,1024]{2,1,0:T(8,128)(2,1)S(1)} async-done(((bf16[4,128,1024]{2,1,0:T(8,128)(2,1)}), bf16[4,128,1024]{2,1,0:T(8,128)(2,1)S(1)}, u32[]{:S(2)}, u32[]{:S(2)}) %all-to-all-start.3) | async-done | bytes 1048608 | tf_op jit(solution)/shard_map/all_to_all | solution.py:577
  186.8 0.9 token_total.1
  (8 shorter events, 0.1 us)
Async XLA Ops:
  9.3 25.2 %all-to-all-start = ((bf16[8,64,1024]{2,1,0:T(8,128)(2,1)}), bf16[8,64,1024]{2,1,0:T(8,128)(2,1)S(1)}, u32[]{:S(2)}, u32[]{:S(2)}) async-start(bf16[8,64,1024]{2,1,0:T(8,128)(2,1)} %cut_tokens.1), calls=%async_computation | async-start | bytes 2097152 | tf_op jit(solution)/shard_map/all_to_all | solution.py:577
  17.3 79.5 %all-gather.5.cloned.1.call-start = ((), (), s32[]{:S(2)}) async-start(), calls=%async_computation.4 | async-start | bytes 2359296 | tf_op jit(solution)/shard_map/all_gather | solution.py:618
  34.5 9.9 %copy-start = (bf16[8,64,1024]{2,1,0:T(8,128)(2,1)}, bf16[8,64,1024]{2,1,0:T(8,128)(2,1)S(1)}, u32[]{:S(2)}) copy-start(bf16[8,64,1024]{2,1,0:T(8,128)(2,1)S(1)} %all-to-all-done.mine_ref) | copy-start | bytes 3145732
  34.5 2.7 %collective-permute-start = (bf16[8,64,1024]{2,1,0:T(8,128)(2,1)S(1)}, bf16[8,64,1024]{2,1,0:T(8,128)(2,1)S(1)}, u32[]{:S(2)}, u32[]{:S(2)}) collective-permute-start(bf16[8,64,1024]{2,1,0:T(8,128)(2,1)S(1)} %all-to-all-done.mine_ref), channel_id=1, source_target_pairs={{0,2},{2,0},{4,6},{6,4},{8,10},{10,8},{12,14},{14,12},{1,3},{3,1},... | collective-permute-start | bytes 3145736 | tf_op jit(solution)/shard_map/ppermute | solution.py:612
  34.6 9.8 %copy-start.2 = (s32[2]{0:T(128)}, s32[2]{0:T(128)S(1)}, u32[]{:S(2)}) copy-start(s32[2]{0:T(128)S(1)} %pad_add_fusion.pos_ref) | copy-start | bytes 28
  34.6 9.8 %collective-permute-start.1 = (bf16[8,16,1024]{2,1,0:T(8,128)(2,1)S(1)}, bf16[8,16,1024]{2,1,0:T(8,128)(2,1)S(1)}, u32[]{:S(2)}, u32[]{:S(2)}) collective-permute-start(bf16[8,16,1024]{2,1,0:T(8,128)(2,1)S(1)} %constant_dynamic-slice_fusion), channel_id=1, source_target_pairs={{0,1},{1,0},{2,3},{3,2},{4,5},{5,4},{6,7},{7,6},{8,9},{9,8},{10,11... | collective-permute-start | bytes 786440 | tf_op jit(solution)/shard_map/ppermute | solution.py:616
  37.2 7.3 %copy-start.1 = (bf16[8,64,1024]{2,1,0:T(8,128)(2,1)}, bf16[8,64,1024]{2,1,0:T(8,128)(2,1)S(1)}, u32[]{:S(2)}) copy-start(bf16[8,64,1024]{2,1,0:T(8,128)(2,1)S(1)} %collective-permute-done.theirs_ref) | copy-start | bytes 3145732
  44.5 0.7 copy-start.5
  45.2 3.9 %copy-start.6 = (f32[3,3,512]{2,1,0:T(4,128)S(1)}, f32[3,3,512]{2,1,0:T(4,128)}, u32[]{:S(2)}) copy-start(f32[3,3,512]{2,1,0:T(4,128)} %param.10) | copy-start | bytes 55300
  45.2 3.9 %copy-start.7 = (f32[512]{0:T(512)S(1)}, f32[512]{0:T(512)}, u32[]{:S(2)}) copy-start(f32[512]{0:T(512)} %param.12) | copy-start | bytes 6148
  45.2 46.9 %copy-start.4 = (f32[8,256]{1,0:T(8,128)S(1)}, f32[8,256]{1,0:T(8,128)}, u32[]{:S(2)}) copy-start(f32[8,256]{1,0:T(8,128)} %constant.48.clone.phase_ref) | copy-start | bytes 24580
  45.2 46.9 %all-to-all-start.1 = ((bf16[8,208,1024]{2,1,0:T(8,128)(2,1)}), bf16[8,208,1024]{2,1,0:T(8,128)(2,1)S(1)}, u32[]{:S(2)}, u32[]{:S(2)}) async-start(bf16[8,208,1024]{2,1,0:T(8,128)(2,1)} %project.1), calls=%async_computation.1 | async-start | bytes 6815744 | tf_op jit(solution)/shard_map/all_to_all | solution.py:577
  49.1 107.3 %all-gather.7.cloned.1.call-start = ((), (), s32[]{:S(2)}) async-start(), calls=%async_computation.5 | async-start | bytes 6684672 | tf_op jit(solution)/shard_map/all_gather | solution.py:627
  109.0 6.9 %collective-permute-start.2 = (bf16[8,64,128]{2,1,0:T(8,128)(2,1)S(1)}, bf16[8,64,128]{2,1,0:T(8,128)(2,1)S(1)}, u32[]{:S(2)}, u32[]{:S(2)}) collective-permute-start(bf16[8,64,128]{2,1,0:T(8,128)(2,1)S(1)} %slice.4), channel_id=1, source_target_pairs={{0,1},{1,0},{2,3},{3,2},{4,5},{5,4},{6,7},{7,6},{8,9},{9,8},{10,11... | collective-permute-start | bytes 393224 | tf_op jit(solution)/shard_map/ppermute | solution.py:629
  126.0 30.3 %copy-start.3 = (s32[2]{0:T(128)S(1)}, s32[2]{0:T(128)}, u32[]{:S(2)}) copy-start(s32[2]{0:T(128)} %copy-done.2) | copy-start | bytes 28
  163.0 2.9 %collective-permute-start.3 = (bf16[512,1024]{1,0:T(8,128)(2,1)}, bf16[512,1024]{1,0:T(8,128)(2,1)S(1)}, u32[]{:S(2)}, u32[]{:S(2)}) collective-permute-start(bf16[512,1024]{1,0:T(8,128)(2,1)} %get-tuple-element.56), channel_id=1, source_target_pairs={{0,2},{2,0},{4,6},{6,4},{8,10},{10,8},{12,14},{14,12},{1,3},{3,1},... | collective-permute-start | bytes 3145736 | tf_op jit(solution)/shard_map/ppermute | solution.py:644
  167.1 19.6 %all-to-all-start.3 = ((bf16[4,128,1024]{2,1,0:T(8,128)(2,1)}), bf16[4,128,1024]{2,1,0:T(8,128)(2,1)S(1)}, u32[]{:S(2)}, u32[]{:S(2)}) async-start(bf16[4,128,1024]{2,1,0:T(8,128)(2,1)} %bitcast.15), calls=%async_computation.3 | async-start | bytes 2097152 | tf_op jit(solution)/shard_map/all_to_all | solution.py:577
Sparse Core Ops, SparseCore 0:
  45.3 22.2 all-gather.4
  97.0 59.2 all-gather.6

commit v8 on v7

--- a/solution.py
+++ b/solution.py
@@ -34,6 +34,11 @@
 
 def matmul(left, right, dims):
     return lax.dot_general(left, right, dims, preferred_element_type=F32)
+
+
+def split(value):
+    high = value.astype(BF)
+    return high, (value - high.astype(F32)).astype(BF)
 
 
 def edge_kernel(cot_ref, filter_ref, out_ref):
@@ -287,6 +292,12 @@
     return jnp.where(lane >= lanes - steps, 0.0, pltpu.roll(value, lanes - steps, 1))
 
 
+def two_part(value, table, dims):
+    rows = value.shape[0]
+    result = matmul(jnp.concatenate(split(value), axis=0), table, dims)
+    return result[:rows] + result[rows:]
+
+
 def spectrum(value, residue, table):
     width = value.shape[1] // BLOCKS
     parts = [value[:, block * width : (block + 1) * width] for block in range(BLOCKS)]
@@ -297,7 +308,7 @@
         real = real + parts[block] * math.cos(angle)
         term = parts[block] * -math.sin(angle)
         imag = term if imag is None else imag + term
-    result = matmul(jnp.concatenate([real, imag], axis=1).astype(BF), table, NN)
+    result = two_part(jnp.concatenate([real, imag], axis=1), table, NN)
     steps = result.shape[1] // 4
     quarter = [result[:, i * steps : (i + 1) * steps] for i in range(4)]
     return jnp.concatenate([quarter[0], quarter[2]], axis=1), jnp.concatenate(
@@ -310,7 +321,7 @@
     value = jnp.concatenate(
         [real[:, :steps], imag[:, :steps], real[:, steps:], imag[:, steps:]], axis=1
     )
-    result = matmul(value.astype(BF), table, NT)
+    result = two_part(value, table, NT)
     width = result.shape[1] // 2
     even, odd = result[:, :width], result[:, width:]
     for block in range(BLOCKS):
@@ -457,12 +468,12 @@
 def token_part(pos, weight, grads):
     streams, chips, cores, rows, cols = weight.shape
     slabs, _, _, chans, positions = grads.shape
-    part = positions // 4
+    part = positions // 2
     return pl.pallas_call(
         token_kernel,
         grid_spec=pltpu.PrefetchScalarGridSpec(
             num_scalar_prefetch=1,
-            grid=(4,),
+            grid=(2,),
             in_specs=[
                 pl.BlockSpec(memory_space=pltpu.VMEM),
                 pl.BlockSpec((slabs, 1, streams, chans, part), lambda j, pos: (0, pos[0], 0, 0, j)),

time: 196 us -> 195 us (level)
  transfers between devices with their start and end apart: 9 -> 9, of which waited for: 7 -> 7; matrix products, arithmetic and copies ran while one was open for 0% -> 0% of each run, Pallas kernels for 22% -> 23%
where the time goes in v8:
time: 195 us; the launch traced here: 194 us
  waiting for transfers between devices  94.9 us (49%)
  Pallas kernels  54.4 us (28%)
  starting transfers between devices  17.7 us (9%)
  between operations  14.2 us (7%)
  blocking collectives  12.2 us (6%)
    all_to_all x3, waiting for transfers between devices, exchange(): lax.all_to_all(value, axis, split_axis=0, concat_axis=0, tiled=True, axis...  56 us
    all_gather x1, waiting for transfers between devices, local(): grads = lax.all_gather(grads, ('seq', 'dp'), axis=0)  28 us
    all_to_all x3, starting transfers between devices, exchange(): lax.all_to_all(value, axis, split_axis=0, concat_axis=0, tiled=True, axis...  16.1 us
    all_to_all x1, blocking collectives, exchange(): lax.all_to_all(value, axis, split_axis=0, concat_axis=0, tiled=True, axis...  12.2 us
    pallas_call x1, Pallas kernels, weight_grad(): pl.pallas_call(functools.partial(weight_kernel, grad_scale), grid_spec=pl...  11.7 us
    pallas_call x1, Pallas kernels, project(): pl.pallas_call(project_kernel, grid_spec=pltpu.PrefetchScalarGridSpec(num...  7.25 us
    ppermute x1, waiting for transfers between devices, local(): finished = finish(outs, lax.ppermute(outs[:, chans:], 'dp', batches))  6.22 us
    pallas_call x1, Pallas kernels, flip_weight(): pl.pallas_call(flip_kernel, grid=(streams, 2), in_specs=[pl.BlockSpec((1,...  5.74 us
  transfers between devices with their start and end apart: 9, of which 7 were waited for; matrix products, arithmetic and copies ran while one was open for 0% of the time, Pallas kernels for 23%

profile of v8, /device:TPU:0, one launch (start us, length us, event | category | flops | bytes accessed | tf_op | source)
XLA Modules:
  0.0 194.5 jit_solution(14311075991389508984)
XLA Ops:
  7.2 2.1 %cut_tokens.1 = bf16[8,64,1024]{2,1,0:T(8,128)(2,1)} custom-call(s32[1]{0:T(128)} %bitcast.1.core_ref, bf16[1,128,8192]{2,1,0:T(8,128)(2,1)} %tokens_ref.1), custom_call_target="tpu_custom_call" | custom-call | bytes 2097152 | tf_op jit(solution)/shard_map/cut_tokens/pallas_call | solution.py:156
  9.3 8.0 %all-to-all-start = ((bf16[8,64,1024]{2,1,0:T(8,128)(2,1)}), bf16[8,64,1024]{2,1,0:T(8,128)(2,1)S(1)}, u32[]{:S(2)}, u32[]{:S(2)}) async-start(bf16[8,64,1024]{2,1,0:T(8,128)(2,1)} %cut_tokens.1), calls=%async_computation | async-start | bytes 2097152 | tf_op jit(solution)/shard_map/all_to_all | solution.py:588
  17.3 0.0 all-gather.5.cloned.1.call-start
  17.4 5.7 %flip_weight.1.weight_ref = bf16[3,512,1024]{2,1,0:T(8,128)(2,1)} custom-call(bf16[3,1024,512]{2,1,0:T(8,128)(2,1)} %bitcast.13), custom_call_target="tpu_custom_call" | custom-call | bytes 6291456 | tf_op jit(solution)/shard_map/flip_weight/pallas_call | solution.py:89
  23.1 1.9 edge_rows.1.edge_ref
  25.0 9.6 %all-to-all-done.mine_ref = bf16[8,64,1024]{2,1,0:T(8,128)(2,1)S(1)} async-done(((bf16[8,64,1024]{2,1,0:T(8,128)(2,1)}), bf16[8,64,1024]{2,1,0:T(8,128)(2,1)S(1)}, u32[]{:S(2)}, u32[]{:S(2)}) %all-to-all-start) | async-done | bytes 1048608 | tf_op jit(solution)/shard_map/all_to_all | solution.py:588
  34.5 0.0 collective-permute-start
  34.5 0.1 pad_add_fusion.pos_ref
  34.6 0.8 collective-permute-start.1
  35.4 1.8 collective-permute-done.theirs_ref
  37.2 7.2 %project.1 = bf16[8,208,1024]{2,1,0:T(8,128)(2,1)} custom-call(s32[2]{0:T(128)S(1)} %pad_add_fusion.pos_ref, bf16[8,64,1024]{2,1,0:T(8,128)(2,1)S(1)} %all-to-all-done.mine_ref, bf16[8,64,1024]{2,1,0:T(8,128)(2,1)S(1)} %collective-permute-done.theirs_ref, bf16[3,512,1024]{2,1,0:T(8,128)(2,1)} %flip_weight.1.weight_ref, bf16[8,16,1024]{2,1,0:T(8,128)(2,1)} %edge_rows.1.edge_ref), custom_call_target="tpu_custom_call" | custom-call | flops 3221225472 | bytes 8388608 | tf_op jit(solution)/shard_map/project/pallas_call | solution.py:203
  44.5 0.0 copy-done
  44.5 0.0 copy-done.2
  44.5 0.0 copy-done.1
  44.5 0.0 collective-permute-done.1
  44.5 0.0 copy-start.5
  44.5 0.7 copy-done.5
  45.2 0.0 all-gather.5.cloned.1.call-update
  45.2 0.0 copy-start.6
  45.2 0.0 copy-start.7
  45.2 0.0 copy-start.4
  45.2 3.8 %all-to-all-start.1 = ((bf16[8,208,1024]{2,1,0:T(8,128)(2,1)}), bf16[8,208,1024]{2,1,0:T(8,128)(2,1)S(1)}, u32[]{:S(2)}, u32[]{:S(2)}) async-start(bf16[8,208,1024]{2,1,0:T(8,128)(2,1)} %project.1), calls=%async_computation.1 | async-start | bytes 6815744 | tf_op jit(solution)/shard_map/all_to_all | solution.py:588
  49.1 0.0 all-gather.7.cloned.1.call-start
  49.1 0.0 copy-done.6
  49.1 0.0 copy-done.7
  49.1 0.1 fusion
  49.2 0.1 copy.16
  49.3 42.8 %all-to-all-done.1.parts_ref = bf16[8,208,1024]{2,1,0:T(8,128)(2,1)S(1)} async-done(((bf16[8,208,1024]{2,1,0:T(8,128)(2,1)}), bf16[8,208,1024]{2,1,0:T(8,128)(2,1)S(1)}, u32[]{:S(2)}, u32[]{:S(2)}) %all-to-all-start.1) | async-done | bytes 3407904 | tf_op jit(solution)/shard_map/all_to_all | solution.py:588
  92.1 0.0 copy-done.4
  92.1 5.7 %operator.1 = (bf16[192,1024]{1,0:T(8,128)(2,1)}, bf16[8,128,128]{2,1,0:T(8,128)(2,1)}) custom-call(bf16[8,208,1024]{2,1,0:T(8,128)(2,1)S(1)} %all-to-all-done.1.parts_ref, f32[64,10]{1,0:T(8,128)S(1)} %bitcast.12, f32[8,256]{1,0:T(8,128)S(1)} %copy-done.4, bf16[4,512,512]{2,1,0:T(8,128)(2,1)} %constant.47.clone.table_ref), custom_call_target="tpu_custom_call" | custom-call | flops 1610612736 | bytes 5505024 | tf_op jit(solution)/shard_map/operator/pallas_call | solution.py:420
  97.8 0.0 all-gather.5.cloned.1.call-done
  97.8 0.0 all-gather.7.cloned.1.call-update
  97.8 12.2 %all_to_all.20.own_ref = bf16[8,128,128]{2,1,0:T(8,128)(2,1)S(1)} all-to-all(bf16[8,128,128]{2,1,0:T(8,128)(2,1)} %get-tuple-element.45), channel_id=1, replica_groups=mesh['seq'=8,'chan'=8,'dp'=2] {'seq'}, dimensions={0} | all-to-all | bytes 524288 | tf_op jit(solution)/shard_map/all_to_all | solution.py:588
  110.0 0.7 collective-permute-start.2
  110.7 6.2 %collective-permute-done.2.other_ref = bf16[8,64,128]{2,1,0:T(8,128)(2,1)S(1)} collective-permute-done((bf16[8,64,128]{2,1,0:T(8,128)(2,1)S(1)}, bf16[8,64,128]{2,1,0:T(8,128)(2,1)S(1)}, u32[]{:S(2)}, u32[]{:S(2)}) %collective-permute-start.2) | collective-permute-done | bytes 131104 | tf_op jit(solution)/shard_map/ppermute | solution.py:640
  116.9 0.9 finish.1
  117.8 4.2 %turn_shares.1.other_ref = bf16[1024,1024]{1,0:T(8,128)(2,1)} custom-call(bf16[4,2,8,16,1024]{4,3,2,1,0:T(8,128)(2,1)} %bitcast.16), custom_call_target="tpu_custom_call" | custom-call | bytes 4194304 | tf_op jit(solution)/shard_map/turn_shares/pallas_call | solution.py:267
  122.0 4.9 %turn_tokens.1.own_ref = bf16[1024,1024]{1,0:T(8,128)(2,1)} custom-call(s32[2]{0:T(128)} %copy-done.2, bf16[8,64,1024]{2,1,0:T(8,128)(2,1)} %copy-done, bf16[8,64,1024]{2,1,0:T(8,128)(2,1)} %copy-done.1), custom_call_target="tpu_custom_call" | custom-call | bytes 4194304 | tf_op jit(solution)/shard_map/turn_tokens/pallas_call | solution.py:237
  126.9 2.3 %near_weight.1.weight_ref = bf16[3,4,2,128,512]{4,3,2,1,0:T(8,128)(2,1)S(1)} custom-call(bf16[3,4,2,128,512]{4,3,2,1,0:T(8,128)(2,1)} %bitcast.14), custom_call_target="tpu_custom_call" | custom-call | bytes 6291456 | tf_op jit(solution)/shard_map/near_weight/pallas_call | solution.py:438
  129.3 28.0 %all-gather.7.cloned.1.call-done = bf16[3072,1024]{1,0:T(8,128)(2,1)} async-done(((bf16[192,1024]{1,0:T(8,128)(2,1)}), bf16[3072,1024]{1,0:T(8,128)(2,1)}) %all-gather.7.cloned.1.call-update) | async-done | bytes 6291472 | tf_op jit(solution)/shard_map/all_gather | solution.py:638
  157.3 5.6 %token_part.1 = (bf16[512,1024]{1,0:T(8,128)(2,1)}, bf16[512,1024]{1,0:T(8,128)(2,1)S(1)}) custom-call(s32[2]{0:T(128)S(1)} %copy-done.3, bf16[3,4,2,128,512]{4,3,2,1,0:T(8,128)(2,1)S(1)} %near_weight.1.weight_ref, bf16[8,2,3,64,1024]{4,3,2,1,0:T(8,128)(2,1)} %bitcast.18), custom_call_target="tpu_custom_call" | custom-call | flops 3221225472 | bytes 4194304 | tf_op jit(solution)/shard_map/token_part/pallas_call | solution.py:472
  162.9 0.1 collective-permute-start.3
  163.0 2.9 %collective-permute-done.3.received_ref = bf16[512,1024]{1,0:T(8,128)(2,1)S(1)} collective-permute-done((bf16[512,1024]{1,0:T(8,128)(2,1)}, bf16[512,1024]{1,0:T(8,128)(2,1)S(1)}, u32[]{:S(2)}, u32[]{:S(2)}) %collective-permute-start.3) | collective-permute-done | bytes 1048608 | tf_op jit(solution)/shard_map/ppermute | solution.py:655
  165.9 1.2 pair_sum.1
  167.1 4.2 %all-to-all-start.3 = ((bf16[4,128,1024]{2,1,0:T(8,128)(2,1)}), bf16[4,128,1024]{2,1,0:T(8,128)(2,1)S(1)}, u32[]{:S(2)}, u32[]{:S(2)}) async-start(bf16[4,128,1024]{2,1,0:T(8,128)(2,1)} %bitcast.15), calls=%async_computation.3 | async-start | bytes 2097152 | tf_op jit(solution)/shard_map/all_to_all | solution.py:588
  171.3 11.7 %weight_grad.1 = bf16[3,1024,512]{2,1,0:T(8,128)(2,1)} custom-call(s32[2]{0:T(128)} %copy-done.2, bf16[1024,1024]{1,0:T(8,128)(2,1)} %turn_tokens.1.own_ref, bf16[1024,1024]{1,0:T(8,128)(2,1)} %turn_shares.1.other_ref, bf16[8,2,3,64,1024]{4,3,2,1,0:T(8,128)(2,1)} %bitcast.19, bf16[8,2,3,64,1024]{4,3,2,1,0:T(8,128)(2,1)} %bitcast.20), custom_call_target="tpu_custom_call" | custom-call | flops 6442450944 | bytes 13631488 | tf_op jit(solution)/shard_map/weight_grad/pallas_call | solution.py:522
  183.0 3.7 %all-to-all-done.3.parts_ref = bf16[4,128,1024]{2,1,0:T(8,128)(2,1)S(1)} async-done(((bf16[4,128,1024]{2,1,0:T(8,128)(2,1)}), bf16[4,128,1024]{2,1,0:T(8,128)(2,1)S(1)}, u32[]{:S(2)}, u32[]{:S(2)}) %all-to-all-start.3) | async-done | bytes 1048608 | tf_op jit(solution)/shard_map/all_to_all | solution.py:588
  186.7 0.9 token_total.1
  (8 shorter events, 0.1 us)
Async XLA Ops:
  9.3 25.2 %all-to-all-start = ((bf16[8,64,1024]{2,1,0:T(8,128)(2,1)}), bf16[8,64,1024]{2,1,0:T(8,128)(2,1)S(1)}, u32[]{:S(2)}, u32[]{:S(2)}) async-start(bf16[8,64,1024]{2,1,0:T(8,128)(2,1)} %cut_tokens.1), calls=%async_computation | async-start | bytes 2097152 | tf_op jit(solution)/shard_map/all_to_all | solution.py:588
  17.3 80.5 %all-gather.5.cloned.1.call-start = ((), (), s32[]{:S(2)}) async-start(), calls=%async_computation.4 | async-start | bytes 2359296 | tf_op jit(solution)/shard_map/all_gather | solution.py:629
  34.5 9.9 %copy-start = (bf16[8,64,1024]{2,1,0:T(8,128)(2,1)}, bf16[8,64,1024]{2,1,0:T(8,128)(2,1)S(1)}, u32[]{:S(2)}) copy-start(bf16[8,64,1024]{2,1,0:T(8,128)(2,1)S(1)} %all-to-all-done.mine_ref) | copy-start | bytes 3145732
  34.5 2.7 %collective-permute-start = (bf16[8,64,1024]{2,1,0:T(8,128)(2,1)S(1)}, bf16[8,64,1024]{2,1,0:T(8,128)(2,1)S(1)}, u32[]{:S(2)}, u32[]{:S(2)}) collective-permute-start(bf16[8,64,1024]{2,1,0:T(8,128)(2,1)S(1)} %all-to-all-done.mine_ref), channel_id=1, source_target_pairs={{0,2},{2,0},{4,6},{6,4},{8,10},{10,8},{12,14},{14,12},{1,3},{3,1},... | collective-permute-start | bytes 3145736 | tf_op jit(solution)/shard_map/ppermute | solution.py:623
  34.6 9.8 %copy-start.2 = (s32[2]{0:T(128)}, s32[2]{0:T(128)S(1)}, u32[]{:S(2)}) copy-start(s32[2]{0:T(128)S(1)} %pad_add_fusion.pos_ref) | copy-start | bytes 28
  34.6 9.8 %collective-permute-start.1 = (bf16[8,16,1024]{2,1,0:T(8,128)(2,1)S(1)}, bf16[8,16,1024]{2,1,0:T(8,128)(2,1)S(1)}, u32[]{:S(2)}, u32[]{:S(2)}) collective-permute-start(bf16[8,16,1024]{2,1,0:T(8,128)(2,1)S(1)} %constant_dynamic-slice_fusion), channel_id=1, source_target_pairs={{0,1},{1,0},{2,3},{3,2},{4,5},{5,4},{6,7},{7,6},{8,9},{9,8},{10,11... | collective-permute-start | bytes 786440 | tf_op jit(solution)/shard_map/ppermute | solution.py:627
  37.2 7.3 %copy-start.1 = (bf16[8,64,1024]{2,1,0:T(8,128)(2,1)}, bf16[8,64,1024]{2,1,0:T(8,128)(2,1)S(1)}, u32[]{:S(2)}) copy-start(bf16[8,64,1024]{2,1,0:T(8,128)(2,1)S(1)} %collective-permute-done.theirs_ref) | copy-start | bytes 3145732
  44.5 0.7 copy-start.5
  45.2 3.9 %copy-start.6 = (f32[3,3,512]{2,1,0:T(4,128)S(1)}, f32[3,3,512]{2,1,0:T(4,128)}, u32[]{:S(2)}) copy-start(f32[3,3,512]{2,1,0:T(4,128)} %param.10) | copy-start | bytes 55300
  45.2 3.9 %copy-start.7 = (f32[512]{0:T(512)S(1)}, f32[512]{0:T(512)}, u32[]{:S(2)}) copy-start(f32[512]{0:T(512)} %param.12) | copy-start | bytes 6148
  45.2 46.9 %copy-start.4 = (f32[8,256]{1,0:T(8,128)S(1)}, f32[8,256]{1,0:T(8,128)}, u32[]{:S(2)}) copy-start(f32[8,256]{1,0:T(8,128)} %constant.48.clone.phase_ref) | copy-start | bytes 24580
  45.2 46.9 %all-to-all-start.1 = ((bf16[8,208,1024]{2,1,0:T(8,128)(2,1)}), bf16[8,208,1024]{2,1,0:T(8,128)(2,1)S(1)}, u32[]{:S(2)}, u32[]{:S(2)}) async-start(bf16[8,208,1024]{2,1,0:T(8,128)(2,1)} %project.1), calls=%async_computation.1 | async-start | bytes 6815744 | tf_op jit(solution)/shard_map/all_to_all | solution.py:588
  49.1 108.2 %all-gather.7.cloned.1.call-start = ((), (), s32[]{:S(2)}) async-start(), calls=%async_computation.5 | async-start | bytes 6684672 | tf_op jit(solution)/shard_map/all_gather | solution.py:638
  110.0 6.9 %collective-permute-start.2 = (bf16[8,64,128]{2,1,0:T(8,128)(2,1)S(1)}, bf16[8,64,128]{2,1,0:T(8,128)(2,1)S(1)}, u32[]{:S(2)}, u32[]{:S(2)}) collective-permute-start(bf16[8,64,128]{2,1,0:T(8,128)(2,1)S(1)} %slice.4), channel_id=1, source_target_pairs={{0,1},{1,0},{2,3},{3,2},{4,5},{5,4},{6,7},{7,6},{8,9},{9,8},{10,11... | collective-permute-start | bytes 393224 | tf_op jit(solution)/shard_map/ppermute | solution.py:640
  126.9 30.3 %copy-start.3 = (s32[2]{0:T(128)S(1)}, s32[2]{0:T(128)}, u32[]{:S(2)}) copy-start(s32[2]{0:T(128)} %copy-done.2) | copy-start | bytes 28
  162.9 3.0 %collective-permute-start.3 = (bf16[512,1024]{1,0:T(8,128)(2,1)}, bf16[512,1024]{1,0:T(8,128)(2,1)S(1)}, u32[]{:S(2)}, u32[]{:S(2)}) collective-permute-start(bf16[512,1024]{1,0:T(8,128)(2,1)} %get-tuple-element.56), channel_id=1, source_target_pairs={{0,2},{2,0},{4,6},{6,4},{8,10},{10,8},{12,14},{14,12},{1,3},{3,1},... | collective-permute-start | bytes 3145736 | tf_op jit(solution)/shard_map/ppermute | solution.py:655
  167.1 19.6 %all-to-all-start.3 = ((bf16[4,128,1024]{2,1,0:T(8,128)(2,1)}), bf16[4,128,1024]{2,1,0:T(8,128)(2,1)S(1)}, u32[]{:S(2)}, u32[]{:S(2)}) async-start(bf16[4,128,1024]{2,1,0:T(8,128)(2,1)} %bitcast.15), calls=%async_computation.3 | async-start | bytes 2097152 | tf_op jit(solution)/shard_map/all_to_all | solution.py:588
Sparse Core Ops, SparseCore 0:
  45.3 22.2 all-gather.4
  98.0 59.2 all-gather.6

commit v9 on v8

--- a/solution.py
+++ b/solution.py
@@ -468,12 +468,12 @@
 def token_part(pos, weight, grads):
     streams, chips, cores, rows, cols = weight.shape
     slabs, _, _, chans, positions = grads.shape
-    part = positions // 2
+    part = positions
     return pl.pallas_call(
         token_kernel,
         grid_spec=pltpu.PrefetchScalarGridSpec(
             num_scalar_prefetch=1,
-            grid=(2,),
+            grid=(1,),
             in_specs=[
                 pl.BlockSpec(memory_space=pltpu.VMEM),
                 pl.BlockSpec((slabs, 1, streams, chans, part), lambda j, pos: (0, pos[0], 0, 0, j)),

time: 195 us -> 196 us (level)
  no operation moved by 1% of the time
where the time goes in v9:
time: 196 us; the launch traced here: 195 us
  waiting for transfers between devices  94.9 us (48%)
  Pallas kernels  54.6 us (28%)
  starting transfers between devices  17.7 us (9%)
  between operations  14.2 us (7%)
  blocking collectives  12.2 us (6%)
    all_to_all x3, waiting for transfers between devices, exchange(): lax.all_to_all(value, axis, split_axis=0, concat_axis=0, tiled=True, axis...  56 us
    all_gather x1, waiting for transfers between devices, local(): grads = lax.all_gather(grads, ('seq', 'dp'), axis=0)  28 us
    all_to_all x3, starting transfers between devices, exchange(): lax.all_to_all(value, axis, split_axis=0, concat_axis=0, tiled=True, axis...  16.1 us
    all_to_all x1, blocking collectives, exchange(): lax.all_to_all(value, axis, split_axis=0, concat_axis=0, tiled=True, axis...  12.2 us
    pallas_call x1, Pallas kernels, weight_grad(): pl.pallas_call(functools.partial(weight_kernel, grad_scale), grid_spec=pl...  11.7 us
    pallas_call x1, Pallas kernels, project(): pl.pallas_call(project_kernel, grid_spec=pltpu.PrefetchScalarGridSpec(num...  7.25 us
    ppermute x1, waiting for transfers between devices, local(): finished = finish(outs, lax.ppermute(outs[:, chans:], 'dp', batches))  6.22 us
    pallas_call x1, Pallas kernels, token_part(): pl.pallas_call(token_kernel, grid_spec=pltpu.PrefetchScalarGridSpec(num_s...  5.85 us
  transfers between devices with their start and end apart: 9, of which 7 were waited for; matrix products, arithmetic and copies ran while one was open for 0% of the time, Pallas kernels for 23%

profile of v9, /device:TPU:0, one launch (start us, length us, event | category | flops | bytes accessed | tf_op | source)
XLA Modules:
  0.0 194.7 jit_solution(13928744236545216991)
XLA Ops:
  7.2 2.1 %cut_tokens.1 = bf16[8,64,1024]{2,1,0:T(8,128)(2,1)} custom-call(s32[1]{0:T(128)} %bitcast.1.core_ref, bf16[1,128,8192]{2,1,0:T(8,128)(2,1)} %tokens_ref.1), custom_call_target="tpu_custom_call" | custom-call | bytes 2097152 | tf_op jit(solution)/shard_map/cut_tokens/pallas_call | solution.py:156
  9.3 8.0 %all-to-all-start = ((bf16[8,64,1024]{2,1,0:T(8,128)(2,1)}), bf16[8,64,1024]{2,1,0:T(8,128)(2,1)S(1)}, u32[]{:S(2)}, u32[]{:S(2)}) async-start(bf16[8,64,1024]{2,1,0:T(8,128)(2,1)} %cut_tokens.1), calls=%async_computation | async-start | bytes 2097152 | tf_op jit(solution)/shard_map/all_to_all | solution.py:588
  17.3 0.0 all-gather.5.cloned.1.call-start
  17.4 5.7 %flip_weight.1.weight_ref = bf16[3,512,1024]{2,1,0:T(8,128)(2,1)} custom-call(bf16[3,1024,512]{2,1,0:T(8,128)(2,1)} %bitcast.13), custom_call_target="tpu_custom_call" | custom-call | bytes 6291456 | tf_op jit(solution)/shard_map/flip_weight/pallas_call | solution.py:89
  23.1 1.9 edge_rows.1.edge_ref
  25.0 9.6 %all-to-all-done.mine_ref = bf16[8,64,1024]{2,1,0:T(8,128)(2,1)S(1)} async-done(((bf16[8,64,1024]{2,1,0:T(8,128)(2,1)}), bf16[8,64,1024]{2,1,0:T(8,128)(2,1)S(1)}, u32[]{:S(2)}, u32[]{:S(2)}) %all-to-all-start) | async-done | bytes 1048608 | tf_op jit(solution)/shard_map/all_to_all | solution.py:588
  34.5 0.0 collective-permute-start
  34.5 0.1 pad_add_fusion.pos_ref
  34.6 0.8 collective-permute-start.1
  35.4 1.8 collective-permute-done.theirs_ref
  37.2 7.2 %project.1 = bf16[8,208,1024]{2,1,0:T(8,128)(2,1)} custom-call(s32[2]{0:T(128)S(1)} %pad_add_fusion.pos_ref, bf16[8,64,1024]{2,1,0:T(8,128)(2,1)S(1)} %all-to-all-done.mine_ref, bf16[8,64,1024]{2,1,0:T(8,128)(2,1)S(1)} %collective-permute-done.theirs_ref, bf16[3,512,1024]{2,1,0:T(8,128)(2,1)} %flip_weight.1.weight_ref, bf16[8,16,1024]{2,1,0:T(8,128)(2,1)} %edge_rows.1.edge_ref), custom_call_target="tpu_custom_call" | custom-call | flops 3221225472 | bytes 8388608 | tf_op jit(solution)/shard_map/project/pallas_call | solution.py:203
  44.5 0.0 copy-done
  44.5 0.0 copy-done.2
  44.5 0.0 copy-done.1
  44.5 0.0 collective-permute-done.1
  44.5 0.0 copy-start.5
  44.5 0.7 copy-done.5
  45.2 0.0 all-gather.5.cloned.1.call-update
  45.2 0.0 copy-start.6
  45.2 0.0 copy-start.7
  45.2 0.0 copy-start.4
  45.2 3.8 %all-to-all-start.1 = ((bf16[8,208,1024]{2,1,0:T(8,128)(2,1)}), bf16[8,208,1024]{2,1,0:T(8,128)(2,1)S(1)}, u32[]{:S(2)}, u32[]{:S(2)}) async-start(bf16[8,208,1024]{2,1,0:T(8,128)(2,1)} %project.1), calls=%async_computation.1 | async-start | bytes 6815744 | tf_op jit(solution)/shard_map/all_to_all | solution.py:588
  49.1 0.0 all-gather.7.cloned.1.call-start
  49.1 0.0 copy-done.6
  49.1 0.0 copy-done.7
  49.1 0.1 fusion
  49.2 0.1 copy.16
  49.3 42.8 %all-to-all-done.1.parts_ref = bf16[8,208,1024]{2,1,0:T(8,128)(2,1)S(1)} async-done(((bf16[8,208,1024]{2,1,0:T(8,128)(2,1)}), bf16[8,208,1024]{2,1,0:T(8,128)(2,1)S(1)}, u32[]{:S(2)}, u32[]{:S(2)}) %all-to-all-start.1) | async-done | bytes 3407904 | tf_op jit(solution)/shard_map/all_to_all | solution.py:588
  92.1 0.0 copy-done.4
  92.1 5.7 %operator.1 = (bf16[192,1024]{1,0:T(8,128)(2,1)}, bf16[8,128,128]{2,1,0:T(8,128)(2,1)}) custom-call(bf16[8,208,1024]{2,1,0:T(8,128)(2,1)S(1)} %all-to-all-done.1.parts_ref, f32[64,10]{1,0:T(8,128)S(1)} %bitcast.12, f32[8,256]{1,0:T(8,128)S(1)} %copy-done.4, bf16[4,512,512]{2,1,0:T(8,128)(2,1)} %constant.47.clone.table_ref), custom_call_target="tpu_custom_call" | custom-call | flops 1610612736 | bytes 5505024 | tf_op jit(solution)/shard_map/operator/pallas_call | solution.py:420
  97.8 0.0 all-gather.5.cloned.1.call-done
  97.8 0.0 all-gather.7.cloned.1.call-update
  97.8 12.2 %all_to_all.20.own_ref = bf16[8,128,128]{2,1,0:T(8,128)(2,1)S(1)} all-to-all(bf16[8,128,128]{2,1,0:T(8,128)(2,1)} %get-tuple-element.45), channel_id=1, replica_groups=mesh['seq'=8,'chan'=8,'dp'=2] {'seq'}, dimensions={0} | all-to-all | bytes 524288 | tf_op jit(solution)/shard_map/all_to_all | solution.py:588
  110.0 0.7 collective-permute-start.2
  110.7 6.2 %collective-permute-done.2.other_ref = bf16[8,64,128]{2,1,0:T(8,128)(2,1)S(1)} collective-permute-done((bf16[8,64,128]{2,1,0:T(8,128)(2,1)S(1)}, bf16[8,64,128]{2,1,0:T(8,128)(2,1)S(1)}, u32[]{:S(2)}, u32[]{:S(2)}) %collective-permute-start.2) | collective-permute-done | bytes 131104 | tf_op jit(solution)/shard_map/ppermute | solution.py:640
  116.9 0.9 finish.1
  117.8 4.2 %turn_shares.1.other_ref = bf16[1024,1024]{1,0:T(8,128)(2,1)} custom-call(bf16[4,2,8,16,1024]{4,3,2,1,0:T(8,128)(2,1)} %bitcast.16), custom_call_target="tpu_custom_call" | custom-call | bytes 4194304 | tf_op jit(solution)/shard_map/turn_shares/pallas_call | solution.py:267
  122.0 4.9 %turn_tokens.1.own_ref = bf16[1024,1024]{1,0:T(8,128)(2,1)} custom-call(s32[2]{0:T(128)} %copy-done.2, bf16[8,64,1024]{2,1,0:T(8,128)(2,1)} %copy-done, bf16[8,64,1024]{2,1,0:T(8,128)(2,1)} %copy-done.1), custom_call_target="tpu_custom_call" | custom-call | bytes 4194304 | tf_op jit(solution)/shard_map/turn_tokens/pallas_call | solution.py:237
  126.9 2.3 %near_weight.1.weight_ref = bf16[3,4,2,128,512]{4,3,2,1,0:T(8,128)(2,1)S(1)} custom-call(bf16[3,4,2,128,512]{4,3,2,1,0:T(8,128)(2,1)} %bitcast.14), custom_call_target="tpu_custom_call" | custom-call | bytes 6291456 | tf_op jit(solution)/shard_map/near_weight/pallas_call | solution.py:438
  129.3 28.0 %all-gather.7.cloned.1.call-done = bf16[3072,1024]{1,0:T(8,128)(2,1)} async-done(((bf16[192,1024]{1,0:T(8,128)(2,1)}), bf16[3072,1024]{1,0:T(8,128)(2,1)}) %all-gather.7.cloned.1.call-update) | async-done | bytes 6291472 | tf_op jit(solution)/shard_map/all_gather | solution.py:638
  157.3 5.8 %token_part.1 = (bf16[512,1024]{1,0:T(8,128)(2,1)}, bf16[512,1024]{1,0:T(8,128)(2,1)S(1)}) custom-call(s32[2]{0:T(128)S(1)} %copy-done.3, bf16[3,4,2,128,512]{4,3,2,1,0:T(8,128)(2,1)S(1)} %near_weight.1.weight_ref, bf16[8,2,3,64,1024]{4,3,2,1,0:T(8,128)(2,1)} %bitcast.18), custom_call_target="tpu_custom_call" | custom-call | flops 3221225472 | bytes 4194304 | tf_op jit(solution)/shard_map/token_part/pallas_call | solution.py:472
  163.1 0.1 collective-permute-start.3
  163.2 2.9 %collective-permute-done.3.received_ref = bf16[512,1024]{1,0:T(8,128)(2,1)S(1)} collective-permute-done((bf16[512,1024]{1,0:T(8,128)(2,1)}, bf16[512,1024]{1,0:T(8,128)(2,1)S(1)}, u32[]{:S(2)}, u32[]{:S(2)}) %collective-permute-start.3) | collective-permute-done | bytes 1048608 | tf_op jit(solution)/shard_map/ppermute | solution.py:655
  166.1 1.2 pair_sum.1
  167.3 4.2 %all-to-all-start.3 = ((bf16[4,128,1024]{2,1,0:T(8,128)(2,1)}), bf16[4,128,1024]{2,1,0:T(8,128)(2,1)S(1)}, u32[]{:S(2)}, u32[]{:S(2)}) async-start(bf16[4,128,1024]{2,1,0:T(8,128)(2,1)} %bitcast.15), calls=%async_computation.3 | async-start | bytes 2097152 | tf_op jit(solution)/shard_map/all_to_all | solution.py:588
  171.6 11.7 %weight_grad.1 = bf16[3,1024,512]{2,1,0:T(8,128)(2,1)} custom-call(s32[2]{0:T(128)} %copy-done.2, bf16[1024,1024]{1,0:T(8,128)(2,1)} %turn_tokens.1.own_ref, bf16[1024,1024]{1,0:T(8,128)(2,1)} %turn_shares.1.other_ref, bf16[8,2,3,64,1024]{4,3,2,1,0:T(8,128)(2,1)} %bitcast.19, bf16[8,2,3,64,1024]{4,3,2,1,0:T(8,128)(2,1)} %bitcast.20), custom_call_target="tpu_custom_call" | custom-call | flops 6442450944 | bytes 13631488 | tf_op jit(solution)/shard_map/weight_grad/pallas_call | solution.py:522
  183.3 3.7 %all-to-all-done.3.parts_ref = bf16[4,128,1024]{2,1,0:T(8,128)(2,1)S(1)} async-done(((bf16[4,128,1024]{2,1,0:T(8,128)(2,1)}), bf16[4,128,1024]{2,1,0:T(8,128)(2,1)S(1)}, u32[]{:S(2)}, u32[]{:S(2)}) %all-to-all-start.3) | async-done | bytes 1048608 | tf_op jit(solution)/shard_map/all_to_all | solution.py:588
  187.0 0.9 token_total.1
  (8 shorter events, 0.1 us)
Async XLA Ops:
  9.3 25.2 %all-to-all-start = ((bf16[8,64,1024]{2,1,0:T(8,128)(2,1)}), bf16[8,64,1024]{2,1,0:T(8,128)(2,1)S(1)}, u32[]{:S(2)}, u32[]{:S(2)}) async-start(bf16[8,64,1024]{2,1,0:T(8,128)(2,1)} %cut_tokens.1), calls=%async_computation | async-start | bytes 2097152 | tf_op jit(solution)/shard_map/all_to_all | solution.py:588
  17.3 80.5 %all-gather.5.cloned.1.call-start = ((), (), s32[]{:S(2)}) async-start(), calls=%async_computation.4 | async-start | bytes 2359296 | tf_op jit(solution)/shard_map/all_gather | solution.py:629
  34.5 9.9 %copy-start = (bf16[8,64,1024]{2,1,0:T(8,128)(2,1)}, bf16[8,64,1024]{2,1,0:T(8,128)(2,1)S(1)}, u32[]{:S(2)}) copy-start(bf16[8,64,1024]{2,1,0:T(8,128)(2,1)S(1)} %all-to-all-done.mine_ref) | copy-start | bytes 3145732
  34.5 2.7 %collective-permute-start = (bf16[8,64,1024]{2,1,0:T(8,128)(2,1)S(1)}, bf16[8,64,1024]{2,1,0:T(8,128)(2,1)S(1)}, u32[]{:S(2)}, u32[]{:S(2)}) collective-permute-start(bf16[8,64,1024]{2,1,0:T(8,128)(2,1)S(1)} %all-to-all-done.mine_ref), channel_id=1, source_target_pairs={{0,2},{2,0},{4,6},{6,4},{8,10},{10,8},{12,14},{14,12},{1,3},{3,1},... | collective-permute-start | bytes 3145736 | tf_op jit(solution)/shard_map/ppermute | solution.py:623
  34.6 9.8 %copy-start.2 = (s32[2]{0:T(128)}, s32[2]{0:T(128)S(1)}, u32[]{:S(2)}) copy-start(s32[2]{0:T(128)S(1)} %pad_add_fusion.pos_ref) | copy-start | bytes 28
  34.6 9.8 %collective-permute-start.1 = (bf16[8,16,1024]{2,1,0:T(8,128)(2,1)S(1)}, bf16[8,16,1024]{2,1,0:T(8,128)(2,1)S(1)}, u32[]{:S(2)}, u32[]{:S(2)}) collective-permute-start(bf16[8,16,1024]{2,1,0:T(8,128)(2,1)S(1)} %constant_dynamic-slice_fusion), channel_id=1, source_target_pairs={{0,1},{1,0},{2,3},{3,2},{4,5},{5,4},{6,7},{7,6},{8,9},{9,8},{10,11... | collective-permute-start | bytes 786440 | tf_op jit(solution)/shard_map/ppermute | solution.py:627
  37.2 7.3 %copy-start.1 = (bf16[8,64,1024]{2,1,0:T(8,128)(2,1)}, bf16[8,64,1024]{2,1,0:T(8,128)(2,1)S(1)}, u32[]{:S(2)}) copy-start(bf16[8,64,1024]{2,1,0:T(8,128)(2,1)S(1)} %collective-permute-done.theirs_ref) | copy-start | bytes 3145732
  44.5 0.7 copy-start.5
  45.2 3.9 %copy-start.6 = (f32[3,3,512]{2,1,0:T(4,128)S(1)}, f32[3,3,512]{2,1,0:T(4,128)}, u32[]{:S(2)}) copy-start(f32[3,3,512]{2,1,0:T(4,128)} %param.10) | copy-start | bytes 55300
  45.2 3.9 %copy-start.7 = (f32[512]{0:T(512)S(1)}, f32[512]{0:T(512)}, u32[]{:S(2)}) copy-start(f32[512]{0:T(512)} %param.12) | copy-start | bytes 6148
  45.2 46.9 %copy-start.4 = (f32[8,256]{1,0:T(8,128)S(1)}, f32[8,256]{1,0:T(8,128)}, u32[]{:S(2)}) copy-start(f32[8,256]{1,0:T(8,128)} %constant.48.clone.phase_ref) | copy-start | bytes 24580
  45.2 46.9 %all-to-all-start.1 = ((bf16[8,208,1024]{2,1,0:T(8,128)(2,1)}), bf16[8,208,1024]{2,1,0:T(8,128)(2,1)S(1)}, u32[]{:S(2)}, u32[]{:S(2)}) async-start(bf16[8,208,1024]{2,1,0:T(8,128)(2,1)} %project.1), calls=%async_computation.1 | async-start | bytes 6815744 | tf_op jit(solution)/shard_map/all_to_all | solution.py:588
  49.1 108.2 %all-gather.7.cloned.1.call-start = ((), (), s32[]{:S(2)}) async-start(), calls=%async_computation.5 | async-start | bytes 6684672 | tf_op jit(solution)/shard_map/all_gather | solution.py:638
  110.0 6.9 %collective-permute-start.2 = (bf16[8,64,128]{2,1,0:T(8,128)(2,1)S(1)}, bf16[8,64,128]{2,1,0:T(8,128)(2,1)S(1)}, u32[]{:S(2)}, u32[]{:S(2)}) collective-permute-start(bf16[8,64,128]{2,1,0:T(8,128)(2,1)S(1)} %slice.4), channel_id=1, source_target_pairs={{0,1},{1,0},{2,3},{3,2},{4,5},{5,4},{6,7},{7,6},{8,9},{9,8},{10,11... | collective-permute-start | bytes 393224 | tf_op jit(solution)/shard_map/ppermute | solution.py:640
  126.9 30.3 %copy-start.3 = (s32[2]{0:T(128)S(1)}, s32[2]{0:T(128)}, u32[]{:S(2)}) copy-start(s32[2]{0:T(128)} %copy-done.2) | copy-start | bytes 28
  163.1 3.0 %collective-permute-start.3 = (bf16[512,1024]{1,0:T(8,128)(2,1)}, bf16[512,1024]{1,0:T(8,128)(2,1)S(1)}, u32[]{:S(2)}, u32[]{:S(2)}) collective-permute-start(bf16[512,1024]{1,0:T(8,128)(2,1)} %get-tuple-element.56), channel_id=1, source_target_pairs={{0,2},{2,0},{4,6},{6,4},{8,10},{10,8},{12,14},{14,12},{1,3},{3,1},... | collective-permute-start | bytes 3145736 | tf_op jit(solution)/shard_map/ppermute | solution.py:655
  167.3 19.6 %all-to-all-start.3 = ((bf16[4,128,1024]{2,1,0:T(8,128)(2,1)}), bf16[4,128,1024]{2,1,0:T(8,128)(2,1)S(1)}, u32[]{:S(2)}, u32[]{:S(2)}) async-start(bf16[4,128,1024]{2,1,0:T(8,128)(2,1)} %bitcast.15), calls=%async_computation.3 | async-start | bytes 2097152 | tf_op jit(solution)/shard_map/all_to_all | solution.py:588
Sparse Core Ops, SparseCore 0:
  45.3 22.2 all-gather.4
  98.0 59.2 all-gather.6
